TPU v7x, 32 devices: a whole 2x2x4 slice. The times are simulated.
32 devices in a mesh: orb: 8 (over y, x, core), slab: 4 (over z).
Axes of the slice: x: 2, y: 2, z: 4, core: 2. Of those that a mesh axis runs over, the one named last changes fastest.
Arguments:
- pool: float32 [16, 32, 32, 128], P('orb', 'slab'), may hold values from -6 to 6
- target_row: int32 [8], P('orb'), may hold values from 0 to 1
- source_index: int32 [3], replicated, may hold values from 0 to 15
- metric: float32 [3, 32, 32, 128], P(None, 'slab'), may hold values from 0.3 to 3
- screening: float32 [32, 32, 128], P('slab'), may hold values from 0.05 to 4
Outputs:
- exchange: float32 [8, 32, 32, 128], P('orb', 'slab')
All inputs are finite; a program needn't handle non-finite values.
Results may differ from a plain program's by a relative error of at most 0.000096.
Values sent between devices are 32-bit elements; how exact they have to be, the bound alone decides.
No kernel may reach another device: no remote copies, remote signals or barrier semaphores. Data moves between devices by JAX's collectives and lax.ppermute only.
A program may use at most 64 MiB of HBM per device.

v0:
```python
import math

import jax
import jax.numpy as jnp
from jax import lax
from jax.sharding import PartitionSpec as P

NSRC = 3
SWEEPS = 6


def extended(cells, sides, width):
    for axis, dim in sides:
        count = lax.axis_size(axis)
        ends = count - 1
        head = lax.slice_in_dim(cells, 0, width, axis=dim)
        tail = lax.slice_in_dim(cells, cells.shape[dim] - width, cells.shape[dim], axis=dim)
        cells = jnp.concatenate(
            [
                lax.ppermute(tail, axis, [(i, (i + 1) % count) for i in range(ends)]),
                cells,
                lax.ppermute(head, axis, [((i + 1) % count, i) for i in range(ends)]),
            ],
            axis=dim,
        )
    return cells


def spread(value, axis, source):
    kept = jnp.where(lax.axis_index(axis) == source, value, 0).astype(value.dtype)
    return lax.psum(kept, axis)


def shifted(array, axis, by):
    size = lax.axis_size(axis)
    pairs = [(i, i + by) for i in range(size) if 0 <= i + by < size]
    return lax.ppermute(array, axis, pairs)


def lower_x(f):
    return jnp.concatenate([jnp.zeros_like(f[..., :1, :]), f[..., :-1, :]], axis=-2)


def upper_x(f):
    return jnp.concatenate([f[..., 1:, :], jnp.zeros_like(f[..., :1, :])], axis=-2)


def lower_y(f):
    return jnp.concatenate([jnp.zeros_like(f[..., :1]), f[..., :-1]], axis=-1)


def upper_y(f):
    return jnp.concatenate([f[..., 1:], jnp.zeros_like(f[..., :1])], axis=-1)


def step_sizes(count):
    return [
        1.0 / (1.025 + 0.975 * math.cos(math.pi * (2 * k + 1) / (2 * count))) for k in range(count)
    ]


def apply_rest(field, up_plane, down_plane, faces, diag):
    face_x, face_y, face_z, below_x, below_y, below_z = faces
    return (
        diag * field
        - face_z * up_plane
        - below_z * down_plane
        - face_x * upper_x(field)
        - below_x * lower_x(field)
        - face_y * upper_y(field)
        - below_y * lower_y(field)
    )


def sweep_rimmed(density, faces, diag, weights):
    field = weights[0] * density / diag
    for k in range(1, SWEEPS):
        padded = extended(field, (("slab", 1),), 1)
        image = apply_rest(field, padded[:, 2:], padded[:, :-2], faces, diag)
        field = field + weights[k] * (density - image) / diag
    return field


def shards(pool, target_row, source_index, metric, screening):
    held = pool.shape[0]
    weights = step_sizes(SWEEPS)
    copies = []
    for s in range(NSRC):
        which = source_index[s]
        mine = lax.dynamic_index_in_dim(pool, which % held, 0, keepdims=False)
        copies.append(spread(mine, "orb", which // held))
    sources = jnp.stack(copies)
    targets = jnp.take(pool, target_row, axis=0)
    face_x, face_y, face_z = (metric[0], metric[1], metric[2])
    last_plane = shifted(face_z[-1:], "slab", 1)
    below_z = jnp.concatenate([last_plane, face_z[:-1]], axis=0)
    below_x, below_y = (lower_x(face_x), lower_y(face_y))
    faces = (face_x, face_y, face_z, below_x, below_y, below_z)
    diag = screening + face_z + below_z + face_x + below_x + face_y + below_y
    density = targets[0][None] * sources
    fields = [sweep_rimmed(density[s : s + 1], faces, diag, weights) for s in range(NSRC)]
    field = jnp.concatenate(fields, axis=0)
    results = [jnp.sum(field * sources, axis=0)]
    return jnp.stack(results)


def solution(mesh):
    in_specs = (
        P("orb", "slab", None, None),
        P("orb"),
        P(),
        P(None, "slab", None, None),
        P("slab", None, None),
    )
    out_specs = P("orb", "slab", None, None)
    return jax.shard_map(shards, mesh=mesh, in_specs=in_specs, out_specs=out_specs, check_vma=False)
```

profile of v0, /device:TPU:0, one launch (start us, length us, event | category | flops | bytes accessed | tf_op | source)
XLA Modules:
  0.0 196.2 jit_solution(3746264836589793208)
XLA Ops:
  6.5 0.7 slice_bitcast_fusion.1
  7.3 4.9 %collective-permute-start = (f32[1,32,128]{2,1,0:T(8,128)S(1)}, f32[1,32,128]{2,1,0:T(8,128)S(1)}, u32[]{:S(2)}, u32[]{:S(2)}) collective-permute-start(f32[1,32,128]{2,1,0:T(8,128)S(1)} %slice_bitcast_fusion.1), channel_id=1, source_target_pairs={{0,1},{1,2},{2,3},{4,5},{5,6},{6,7},{8,9},{9,10},{10,11},{12,13},{... | collective-permute-start | bytes 49160 | tf_op jit(solution)/shard_map/ppermute | solution.py:37
  20.8 1.8 fusion.186
  22.7 1.0 copy-done
  23.7 54.0 %all-reduce.65.cloned.1.call-done = (f32[1,8,32,128]{3,2,1,0:T(8,128)}, f32[1,8,32,128]{3,2,1,0:T(8,128)}, f32[1,8,32,128]{3,2,1,0:T(8,128)}) async-done(((f32[1,8,32,128]{3,2,1,0:T(8,128)}, f32[1,8,32,128]{3,2,1,0:T(8,128)}, f32[1,8,32,128]{3,2,1,0:T(8,128)}), (f32[1,8,32,128]{3,2,1,0:T(8,128)}, f32[1,8,32,128]{3,2,1,0:T(8,128)}, f32[1,8,32,128]{3,2,1,0:T(8,128)})) %all-reduce.65.cloned.1.call-update) | async-done | bytes 393232 | tf_op jit(solution)/shard_map/psum | solution.py:31
  77.7 0.9 constant_dynamic-update-slice_fusion.2
  78.7 0.9 copy-done.2
  79.6 0.8 copy-done.1
  80.6 1.3 collective-permute-start.1
  81.9 4.5 %collective-permute-start.2 = (f32[1,1,32,128]{3,2,1,0:T(8,128)S(1)}, f32[1,1,32,128]{3,2,1,0:T(8,128)S(1)}, u32[]{:S(2)}, u32[]{:S(2)}) collective-permute-start(f32[1,1,32,128]{3,2,1,0:T(8,128)S(1)} %get-tuple-element.60), channel_id=1, source_target_pairs={{0,1},{1,2},{2,3},{4,5},{5,6},{6,7},{8,9},{9,10},{10,11},{12,13},{... | collective-permute-start | bytes 49160 | tf_op jit(solution)/shard_map/ppermute | solution.py:20
  86.6 1.3 collective-permute-done.2
  88.2 1.3 collective-permute-start.3
  89.5 4.8 %collective-permute-start.4 = (f32[1,1,32,128]{3,2,1,0:T(8,128)S(1)}, f32[1,1,32,128]{3,2,1,0:T(8,128)S(1)}, u32[]{:S(2)}, u32[]{:S(2)}) collective-permute-start(f32[1,1,32,128]{3,2,1,0:T(8,128)S(1)} %get-tuple-element.54), channel_id=1, source_target_pairs={{0,1},{1,2},{2,3},{4,5},{5,6},{6,7},{8,9},{9,10},{10,11},{12,13},{... | collective-permute-start | bytes 49160 | tf_op jit(solution)/shard_map/ppermute | solution.py:20
  94.4 1.3 collective-permute-done.4
  96.0 1.3 collective-permute-start.5
  97.3 4.8 %collective-permute-start.6 = (f32[1,1,32,128]{3,2,1,0:T(8,128)S(1)}, f32[1,1,32,128]{3,2,1,0:T(8,128)S(1)}, u32[]{:S(2)}, u32[]{:S(2)}) collective-permute-start(f32[1,1,32,128]{3,2,1,0:T(8,128)S(1)} %get-tuple-element.48), channel_id=1, source_target_pairs={{0,1},{1,2},{2,3},{4,5},{5,6},{6,7},{8,9},{9,10},{10,11},{12,13},{... | collective-permute-start | bytes 49160 | tf_op jit(solution)/shard_map/ppermute | solution.py:20
  102.2 1.3 collective-permute-done.6
  103.8 1.3 collective-permute-start.7
  105.1 4.8 %collective-permute-start.8 = (f32[1,1,32,128]{3,2,1,0:T(8,128)S(1)}, f32[1,1,32,128]{3,2,1,0:T(8,128)S(1)}, u32[]{:S(2)}, u32[]{:S(2)}) collective-permute-start(f32[1,1,32,128]{3,2,1,0:T(8,128)S(1)} %get-tuple-element.42), channel_id=1, source_target_pairs={{0,1},{1,2},{2,3},{4,5},{5,6},{6,7},{8,9},{9,10},{10,11},{12,13},{... | collective-permute-start | bytes 49160 | tf_op jit(solution)/shard_map/ppermute | solution.py:20
  110.1 1.3 collective-permute-done.8
  111.8 1.3 collective-permute-start.11
  113.1 4.8 %collective-permute-start.12 = (f32[1,1,32,128]{3,2,1,0:T(8,128)S(1)}, f32[1,1,32,128]{3,2,1,0:T(8,128)S(1)}, u32[]{:S(2)}, u32[]{:S(2)}) collective-permute-start(f32[1,1,32,128]{3,2,1,0:T(8,128)S(1)} %get-tuple-element.90), channel_id=1, source_target_pairs={{0,1},{1,2},{2,3},{4,5},{5,6},{6,7},{8,9},{9,10},{10,11},{12,13},{... | collective-permute-start | bytes 49160 | tf_op jit(solution)/shard_map/ppermute | solution.py:20
  117.9 3.9 %collective-permute-start.10 = (f32[1,1,32,128]{3,2,1,0:T(8,128)S(1)}, f32[1,1,32,128]{3,2,1,0:T(8,128)S(1)}, u32[]{:S(2)}, u32[]{:S(2)}) collective-permute-start(f32[1,1,32,128]{3,2,1,0:T(8,128)S(1)} %get-tuple-element.36), channel_id=1, source_target_pairs={{0,1},{1,2},{2,3},{4,5},{5,6},{6,7},{8,9},{9,10},{10,11},{12,13},{... | collective-permute-start | bytes 49160 | tf_op jit(solution)/shard_map/ppermute | solution.py:20
  121.9 1.3 collective-permute-start.9
  123.6 3.9 %collective-permute-done.9 = f32[1,1,32,128]{3,2,1,0:T(8,128)S(1)} collective-permute-done((f32[1,1,32,128]{3,2,1,0:T(8,128)S(1)}, f32[1,1,32,128]{3,2,1,0:T(8,128)S(1)}, u32[]{:S(2)}, u32[]{:S(2)}) %collective-permute-start.9) | collective-permute-done | bytes 16416 | tf_op jit(solution)/shard_map/ppermute | solution.py:22
  127.8 1.3 collective-permute-start.13
  129.2 4.5 %collective-permute-start.14 = (f32[1,1,32,128]{3,2,1,0:T(8,128)S(1)}, f32[1,1,32,128]{3,2,1,0:T(8,128)S(1)}, u32[]{:S(2)}, u32[]{:S(2)}) collective-permute-start(f32[1,1,32,128]{3,2,1,0:T(8,128)S(1)} %get-tuple-element.84), channel_id=1, source_target_pairs={{0,1},{1,2},{2,3},{4,5},{5,6},{6,7},{8,9},{9,10},{10,11},{12,13},{... | collective-permute-start | bytes 49160 | tf_op jit(solution)/shard_map/ppermute | solution.py:20
  133.7 1.3 collective-permute-start.21
  135.0 4.6 %collective-permute-start.22 = (f32[1,1,32,128]{3,2,1,0:T(8,128)S(1)}, f32[1,1,32,128]{3,2,1,0:T(8,128)S(1)}, u32[]{:S(2)}, u32[]{:S(2)}) collective-permute-start(f32[1,1,32,128]{3,2,1,0:T(8,128)S(1)} %get-tuple-element.120), channel_id=1, source_target_pairs={{0,1},{1,2},{2,3},{4,5},{5,6},{6,7},{8,9},{9,10},{10,11},{12,13},{... | collective-permute-start | bytes 49160 | tf_op jit(solution)/shard_map/ppermute | solution.py:20
  140.0 1.0 collective-permute-done.22
  141.3 1.3 collective-permute-start.15
  142.6 4.8 %collective-permute-start.16 = (f32[1,1,32,128]{3,2,1,0:T(8,128)S(1)}, f32[1,1,32,128]{3,2,1,0:T(8,128)S(1)}, u32[]{:S(2)}, u32[]{:S(2)}) collective-permute-start(f32[1,1,32,128]{3,2,1,0:T(8,128)S(1)} %get-tuple-element.78), channel_id=1, source_target_pairs={{0,1},{1,2},{2,3},{4,5},{5,6},{6,7},{8,9},{9,10},{10,11},{12,13},{... | collective-permute-start | bytes 49160 | tf_op jit(solution)/shard_map/ppermute | solution.py:20
  147.5 1.3 collective-permute-start.23
  148.8 4.6 %collective-permute-start.24 = (f32[1,1,32,128]{3,2,1,0:T(8,128)S(1)}, f32[1,1,32,128]{3,2,1,0:T(8,128)S(1)}, u32[]{:S(2)}, u32[]{:S(2)}) collective-permute-start(f32[1,1,32,128]{3,2,1,0:T(8,128)S(1)} %get-tuple-element.114), channel_id=1, source_target_pairs={{0,1},{1,2},{2,3},{4,5},{5,6},{6,7},{8,9},{9,10},{10,11},{12,13},{... | collective-permute-start | bytes 49160 | tf_op jit(solution)/shard_map/ppermute | solution.py:20
  153.7 1.0 collective-permute-done.24
  155.1 1.3 collective-permute-start.17
  156.4 4.8 %collective-permute-start.18 = (f32[1,1,32,128]{3,2,1,0:T(8,128)S(1)}, f32[1,1,32,128]{3,2,1,0:T(8,128)S(1)}, u32[]{:S(2)}, u32[]{:S(2)}) collective-permute-start(f32[1,1,32,128]{3,2,1,0:T(8,128)S(1)} %get-tuple-element.72), channel_id=1, source_target_pairs={{0,1},{1,2},{2,3},{4,5},{5,6},{6,7},{8,9},{9,10},{10,11},{12,13},{... | collective-permute-start | bytes 49160 | tf_op jit(solution)/shard_map/ppermute | solution.py:20
  161.3 1.3 collective-permute-start.25
  162.6 4.6 %collective-permute-start.26 = (f32[1,1,32,128]{3,2,1,0:T(8,128)S(1)}, f32[1,1,32,128]{3,2,1,0:T(8,128)S(1)}, u32[]{:S(2)}, u32[]{:S(2)}) collective-permute-start(f32[1,1,32,128]{3,2,1,0:T(8,128)S(1)} %get-tuple-element.108), channel_id=1, source_target_pairs={{0,1},{1,2},{2,3},{4,5},{5,6},{6,7},{8,9},{9,10},{10,11},{12,13},{... | collective-permute-start | bytes 49160 | tf_op jit(solution)/shard_map/ppermute | solution.py:20
  167.5 1.0 collective-permute-done.26
  168.9 1.3 collective-permute-start.27
  170.2 4.8 %collective-permute-start.28 = (f32[1,1,32,128]{3,2,1,0:T(8,128)S(1)}, f32[1,1,32,128]{3,2,1,0:T(8,128)S(1)}, u32[]{:S(2)}, u32[]{:S(2)}) collective-permute-start(f32[1,1,32,128]{3,2,1,0:T(8,128)S(1)} %get-tuple-element.102), channel_id=1, source_target_pairs={{0,1},{1,2},{2,3},{4,5},{5,6},{6,7},{8,9},{9,10},{10,11},{12,13},{... | collective-permute-start | bytes 49160 | tf_op jit(solution)/shard_map/ppermute | solution.py:20
  175.0 1.3 collective-permute-start.19
  176.3 4.6 %collective-permute-start.20 = (f32[1,1,32,128]{3,2,1,0:T(8,128)S(1)}, f32[1,1,32,128]{3,2,1,0:T(8,128)S(1)}, u32[]{:S(2)}, u32[]{:S(2)}) collective-permute-start(f32[1,1,32,128]{3,2,1,0:T(8,128)S(1)} %get-tuple-element.66), channel_id=1, source_target_pairs={{0,1},{1,2},{2,3},{4,5},{5,6},{6,7},{8,9},{9,10},{10,11},{12,13},{... | collective-permute-start | bytes 49160 | tf_op jit(solution)/shard_map/ppermute | solution.py:20
  181.2 1.3 collective-permute-start.29
  182.5 4.6 %collective-permute-start.30 = (f32[1,1,32,128]{3,2,1,0:T(8,128)S(1)}, f32[1,1,32,128]{3,2,1,0:T(8,128)S(1)}, u32[]{:S(2)}, u32[]{:S(2)}) collective-permute-start(f32[1,1,32,128]{3,2,1,0:T(8,128)S(1)} %get-tuple-element.96), channel_id=1, source_target_pairs={{0,1},{1,2},{2,3},{4,5},{5,6},{6,7},{8,9},{9,10},{10,11},{12,13},{... | collective-permute-start | bytes 49160 | tf_op jit(solution)/shard_map/ppermute | solution.py:20
  187.4 1.1 collective-permute-done.30
  188.7 0.7 fusion
  (96 shorter events, 5.8 us)
Async XLA Ops:
  6.5 71.2 %all-reduce.65.cloned.1.call-start = ((), (), s32[]{:S(2)}) async-start(), calls=%async_computation | async-start | bytes 786432 | tf_op jit(solution)/shard_map/psum | solution.py:31
  6.5 5.7 %copy-start.4 = (s32[3]{0:T(128)S(1)}, s32[3]{0:T(128)}, u32[]{:S(2)}) copy-start(s32[3]{0:T(128)} %param.7) | copy-start | bytes 40
  7.3 72.4 %collective-permute-start = (f32[1,32,128]{2,1,0:T(8,128)S(1)}, f32[1,32,128]{2,1,0:T(8,128)S(1)}, u32[]{:S(2)}, u32[]{:S(2)}) collective-permute-start(f32[1,32,128]{2,1,0:T(8,128)S(1)} %slice_bitcast_fusion.1), channel_id=1, source_target_pairs={{0,1},{1,2},{2,3},{4,5},{5,6},{6,7},{8,9},{9,10},{10,11},{12,13},{... | collective-permute-start | bytes 49160 | tf_op jit(solution)/shard_map/ppermute | solution.py:37
  22.7 1.0 copy-start
  77.7 1.0 copy-start.3
  78.7 0.9 copy-start.2
  79.6 0.9 copy-start.1
  80.6 6.0 %collective-permute-start.1 = (f32[1,1,32,128]{3,2,1,0:T(8,128)S(1)}, f32[1,1,32,128]{3,2,1,0:T(8,128)S(1)}, u32[]{:S(2)}, u32[]{:S(2)}) collective-permute-start(f32[1,1,32,128]{3,2,1,0:T(8,128)S(1)} %get-tuple-element.59), channel_id=1, source_target_pairs={{1,0},{2,1},{3,2},{5,4},{6,5},{7,6},{9,8},{10,9},{11,10},{13,12},{... | collective-permute-start | bytes 49160 | tf_op jit(solution)/shard_map/ppermute | solution.py:22
  81.9 6.0 %collective-permute-start.2 = (f32[1,1,32,128]{3,2,1,0:T(8,128)S(1)}, f32[1,1,32,128]{3,2,1,0:T(8,128)S(1)}, u32[]{:S(2)}, u32[]{:S(2)}) collective-permute-start(f32[1,1,32,128]{3,2,1,0:T(8,128)S(1)} %get-tuple-element.60), channel_id=1, source_target_pairs={{0,1},{1,2},{2,3},{4,5},{5,6},{6,7},{8,9},{9,10},{10,11},{12,13},{... | collective-permute-start | bytes 49160 | tf_op jit(solution)/shard_map/ppermute | solution.py:20
  88.2 6.2 %collective-permute-start.3 = (f32[1,1,32,128]{3,2,1,0:T(8,128)S(1)}, f32[1,1,32,128]{3,2,1,0:T(8,128)S(1)}, u32[]{:S(2)}, u32[]{:S(2)}) collective-permute-start(f32[1,1,32,128]{3,2,1,0:T(8,128)S(1)} %get-tuple-element.53), channel_id=1, source_target_pairs={{1,0},{2,1},{3,2},{5,4},{6,5},{7,6},{9,8},{10,9},{11,10},{13,12},{... | collective-permute-start | bytes 49160 | tf_op jit(solution)/shard_map/ppermute | solution.py:22
  89.5 6.3 %collective-permute-start.4 = (f32[1,1,32,128]{3,2,1,0:T(8,128)S(1)}, f32[1,1,32,128]{3,2,1,0:T(8,128)S(1)}, u32[]{:S(2)}, u32[]{:S(2)}) collective-permute-start(f32[1,1,32,128]{3,2,1,0:T(8,128)S(1)} %get-tuple-element.54), channel_id=1, source_target_pairs={{0,1},{1,2},{2,3},{4,5},{5,6},{6,7},{8,9},{9,10},{10,11},{12,13},{... | collective-permute-start | bytes 49160 | tf_op jit(solution)/shard_map/ppermute | solution.py:20
  96.0 6.2 %collective-permute-start.5 = (f32[1,1,32,128]{3,2,1,0:T(8,128)S(1)}, f32[1,1,32,128]{3,2,1,0:T(8,128)S(1)}, u32[]{:S(2)}, u32[]{:S(2)}) collective-permute-start(f32[1,1,32,128]{3,2,1,0:T(8,128)S(1)} %get-tuple-element.47), channel_id=1, source_target_pairs={{1,0},{2,1},{3,2},{5,4},{6,5},{7,6},{9,8},{10,9},{11,10},{13,12},{... | collective-permute-start | bytes 49160 | tf_op jit(solution)/shard_map/ppermute | solution.py:22
  97.3 6.3 %collective-permute-start.6 = (f32[1,1,32,128]{3,2,1,0:T(8,128)S(1)}, f32[1,1,32,128]{3,2,1,0:T(8,128)S(1)}, u32[]{:S(2)}, u32[]{:S(2)}) collective-permute-start(f32[1,1,32,128]{3,2,1,0:T(8,128)S(1)} %get-tuple-element.48), channel_id=1, source_target_pairs={{0,1},{1,2},{2,3},{4,5},{5,6},{6,7},{8,9},{9,10},{10,11},{12,13},{... | collective-permute-start | bytes 49160 | tf_op jit(solution)/shard_map/ppermute | solution.py:20
  103.8 6.2 %collective-permute-start.7 = (f32[1,1,32,128]{3,2,1,0:T(8,128)S(1)}, f32[1,1,32,128]{3,2,1,0:T(8,128)S(1)}, u32[]{:S(2)}, u32[]{:S(2)}) collective-permute-start(f32[1,1,32,128]{3,2,1,0:T(8,128)S(1)} %get-tuple-element.41), channel_id=1, source_target_pairs={{1,0},{2,1},{3,2},{5,4},{6,5},{7,6},{9,8},{10,9},{11,10},{13,12},{... | collective-permute-start | bytes 49160 | tf_op jit(solution)/shard_map/ppermute | solution.py:22
  105.1 6.3 %collective-permute-start.8 = (f32[1,1,32,128]{3,2,1,0:T(8,128)S(1)}, f32[1,1,32,128]{3,2,1,0:T(8,128)S(1)}, u32[]{:S(2)}, u32[]{:S(2)}) collective-permute-start(f32[1,1,32,128]{3,2,1,0:T(8,128)S(1)} %get-tuple-element.42), channel_id=1, source_target_pairs={{0,1},{1,2},{2,3},{4,5},{5,6},{6,7},{8,9},{9,10},{10,11},{12,13},{... | collective-permute-start | bytes 49160 | tf_op jit(solution)/shard_map/ppermute | solution.py:20
  111.8 11.4 %collective-permute-start.11 = (f32[1,1,32,128]{3,2,1,0:T(8,128)S(1)}, f32[1,1,32,128]{3,2,1,0:T(8,128)S(1)}, u32[]{:S(2)}, u32[]{:S(2)}) collective-permute-start(f32[1,1,32,128]{3,2,1,0:T(8,128)S(1)} %get-tuple-element.89), channel_id=1, source_target_pairs={{1,0},{2,1},{3,2},{5,4},{6,5},{7,6},{9,8},{10,9},{11,10},{13,12},{... | collective-permute-start | bytes 49160 | tf_op jit(solution)/shard_map/ppermute | solution.py:22
  113.1 10.1 %collective-permute-start.12 = (f32[1,1,32,128]{3,2,1,0:T(8,128)S(1)}, f32[1,1,32,128]{3,2,1,0:T(8,128)S(1)}, u32[]{:S(2)}, u32[]{:S(2)}) collective-permute-start(f32[1,1,32,128]{3,2,1,0:T(8,128)S(1)} %get-tuple-element.90), channel_id=1, source_target_pairs={{0,1},{1,2},{2,3},{4,5},{5,6},{6,7},{8,9},{9,10},{10,11},{12,13},{... | collective-permute-start | bytes 49160 | tf_op jit(solution)/shard_map/ppermute | solution.py:20
  117.9 5.6 %collective-permute-start.10 = (f32[1,1,32,128]{3,2,1,0:T(8,128)S(1)}, f32[1,1,32,128]{3,2,1,0:T(8,128)S(1)}, u32[]{:S(2)}, u32[]{:S(2)}) collective-permute-start(f32[1,1,32,128]{3,2,1,0:T(8,128)S(1)} %get-tuple-element.36), channel_id=1, source_target_pairs={{0,1},{1,2},{2,3},{4,5},{5,6},{6,7},{8,9},{9,10},{10,11},{12,13},{... | collective-permute-start | bytes 49160 | tf_op jit(solution)/shard_map/ppermute | solution.py:20
  121.9 5.6 %collective-permute-start.9 = (f32[1,1,32,128]{3,2,1,0:T(8,128)S(1)}, f32[1,1,32,128]{3,2,1,0:T(8,128)S(1)}, u32[]{:S(2)}, u32[]{:S(2)}) collective-permute-start(f32[1,1,32,128]{3,2,1,0:T(8,128)S(1)} %get-tuple-element.35), channel_id=1, source_target_pairs={{1,0},{2,1},{3,2},{5,4},{6,5},{7,6},{9,8},{10,9},{11,10},{13,12},{... | collective-permute-start | bytes 49160 | tf_op jit(solution)/shard_map/ppermute | solution.py:22
  127.8 11.7 %collective-permute-start.13 = (f32[1,1,32,128]{3,2,1,0:T(8,128)S(1)}, f32[1,1,32,128]{3,2,1,0:T(8,128)S(1)}, u32[]{:S(2)}, u32[]{:S(2)}) collective-permute-start(f32[1,1,32,128]{3,2,1,0:T(8,128)S(1)} %get-tuple-element.83), channel_id=1, source_target_pairs={{1,0},{2,1},{3,2},{5,4},{6,5},{7,6},{9,8},{10,9},{11,10},{13,12},{... | collective-permute-start | bytes 49160 | tf_op jit(solution)/shard_map/ppermute | solution.py:22
  129.2 10.4 %collective-permute-start.14 = (f32[1,1,32,128]{3,2,1,0:T(8,128)S(1)}, f32[1,1,32,128]{3,2,1,0:T(8,128)S(1)}, u32[]{:S(2)}, u32[]{:S(2)}) collective-permute-start(f32[1,1,32,128]{3,2,1,0:T(8,128)S(1)} %get-tuple-element.84), channel_id=1, source_target_pairs={{0,1},{1,2},{2,3},{4,5},{5,6},{6,7},{8,9},{9,10},{10,11},{12,13},{... | collective-permute-start | bytes 49160 | tf_op jit(solution)/shard_map/ppermute | solution.py:20
  133.7 6.2 %collective-permute-start.21 = (f32[1,1,32,128]{3,2,1,0:T(8,128)S(1)}, f32[1,1,32,128]{3,2,1,0:T(8,128)S(1)}, u32[]{:S(2)}, u32[]{:S(2)}) collective-permute-start(f32[1,1,32,128]{3,2,1,0:T(8,128)S(1)} %get-tuple-element.119), channel_id=1, source_target_pairs={{1,0},{2,1},{3,2},{5,4},{6,5},{7,6},{9,8},{10,9},{11,10},{13,12},{... | collective-permute-start | bytes 49160 | tf_op jit(solution)/shard_map/ppermute | solution.py:22
  135.0 6.0 %collective-permute-start.22 = (f32[1,1,32,128]{3,2,1,0:T(8,128)S(1)}, f32[1,1,32,128]{3,2,1,0:T(8,128)S(1)}, u32[]{:S(2)}, u32[]{:S(2)}) collective-permute-start(f32[1,1,32,128]{3,2,1,0:T(8,128)S(1)} %get-tuple-element.120), channel_id=1, source_target_pairs={{0,1},{1,2},{2,3},{4,5},{5,6},{6,7},{8,9},{9,10},{10,11},{12,13},{... | collective-permute-start | bytes 49160 | tf_op jit(solution)/shard_map/ppermute | solution.py:20
  141.3 12.0 %collective-permute-start.15 = (f32[1,1,32,128]{3,2,1,0:T(8,128)S(1)}, f32[1,1,32,128]{3,2,1,0:T(8,128)S(1)}, u32[]{:S(2)}, u32[]{:S(2)}) collective-permute-start(f32[1,1,32,128]{3,2,1,0:T(8,128)S(1)} %get-tuple-element.77), channel_id=1, source_target_pairs={{1,0},{2,1},{3,2},{5,4},{6,5},{7,6},{9,8},{10,9},{11,10},{13,12},{... | collective-permute-start | bytes 49160 | tf_op jit(solution)/shard_map/ppermute | solution.py:22
  142.6 10.7 %collective-permute-start.16 = (f32[1,1,32,128]{3,2,1,0:T(8,128)S(1)}, f32[1,1,32,128]{3,2,1,0:T(8,128)S(1)}, u32[]{:S(2)}, u32[]{:S(2)}) collective-permute-start(f32[1,1,32,128]{3,2,1,0:T(8,128)S(1)} %get-tuple-element.78), channel_id=1, source_target_pairs={{0,1},{1,2},{2,3},{4,5},{5,6},{6,7},{8,9},{9,10},{10,11},{12,13},{... | collective-permute-start | bytes 49160 | tf_op jit(solution)/shard_map/ppermute | solution.py:20
  147.5 6.2 %collective-permute-start.23 = (f32[1,1,32,128]{3,2,1,0:T(8,128)S(1)}, f32[1,1,32,128]{3,2,1,0:T(8,128)S(1)}, u32[]{:S(2)}, u32[]{:S(2)}) collective-permute-start(f32[1,1,32,128]{3,2,1,0:T(8,128)S(1)} %get-tuple-element.113), channel_id=1, source_target_pairs={{1,0},{2,1},{3,2},{5,4},{6,5},{7,6},{9,8},{10,9},{11,10},{13,12},{... | collective-permute-start | bytes 49160 | tf_op jit(solution)/shard_map/ppermute | solution.py:22
  148.8 6.0 %collective-permute-start.24 = (f32[1,1,32,128]{3,2,1,0:T(8,128)S(1)}, f32[1,1,32,128]{3,2,1,0:T(8,128)S(1)}, u32[]{:S(2)}, u32[]{:S(2)}) collective-permute-start(f32[1,1,32,128]{3,2,1,0:T(8,128)S(1)} %get-tuple-element.114), channel_id=1, source_target_pairs={{0,1},{1,2},{2,3},{4,5},{5,6},{6,7},{8,9},{9,10},{10,11},{12,13},{... | collective-permute-start | bytes 49160 | tf_op jit(solution)/shard_map/ppermute | solution.py:20
  155.1 12.0 %collective-permute-start.17 = (f32[1,1,32,128]{3,2,1,0:T(8,128)S(1)}, f32[1,1,32,128]{3,2,1,0:T(8,128)S(1)}, u32[]{:S(2)}, u32[]{:S(2)}) collective-permute-start(f32[1,1,32,128]{3,2,1,0:T(8,128)S(1)} %get-tuple-element.71), channel_id=1, source_target_pairs={{1,0},{2,1},{3,2},{5,4},{6,5},{7,6},{9,8},{10,9},{11,10},{13,12},{... | collective-permute-start | bytes 49160 | tf_op jit(solution)/shard_map/ppermute | solution.py:22
  156.4 10.7 %collective-permute-start.18 = (f32[1,1,32,128]{3,2,1,0:T(8,128)S(1)}, f32[1,1,32,128]{3,2,1,0:T(8,128)S(1)}, u32[]{:S(2)}, u32[]{:S(2)}) collective-permute-start(f32[1,1,32,128]{3,2,1,0:T(8,128)S(1)} %get-tuple-element.72), channel_id=1, source_target_pairs={{0,1},{1,2},{2,3},{4,5},{5,6},{6,7},{8,9},{9,10},{10,11},{12,13},{... | collective-permute-start | bytes 49160 | tf_op jit(solution)/shard_map/ppermute | solution.py:20
  161.3 6.2 %collective-permute-start.25 = (f32[1,1,32,128]{3,2,1,0:T(8,128)S(1)}, f32[1,1,32,128]{3,2,1,0:T(8,128)S(1)}, u32[]{:S(2)}, u32[]{:S(2)}) collective-permute-start(f32[1,1,32,128]{3,2,1,0:T(8,128)S(1)} %get-tuple-element.107), channel_id=1, source_target_pairs={{1,0},{2,1},{3,2},{5,4},{6,5},{7,6},{9,8},{10,9},{11,10},{13,12},{... | collective-permute-start | bytes 49160 | tf_op jit(solution)/shard_map/ppermute | solution.py:22
  162.6 6.0 %collective-permute-start.26 = (f32[1,1,32,128]{3,2,1,0:T(8,128)S(1)}, f32[1,1,32,128]{3,2,1,0:T(8,128)S(1)}, u32[]{:S(2)}, u32[]{:S(2)}) collective-permute-start(f32[1,1,32,128]{3,2,1,0:T(8,128)S(1)} %get-tuple-element.108), channel_id=1, source_target_pairs={{0,1},{1,2},{2,3},{4,5},{5,6},{6,7},{8,9},{9,10},{10,11},{12,13},{... | collective-permute-start | bytes 49160 | tf_op jit(solution)/shard_map/ppermute | solution.py:20
  168.9 12.0 %collective-permute-start.27 = (f32[1,1,32,128]{3,2,1,0:T(8,128)S(1)}, f32[1,1,32,128]{3,2,1,0:T(8,128)S(1)}, u32[]{:S(2)}, u32[]{:S(2)}) collective-permute-start(f32[1,1,32,128]{3,2,1,0:T(8,128)S(1)} %get-tuple-element.101), channel_id=1, source_target_pairs={{1,0},{2,1},{3,2},{5,4},{6,5},{7,6},{9,8},{10,9},{11,10},{13,12},{... | collective-permute-start | bytes 49160 | tf_op jit(solution)/shard_map/ppermute | solution.py:22
  170.2 10.7 %collective-permute-start.28 = (f32[1,1,32,128]{3,2,1,0:T(8,128)S(1)}, f32[1,1,32,128]{3,2,1,0:T(8,128)S(1)}, u32[]{:S(2)}, u32[]{:S(2)}) collective-permute-start(f32[1,1,32,128]{3,2,1,0:T(8,128)S(1)} %get-tuple-element.102), channel_id=1, source_target_pairs={{0,1},{1,2},{2,3},{4,5},{5,6},{6,7},{8,9},{9,10},{10,11},{12,13},{... | collective-permute-start | bytes 49160 | tf_op jit(solution)/shard_map/ppermute | solution.py:20
  175.0 12.0 %collective-permute-start.19 = (f32[1,1,32,128]{3,2,1,0:T(8,128)S(1)}, f32[1,1,32,128]{3,2,1,0:T(8,128)S(1)}, u32[]{:S(2)}, u32[]{:S(2)}) collective-permute-start(f32[1,1,32,128]{3,2,1,0:T(8,128)S(1)} %get-tuple-element.65), channel_id=1, source_target_pairs={{1,0},{2,1},{3,2},{5,4},{6,5},{7,6},{9,8},{10,9},{11,10},{13,12},{... | collective-permute-start | bytes 49160 | tf_op jit(solution)/shard_map/ppermute | solution.py:22
  176.3 10.7 %collective-permute-start.20 = (f32[1,1,32,128]{3,2,1,0:T(8,128)S(1)}, f32[1,1,32,128]{3,2,1,0:T(8,128)S(1)}, u32[]{:S(2)}, u32[]{:S(2)}) collective-permute-start(f32[1,1,32,128]{3,2,1,0:T(8,128)S(1)} %get-tuple-element.66), channel_id=1, source_target_pairs={{0,1},{1,2},{2,3},{4,5},{5,6},{6,7},{8,9},{9,10},{10,11},{12,13},{... | collective-permute-start | bytes 49160 | tf_op jit(solution)/shard_map/ppermute | solution.py:20
  181.2 6.2 %collective-permute-start.29 = (f32[1,1,32,128]{3,2,1,0:T(8,128)S(1)}, f32[1,1,32,128]{3,2,1,0:T(8,128)S(1)}, u32[]{:S(2)}, u32[]{:S(2)}) collective-permute-start(f32[1,1,32,128]{3,2,1,0:T(8,128)S(1)} %get-tuple-element.95), channel_id=1, source_target_pairs={{1,0},{2,1},{3,2},{5,4},{6,5},{7,6},{9,8},{10,9},{11,10},{13,12},{... | collective-permute-start | bytes 49160 | tf_op jit(solution)/shard_map/ppermute | solution.py:22
  182.5 6.0 %collective-permute-start.30 = (f32[1,1,32,128]{3,2,1,0:T(8,128)S(1)}, f32[1,1,32,128]{3,2,1,0:T(8,128)S(1)}, u32[]{:S(2)}, u32[]{:S(2)}) collective-permute-start(f32[1,1,32,128]{3,2,1,0:T(8,128)S(1)} %get-tuple-element.96), channel_id=1, source_target_pairs={{0,1},{1,2},{2,3},{4,5},{5,6},{6,7},{8,9},{9,10},{10,11},{12,13},{... | collective-permute-start | bytes 49160 | tf_op jit(solution)/shard_map/ppermute | solution.py:20
Sparse Core Ops, SparseCore 0:
  22.8 54.8 all-reduce.64
where the time goes:
time: 198 us; the launch traced here: 196 us
  starting transfers between devices  93.9 us (47%)
  waiting for transfers between devices  67.4 us (34%)
  between operations  22.3 us (11%)
  local copies, waits for them, and re-layouts  6.69 us (3%)
  other arithmetic  5.98 us (3%)
    ppermute x15, starting transfers between devices, extended(): lax.ppermute(tail, axis, [(i, (i + 1) % count) for i in range(ends)])  69.6 us
    psum x1, waiting for transfers between devices, spread(): return lax.psum(kept, axis)  54 us
    ppermute x15, starting transfers between devices, extended(): lax.ppermute(head, axis, [((i + 1) % count, i) for i in range(ends)])  19.4 us
    ppermute x15, waiting for transfers between devices, extended(): lax.ppermute(tail, axis, [(i, (i + 1) % count) for i in range(ends)])  9.47 us
    ppermute x1, starting transfers between devices, shifted(): return lax.ppermute(array, axis, pairs)  4.92 us
    ppermute x15, waiting for transfers between devices, extended(): lax.ppermute(head, axis, [((i + 1) % count, i) for i in range(ends)])  3.98 us
  transfers between devices with their start and end apart: 32, of which 10 were waited for; matrix products, arithmetic and copies ran while one was open for 3% of the time, Pallas kernels for 0%

commit v1 on v0

v1 whole, which is shorter than its diff:
```python
import functools
import math

import jax
import jax.numpy as jnp
from jax import lax
from jax.experimental import pallas as pl
from jax.experimental.pallas import tpu as pltpu
from jax.sharding import PartitionSpec as P

NSRC = 3
SWEEPS = 6
HALO = SWEEPS - 1
AXES = ("orb", "slab")
VMEM = pl.BlockSpec(memory_space=pltpu.VMEM)
SMEM = pl.BlockSpec(memory_space=pltpu.SMEM)


def step_sizes(count):
    return [
        1.0 / (1.025 + 0.975 * math.cos(math.pi * (2 * k + 1) / (2 * count))) for k in range(count)
    ]


def call(kernel, out_shapes, in_specs, scratch=(), flops=0, moved=0):
    return pl.pallas_call(
        kernel,
        out_shape=[jax.ShapeDtypeStruct(s, jnp.float32) for s in out_shapes],
        in_specs=in_specs,
        out_specs=[VMEM] * len(out_shapes),
        scratch_shapes=list(scratch),
        compiler_params=pltpu.CompilerParams(vmem_limit_bytes=16 << 20),
        cost_estimate=pl.CostEstimate(flops=flops, transcendentals=0, bytes_accessed=moved),
    )


def pick_kernel(where, index, row, pool, send, own):
    orb, core = where[0], where[1]
    held, planes = pool.shape[0], pool.shape[1]
    mine = core * (planes - HALO)
    other = (1 - core) * (planes - HALO)
    for out, start in ((send, other), (own, mine)):
        for s in range(NSRC):
            held_here = index[s] // held == orb
            cells = pool[index[s] % held, pl.ds(start, HALO)]
            out[s] = jnp.where(held_here, cells, 0.0)
        out[NSRC] = pool[row[0], pl.ds(start, HALO)]


def coefficient_kernel(
    where, row, pool, metric, screening, near, far, coef, scaled, fx, fy, fz, scr, tgt
):
    core, slab, slabs = where[1], where[2], where[3]
    planes, gx, gy = screening.shape
    total = planes + 2 * HALO
    lower = core * (HALO + planes)
    upper = (1 - core) * (HALO + planes)
    h = HALO
    for halo, at, own_slot in ((near, lower, 5 * h + 1), (far, upper, 4 * h + 1)):
        scr[pl.ds(at, h)] = halo[0:h]
        fx[pl.ds(at, h)] = halo[h : 2 * h]
        fy[pl.ds(at, h)] = halo[2 * h : 3 * h]
        tgt[pl.ds(at, h)] = halo[own_slot : own_slot + h]
    low_z = jnp.where(core == 0, near[3 * h : 4 * h + 1], far[3 * h : 4 * h + 1])
    high_z = jnp.where(core == 0, far[3 * h : 4 * h], near[3 * h : 4 * h])
    fz[0 : h + 1] = low_z
    fz[h + 1 : h + 1 + planes] = metric[2]
    fz[h + 1 + planes :] = high_z
    scr[h : h + planes] = screening[...]
    fx[h : h + planes] = metric[0]
    fy[h : h + planes] = metric[1]
    tgt[h : h + planes] = pool[row[0]]
    first = jnp.where(slab == 0, h, 0)
    last = jnp.where(slab == slabs - 1, h + planes, total)
    x_id = lax.broadcasted_iota(jnp.int32, (gx, gy), 0)
    y_id = lax.broadcasted_iota(jnp.int32, (gx, gy), 1)

    @pl.loop(0, total)
    def _(e):
        z_hi, z_lo = fz[e + 1], fz[e]
        x_hi, y_hi = fx[e], fy[e]
        x_lo = jnp.where(x_id == 0, 0.0, pltpu.roll(x_hi, 1, 0))
        y_lo = jnp.where(y_id == 0, 0.0, pltpu.roll(y_hi, 1, 1))
        diag = scr[e] + z_hi + z_lo + x_hi + x_lo + y_hi + y_lo
        inside = jnp.logical_and(e >= first, e < last)
        inverse = 1.0 / jnp.where(inside, diag, 1.0)
        inverse = jnp.where(inside, inverse, 0.0)
        rows = pl.ds(pl.multiple_of(e * gx, gx), gx)
        coef[0, rows] = z_hi * inverse
        coef[1, rows] = z_lo * inverse
        coef[2, rows] = jnp.where(x_id == gx - 1, 0.0, x_hi * inverse)
        coef[3, rows] = x_lo * inverse
        coef[4, rows] = jnp.where(y_id == gy - 1, 0.0, y_hi * inverse)
        coef[5, rows] = y_lo * inverse
        scaled[rows] = tgt[e] * inverse


def sweep_kernel(weights, where, coef, scaled, middle, halo, sibling, out, src, base, ping, pong):
    core = where[1]
    h = HALO
    gx, gy = out.shape[-2:]
    planes = out.shape[1]
    total = planes + 2 * h
    extra = middle.shape[1]
    kept = planes
    halo_at = core * (h + planes)
    middle_at = h + core * (planes - extra)
    sibling_at = (1 - core) * (h + extra)
    for part, at in ((halo, halo_at), (middle, middle_at), (sibling, sibling_at)):
        count = part.shape[1]
        for s in range(NSRC):
            src[s, pl.ds(pl.multiple_of(at * gx, gx), count * gx)] = part[s].reshape(count * gx, gy)

    @pl.loop(0, total)
    def _(e):
        rows = pl.ds(pl.multiple_of(e * gx, gx), gx)
        t = scaled[rows]
        for s in range(NSRC):
            b = t * src[s, rows]
            base[s, rows] = b
            ping[s, rows] = weights[0] * b

    old, new = ping, pong
    for k in range(1, SWEEPS):
        w = weights[k]
        lastly = k == SWEEPS - 1

        @pl.loop(k, total - k)
        def _(e):
            start = pl.multiple_of(e * gx, gx)
            for j in range(0, gx, 8):
                at = start + j
                rows = pl.ds(at, 8)
                c = [coef[i, rows] for i in range(6)]
                acc = None
                for s in range(NSRC):
                    v = old[s, rows]
                    total_s = base[s, rows]
                    total_s += c[0] * old[s, pl.ds(at + gx, 8)]
                    total_s += c[1] * old[s, pl.ds(at - gx, 8)]
                    total_s += c[2] * old[s, pl.ds(at + 1, 8)]
                    total_s += c[3] * old[s, pl.ds(at - 1, 8)]
                    total_s += c[4] * pltpu.roll(v, gy - 1, 1)
                    total_s += c[5] * pltpu.roll(v, 1, 1)
                    v = (1.0 - w) * v + w * total_s
                    if lastly:
                        term = v * src[s, rows]
                        acc = term if acc is None else acc + term
                    else:
                        new[s, rows] = v
                if lastly:
                    out[0, e - h, j : j + 8] = acc

        old, new = new, old


def shards(pool, target_row, source_index, metric, screening):
    held, planes, gx, gy = pool.shape
    n_orb, n_slab = lax.axis_size("orb"), lax.axis_size("slab")
    h = HALO
    weights = step_sizes(SWEEPS)
    orb, slab = lax.axis_index("orb"), lax.axis_index("slab")
    core = orb % 2
    where = jnp.stack([orb, core, slab, jnp.int32(n_slab)])

    def place(o, z):
        return o * n_slab + z

    def among(moved):
        pairs = [
            (place(o, z), place(*moved(o, z)))
            for o in range(n_orb)
            for z in range(n_slab)
            if 0 <= moved(o, z)[1] < n_slab
        ]
        return lambda x: lax.ppermute(x, AXES, pairs)

    to_sibling = among(lambda o, z: (o ^ 1, z))
    to_slab = among(lambda o, z: (o ^ 1, z + 1 if o % 2 else z - 1))
    bits = [1 << b for b in range(1, n_orb.bit_length() - 1)]

    send, own = call(
        pick_kernel,
        [(NSRC + 1, h, gx, gy)] * 2,
        [SMEM, SMEM, SMEM, VMEM],
    )(where, source_index, target_row, pool)
    got = to_sibling(send)
    part = own[:NSRC] + got[:NSRC]
    start = core * (planes - h)
    near_z = core * (planes - h - 1)
    half = functools.partial(lax.dynamic_slice_in_dim, start_index=start, slice_size=h, axis=0)
    edge = jnp.concatenate(
        [
            half(screening),
            half(metric[0]),
            half(metric[1]),
            lax.dynamic_slice_in_dim(metric[2], near_z, h + 1, axis=0),
            own[NSRC],
            got[NSRC],
        ],
        axis=0,
    )
    near = to_slab(edge)
    for low, high in zip(bits, reversed(bits)):
        part = part + among(lambda o, z: (o ^ (high if o % 2 else low), z))(part)
    halo = to_slab(part)
    far = to_sibling(near[: 5 * h + 1])
    kept = planes - h
    lacks = jnp.where(
        core == 0,
        jnp.concatenate([halo, part[:, :kept]], axis=1),
        jnp.concatenate([part[:, h - kept :], halo], axis=1),
    )
    sibling = to_sibling(lacks)
    total = planes + 2 * h
    coef, scaled = call(
        coefficient_kernel,
        [(6, total * gx, gy), (total * gx, gy)],
        [SMEM, SMEM] + [VMEM] * 5,
        [pltpu.VMEM((total, gx, gy), jnp.float32)] * 2
        + [pltpu.VMEM((total + 1, gx, gy), jnp.float32)]
        + [pltpu.VMEM((total, gx, gy), jnp.float32)] * 2,
    )(where, target_row, pool, metric, screening, near, far)
    field = pltpu.VMEM((NSRC, total * gx, gy), jnp.float32)
    (out,) = call(
        functools.partial(sweep_kernel, weights),
        [(1, planes, gx, gy)],
        [SMEM] + [VMEM] * 5,
        [field] * 4,
    )(where, coef, scaled, part, halo, sibling)
    return out


def solution(mesh):
    in_specs = (
        P("orb", "slab", None, None),
        P("orb"),
        P(),
        P(None, "slab", None, None),
        P("slab", None, None),
    )
    out_specs = P("orb", "slab", None, None)
    return jax.shard_map(shards, mesh=mesh, in_specs=in_specs, out_specs=out_specs, check_vma=False)
```

time: 198 us -> 36.8 us (0.19)
  starting transfers between devices: 93.9 us -> 14 us
  waiting for transfers between devices: 67.4 us -> 7.48 us
  between operations: 22.3 us -> 0.82 us
  Pallas kernels: 0 us -> 10.3 us
  other arithmetic: 5.98 us -> 0.24 us
  local copies, waits for them, and re-layouts: 6.69 us -> 3.68 us
    ppermute x31 -> x7, starting transfers between devices: 93.9 us -> 14 us  [among(): return lambda x: lax.ppermute(x, AXES, pairs)]
    psum x1 -> x0, waiting for transfers between devices: 54 us -> none  [spread(): return lax.psum(kept, axis)]
    pallas_call x0 -> x3, Pallas kernels: none -> 10.3 us  [the longest x1 7.54 us: shards(): call(functools.partial(sweep_kernel, weights), [(1, planes, gx, gy)], [SM...]
    ppermute x31 -> x7, waiting for transfers between devices: 13.5 us -> 7.48 us  [among(): return lambda x: lax.ppermute(x, AXES, pairs)]
    add x15 -> x3, other arithmetic: 3.27 us -> 0.12 us  [the longest x2 0.08 us: shards(): part = part + among(lambda o, z: (o ^ (high if o % 2 else low), z))(part)]
  transfers between devices with their start and end apart: 32 -> 7, of which waited for: 10 -> 2; matrix products, arithmetic and copies ran while one was open for 3% -> 6% of each run, Pallas kernels for 0% -> 6%
where the time goes in v1:
time: 36.8 us; the launch traced here: 36.6 us
  starting transfers between devices  14 us (38%)
  Pallas kernels  10.3 us (28%)
  waiting for transfers between devices  7.48 us (20%)
  local copies, waits for them, and re-layouts  3.68 us (10%)
  between operations  0.82 us (2%)
    ppermute x7, starting transfers between devices, among(): return lambda x: lax.ppermute(x, AXES, pairs)  14 us
    pallas_call x1, Pallas kernels, shards(): call(functools.partial(sweep_kernel, weights), [(1, planes, gx, gy)], [SM...  7.54 us
    ppermute x7, waiting for transfers between devices, among(): return lambda x: lax.ppermute(x, AXES, pairs)  7.48 us
    unnamed x15, local copies, waits for them, and re-layouts  2.57 us
    pallas_call x1, Pallas kernels, shards(): call(coefficient_kernel, [(6, total * gx, gy), (total * gx, gy)], [SMEM,...  2.18 us
    slice x1, local copies, waits for them, and re-layouts, shards(): metric[2]  1.06 us
  transfers between devices with their start and end apart: 7, of which 2 were waited for; matrix products, arithmetic and copies ran while one was open for 6% of the time, Pallas kernels for 6%

profile of v1, /device:TPU:0, one launch (start us, length us, event | category | flops | bytes accessed | tf_op | source)
XLA Modules:
  0.0 36.6 jit_solution(2492844861871277141)
XLA Ops:
  0.7 0.1 pad_add_fusion.where
  0.7 0.0 copy-start.1
  0.7 0.9 %copy-done.1 = f32[2,8,32,128]{3,2,1,0:T(8,128)S(1)} copy-done((f32[2,8,32,128]{3,2,1,0:T(8,128)S(1)}, f32[2,8,32,128]{3,2,1,0:T(8,128)}, u32[]{:S(2)}) %copy-start.1) | copy-done | bytes 262168
  1.7 0.0 copy-start.4
  1.7 0.7 %copy-done.4 = s32[3]{0:T(128)S(1)} copy-done((s32[3]{0:T(128)S(1)}, s32[3]{0:T(128)}, u32[]{:S(2)}) %copy-start.4) | copy-done | bytes 36
  2.3 0.6 %shard_map.55 = (f32[4,5,32,128]{3,2,1,0:T(8,128)S(1)}, f32[4,5,32,128]{3,2,1,0:T(8,128)S(1)}) custom-call(s32[4]{0:T(128)S(1)} %pad_add_fusion.where, s32[3]{0:T(128)S(1)} %copy-done.4, s32[1]{0:T(128)S(6)} %copy.11.row, f32[2,8,32,128]{3,2,1,0:T(8,128)S(1)} %copy-done.1), custom_call_target="tpu_custom_call" | custom-call | tf_op jit(solution)/shard_map/pallas_call | solution.py:182
  3.0 0.5 %collective-permute-start = (f32[4,5,32,128]{3,2,1,0:T(8,128)S(1)}, f32[4,5,32,128]{3,2,1,0:T(8,128)S(1)}, u32[]{:S(2)}, u32[]{:S(2)}) collective-permute-start(f32[4,5,32,128]{3,2,1,0:T(8,128)S(1)} %get-tuple-element.10), channel_id=1, source_target_pairs={{0,4},{1,5},{2,6},{3,7},{4,0},{5,1},{6,2},{7,3},{8,12},{9,13},{10,... | collective-permute-start | bytes 983048 | tf_op jit(solution)/shard_map/ppermute | solution.py:176
  3.5 1.1 %fusion.1 = (f32[1,8,32,128]{3,2,1,0:T(8,128)S(1)}, f32[1,8,32,128]{3,2,1,0:T(8,128)S(1)}, f32[1,8,32,128]{3,2,1,0:T(8,128)S(1)}) fusion(f32[3,8,32,128]{3,2,1,0:T(8,128)} %metric.1), kind=kLoop, calls=%fused_computation.10 | loop fusion | bytes 786432 | tf_op jit(solution)/shard_map/slice | solution.py:197
  4.6 0.9 %dynamic-slice_dynamic-update-slice_fusion = f32[31,32,128]{2,1,0:T(8,128)S(1)} fusion(f32[8,32,128]{2,1,0:T(8,128)} %screening.1, s32[]{:T(128)S(6)} %select_n.24), kind=kLoop, calls=%fused_computation.8 | loop fusion | bytes 163844
  5.5 0.0 collective-permute-done
  5.6 2.6 %collective-permute-start.3 = (f32[3,5,32,128]{3,2,1,0:T(8,128)S(1)}, f32[3,5,32,128]{3,2,1,0:T(8,128)S(1)}, u32[]{:S(2)}, u32[]{:S(2)}) collective-permute-start(f32[3,5,32,128]{3,2,1,0:T(8,128)S(1)} %slice_add_fusion), channel_id=1, source_target_pairs={{0,8},{1,9},{2,10},{3,11},{4,20},{5,21},{6,22},{7,23},{8,0},{9,1},... | collective-permute-start | bytes 737288 | tf_op jit(solution)/shard_map/ppermute | solution.py:176
  8.2 0.0 copy-start
  8.2 0.0 copy-start.2
  8.2 0.0 copy-start.3
  8.2 0.8 %collective-permute-start.1 = (f32[31,32,128]{2,1,0:T(8,128)S(1)}, f32[31,32,128]{2,1,0:T(8,128)S(1)}, u32[]{:S(2)}, u32[]{:S(2)}) collective-permute-start(f32[31,32,128]{2,1,0:T(8,128)S(1)} %fusion), channel_id=1, source_target_pairs={{1,4},{2,5},{3,6},{4,1},{5,2},{6,3},{9,12},{10,13},{11,14},{12,9},... | collective-permute-start | bytes 1523720 | tf_op jit(solution)/shard_map/ppermute | solution.py:176
  9.0 3.3 %collective-permute-done.3 = f32[3,5,32,128]{3,2,1,0:T(8,128)S(1)} collective-permute-done((f32[3,5,32,128]{3,2,1,0:T(8,128)S(1)}, f32[3,5,32,128]{3,2,1,0:T(8,128)S(1)}, u32[]{:S(2)}, u32[]{:S(2)}) %collective-permute-start.3) | collective-permute-done | bytes 245792 | tf_op jit(solution)/shard_map/ppermute | solution.py:176
  12.4 2.1 %collective-permute-start.4 = (f32[3,5,32,128]{3,2,1,0:T(8,128)S(1)}, f32[3,5,32,128]{3,2,1,0:T(8,128)S(1)}, u32[]{:S(2)}, u32[]{:S(2)}) collective-permute-start(f32[3,5,32,128]{3,2,1,0:T(8,128)S(1)} %add.25), channel_id=1, source_target_pairs={{0,16},{1,17},{2,18},{3,19},{4,12},{5,13},{6,14},{7,15},{8,24},{9,... | collective-permute-start | bytes 737288 | tf_op jit(solution)/shard_map/ppermute | solution.py:176
  14.5 4.2 %collective-permute-done.4 = f32[3,5,32,128]{3,2,1,0:T(8,128)S(1)} collective-permute-done((f32[3,5,32,128]{3,2,1,0:T(8,128)S(1)}, f32[3,5,32,128]{3,2,1,0:T(8,128)S(1)}, u32[]{:S(2)}, u32[]{:S(2)}) %collective-permute-start.4) | collective-permute-done | bytes 245792 | tf_op jit(solution)/shard_map/ppermute | solution.py:176
  18.7 0.7 %collective-permute-start.5 = (f32[3,5,32,128]{3,2,1,0:T(8,128)S(1)}, f32[3,5,32,128]{3,2,1,0:T(8,128)S(1)}, u32[]{:S(2)}, u32[]{:S(2)}) collective-permute-start(f32[3,5,32,128]{3,2,1,0:T(8,128)S(1)} %add.26.middle), channel_id=1, source_target_pairs={{1,4},{2,5},{3,6},{4,1},{5,2},{6,3},{9,12},{10,13},{11,14},{12,9},... | collective-permute-start | bytes 737288 | tf_op jit(solution)/shard_map/ppermute | solution.py:176
  19.4 0.0 collective-permute-done.1.near
  19.5 3.5 %collective-permute-start.2 = (f32[26,32,128]{2,1,0:T(8,128)S(1)}, f32[26,32,128]{2,1,0:T(8,128)S(1)}, u32[]{:S(2)}, u32[]{:S(2)}) collective-permute-start(f32[26,32,128]{2,1,0:T(8,128)S(1)} %slice.41), channel_id=1, source_target_pairs={{0,4},{1,5},{2,6},{3,7},{4,0},{5,1},{6,2},{7,3},{8,12},{9,13},{10,... | collective-permute-start | bytes 1277960 | tf_op jit(solution)/shard_map/ppermute | solution.py:176
  23.0 0.0 collective-permute-done.5.halo
  23.0 3.8 %collective-permute-start.6 = (f32[3,8,32,128]{3,2,1,0:T(8,128)S(1)}, f32[3,8,32,128]{3,2,1,0:T(8,128)S(1)}, u32[]{:S(2)}, u32[]{:S(2)}) collective-permute-start(f32[3,8,32,128]{3,2,1,0:T(8,128)S(1)} %maximum_select_fusion), channel_id=1, source_target_pairs={{0,4},{1,5},{2,6},{3,7},{4,0},{5,1},{6,2},{7,3},{8,12},{9,13},{10,... | collective-permute-start | bytes 1179656 | tf_op jit(solution)/shard_map/ppermute | solution.py:176
  26.8 0.0 collective-permute-done.2.far
  26.8 0.0 copy-done
  26.8 0.0 copy-done.2
  26.8 0.0 copy-done.3
  26.8 2.2 %shard_map.56 = (f32[6,576,128]{2,1,0:T(8,128)S(1)}, f32[576,128]{1,0:T(8,128)S(1)}) custom-call(s32[4]{0:T(128)S(1)} %pad_add_fusion.where, s32[1]{0:T(128)S(6)} %copy.11.row, f32[2,8,32,128]{3,2,1,0:T(8,128)S(1)} %copy-done.2, f32[3,8,32,128]{3,2,1,0:T(8,128)S(1)} %copy-done, f32[8,32,128]{2,1,0:T(8,128)S(1)} %copy-done.3, ...), custom_call_target="tpu_custom_call" | custom-call | tf_op jit(solution)/shard_map/pallas_call | solution.py:216
  29.0 0.0 collective-permute-done.6.sibling
  29.0 7.5 %shard_map.57 = f32[1,8,32,128]{3,2,1,0:T(8,128)} custom-call(s32[4]{0:T(128)S(1)} %pad_add_fusion.where, f32[6,576,128]{2,1,0:T(8,128)S(1)} %get-tuple-element.11.coef, f32[576,128]{1,0:T(8,128)S(1)} %get-tuple-element.12.scaled, f32[3,5,32,128]{3,2,1,0:T(8,128)S(1)} %add.26.middle, f32[3,5,32,128]{3,2,1,0:T(8,128)S(1)} %collective-permute-done.5.halo, ...), custom_call_target="tpu_custom_call" | custom-call | tf_op jit(solution)/shard_map/pallas_call | solution.py:225
  (11 shorter events, 0.3 us)
Async XLA Ops:
  0.7 1.0 %copy-start.1 = (f32[2,8,32,128]{3,2,1,0:T(8,128)S(1)}, f32[2,8,32,128]{3,2,1,0:T(8,128)}, u32[]{:S(2)}) copy-start(f32[2,8,32,128]{3,2,1,0:T(8,128)} %pool.3) | copy-start | bytes 786436
  1.7 0.7 %copy-start.4 = (s32[3]{0:T(128)S(1)}, s32[3]{0:T(128)}, u32[]{:S(2)}) copy-start(s32[3]{0:T(128)} %index.1) | copy-start | bytes 40
  3.0 2.5 %collective-permute-start = (f32[4,5,32,128]{3,2,1,0:T(8,128)S(1)}, f32[4,5,32,128]{3,2,1,0:T(8,128)S(1)}, u32[]{:S(2)}, u32[]{:S(2)}) collective-permute-start(f32[4,5,32,128]{3,2,1,0:T(8,128)S(1)} %get-tuple-element.10), channel_id=1, source_target_pairs={{0,4},{1,5},{2,6},{3,7},{4,0},{5,1},{6,2},{7,3},{8,12},{9,13},{10,... | collective-permute-start | bytes 983048 | tf_op jit(solution)/shard_map/ppermute | solution.py:176
  5.6 6.8 %collective-permute-start.3 = (f32[3,5,32,128]{3,2,1,0:T(8,128)S(1)}, f32[3,5,32,128]{3,2,1,0:T(8,128)S(1)}, u32[]{:S(2)}, u32[]{:S(2)}) collective-permute-start(f32[3,5,32,128]{3,2,1,0:T(8,128)S(1)} %slice_add_fusion), channel_id=1, source_target_pairs={{0,8},{1,9},{2,10},{3,11},{4,20},{5,21},{6,22},{7,23},{8,0},{9,1},... | collective-permute-start | bytes 737288 | tf_op jit(solution)/shard_map/ppermute | solution.py:176
  8.2 18.6 %copy-start = (f32[3,8,32,128]{3,2,1,0:T(8,128)S(1)}, f32[3,8,32,128]{3,2,1,0:T(8,128)}, u32[]{:S(2)}) copy-start(f32[3,8,32,128]{3,2,1,0:T(8,128)} %metric.1) | copy-start | bytes 1179652
  8.2 18.6 %copy-start.2 = (f32[2,8,32,128]{3,2,1,0:T(8,128)S(1)}, f32[2,8,32,128]{3,2,1,0:T(8,128)}, u32[]{:S(2)}) copy-start(f32[2,8,32,128]{3,2,1,0:T(8,128)} %pool.3) | copy-start | bytes 786436
  8.2 18.6 %copy-start.3 = (f32[8,32,128]{2,1,0:T(8,128)S(1)}, f32[8,32,128]{2,1,0:T(8,128)}, u32[]{:S(2)}) copy-start(f32[8,32,128]{2,1,0:T(8,128)} %screening.1) | copy-start | bytes 393220
  8.2 11.2 %collective-permute-start.1 = (f32[31,32,128]{2,1,0:T(8,128)S(1)}, f32[31,32,128]{2,1,0:T(8,128)S(1)}, u32[]{:S(2)}, u32[]{:S(2)}) collective-permute-start(f32[31,32,128]{2,1,0:T(8,128)S(1)} %fusion), channel_id=1, source_target_pairs={{1,4},{2,5},{3,6},{4,1},{5,2},{6,3},{9,12},{10,13},{11,14},{12,9},... | collective-permute-start | bytes 1523720 | tf_op jit(solution)/shard_map/ppermute | solution.py:176
  12.4 6.3 %collective-permute-start.4 = (f32[3,5,32,128]{3,2,1,0:T(8,128)S(1)}, f32[3,5,32,128]{3,2,1,0:T(8,128)S(1)}, u32[]{:S(2)}, u32[]{:S(2)}) collective-permute-start(f32[3,5,32,128]{3,2,1,0:T(8,128)S(1)} %add.25), channel_id=1, source_target_pairs={{0,16},{1,17},{2,18},{3,19},{4,12},{5,13},{6,14},{7,15},{8,24},{9,... | collective-permute-start | bytes 737288 | tf_op jit(solution)/shard_map/ppermute | solution.py:176
  18.7 4.3 %collective-permute-start.5 = (f32[3,5,32,128]{3,2,1,0:T(8,128)S(1)}, f32[3,5,32,128]{3,2,1,0:T(8,128)S(1)}, u32[]{:S(2)}, u32[]{:S(2)}) collective-permute-start(f32[3,5,32,128]{3,2,1,0:T(8,128)S(1)} %add.26.middle), channel_id=1, source_target_pairs={{1,4},{2,5},{3,6},{4,1},{5,2},{6,3},{9,12},{10,13},{11,14},{12,9},... | collective-permute-start | bytes 737288 | tf_op jit(solution)/shard_map/ppermute | solution.py:176
  19.5 7.3 %collective-permute-start.2 = (f32[26,32,128]{2,1,0:T(8,128)S(1)}, f32[26,32,128]{2,1,0:T(8,128)S(1)}, u32[]{:S(2)}, u32[]{:S(2)}) collective-permute-start(f32[26,32,128]{2,1,0:T(8,128)S(1)} %slice.41), channel_id=1, source_target_pairs={{0,4},{1,5},{2,6},{3,7},{4,0},{5,1},{6,2},{7,3},{8,12},{9,13},{10,... | collective-permute-start | bytes 1277960 | tf_op jit(solution)/shard_map/ppermute | solution.py:176
  23.0 6.0 %collective-permute-start.6 = (f32[3,8,32,128]{3,2,1,0:T(8,128)S(1)}, f32[3,8,32,128]{3,2,1,0:T(8,128)S(1)}, u32[]{:S(2)}, u32[]{:S(2)}) collective-permute-start(f32[3,8,32,128]{3,2,1,0:T(8,128)S(1)} %maximum_select_fusion), channel_id=1, source_target_pairs={{0,4},{1,5},{2,6},{3,7},{4,0},{5,1},{6,2},{7,3},{8,12},{9,13},{10,... | collective-permute-start | bytes 1179656 | tf_op jit(solution)/shard_map/ppermute | solution.py:176

commit v2 on v1

--- a/solution.py
+++ b/solution.py
@@ -14,6 +14,7 @@
 AXES = ("orb", "slab")
 VMEM = pl.BlockSpec(memory_space=pltpu.VMEM)
 SMEM = pl.BlockSpec(memory_space=pltpu.SMEM)
+HBM = pl.BlockSpec(memory_space=pltpu.HBM)
 
 
 def step_sizes(count):
@@ -34,23 +35,50 @@
     )
 
 
-def pick_kernel(where, index, row, pool, send, own):
-    orb, core = where[0], where[1]
+def pick_kernel(
+    row, index_hbm, pool_hbm, metric_hbm, screening_hbm,
+    send, own, edge, target, index, pool, sems,
+):
+    h = HALO
     held, planes = pool.shape[0], pool.shape[1]
-    mine = core * (planes - HALO)
-    other = (1 - core) * (planes - HALO)
+    orb = lax.axis_index("orb")
+    core = lax.rem(orb, 2)
+    mine = core * (planes - h)
+    other = (1 - core) * (planes - h)
+    parts = [
+        (index_hbm, index),
+        (pool_hbm, pool),
+        (screening_hbm.at[pl.ds(mine, h)], edge.at[pl.ds(0, h)]),
+        (metric_hbm.at[0, pl.ds(mine, h)], edge.at[pl.ds(h, h)]),
+        (metric_hbm.at[1, pl.ds(mine, h)], edge.at[pl.ds(2 * h, h)]),
+        (
+            metric_hbm.at[2, pl.ds(core * (planes - h - 1), h + 1)],
+            edge.at[pl.ds(3 * h, h + 1)],
+        ),
+    ]
+    copies = [pltpu.make_async_copy(a, b, sems.at[i]) for i, (a, b) in enumerate(parts)]
+    for copy in copies:
+        copy.start()
+    for copy in copies[:2]:
+        copy.wait()
     for out, start in ((send, other), (own, mine)):
         for s in range(NSRC):
             held_here = index[s] // held == orb
-            cells = pool[index[s] % held, pl.ds(start, HALO)]
+            cells = pool[lax.rem(index[s], held), pl.ds(start, h)]
             out[s] = jnp.where(held_here, cells, 0.0)
-        out[NSRC] = pool[row[0], pl.ds(start, HALO)]
+        out[NSRC] = pool[row[0], pl.ds(start, h)]
+    target[...] = pool[row[0]]
+    edge[pl.ds(4 * h + 1, h)] = pool[row[0], pl.ds(mine, h)]
+    edge[pl.ds(5 * h + 1, h)] = jnp.zeros((h,) + edge.shape[1:], jnp.float32)
+    for copy in copies[2:]:
+        copy.wait()
 
 
 def coefficient_kernel(
-    where, row, pool, metric, screening, near, far, coef, scaled, fx, fy, fz, scr, tgt
+    target, metric, screening, near, far, coef, scaled, fx, fy, fz, scr, tgt
 ):
-    core, slab, slabs = where[1], where[2], where[3]
+    core = lax.rem(lax.axis_index("orb"), 2)
+    slab, slabs = lax.axis_index("slab"), lax.axis_size("slab")
     planes, gx, gy = screening.shape
     total = planes + 2 * HALO
     lower = core * (HALO + planes)
@@ -69,7 +97,7 @@
     scr[h : h + planes] = screening[...]
     fx[h : h + planes] = metric[0]
     fy[h : h + planes] = metric[1]
-    tgt[h : h + planes] = pool[row[0]]
+    tgt[h : h + planes] = target[...]
     first = jnp.where(slab == 0, h, 0)
     last = jnp.where(slab == slabs - 1, h + planes, total)
     x_id = lax.broadcasted_iota(jnp.int32, (gx, gy), 0)
@@ -95,14 +123,13 @@
         scaled[rows] = tgt[e] * inverse
 
 
-def sweep_kernel(weights, where, coef, scaled, middle, halo, sibling, out, src, base, ping, pong):
-    core = where[1]
+def sweep_kernel(weights, coef, scaled, middle, halo, sibling, out, src, base, ping, pong):
+    core = lax.rem(lax.axis_index("orb"), 2)
     h = HALO
     gx, gy = out.shape[-2:]
     planes = out.shape[1]
     total = planes + 2 * h
     extra = middle.shape[1]
-    kept = planes
     halo_at = core * (h + planes)
     middle_at = h + core * (planes - extra)
     sibling_at = (1 - core) * (h + extra)
@@ -125,7 +152,7 @@
         w = weights[k]
         lastly = k == SWEEPS - 1
 
-        @pl.loop(k, total - k)
+        @pl.loop(k, total - k, unroll=4)
         def _(e):
             start = pl.multiple_of(e * gx, gx)
             for j in range(0, gx, 8):
@@ -159,9 +186,7 @@
     n_orb, n_slab = lax.axis_size("orb"), lax.axis_size("slab")
     h = HALO
     weights = step_sizes(SWEEPS)
-    orb, slab = lax.axis_index("orb"), lax.axis_index("slab")
-    core = orb % 2
-    where = jnp.stack([orb, core, slab, jnp.int32(n_slab)])
+    core = lax.axis_index("orb") % 2
 
     def place(o, z):
         return o * n_slab + z
@@ -179,32 +204,36 @@
     to_slab = among(lambda o, z: (o ^ 1, z + 1 if o % 2 else z - 1))
     bits = [1 << b for b in range(1, n_orb.bit_length() - 1)]
 
-    send, own = call(
+    send, own, edge, target = call(
         pick_kernel,
-        [(NSRC + 1, h, gx, gy)] * 2,
-        [SMEM, SMEM, SMEM, VMEM],
-    )(where, source_index, target_row, pool)
+        [(NSRC + 1, h, gx, gy)] * 2 + [(6 * h + 1, gx, gy), (planes, gx, gy)],
+        [SMEM] + [HBM] * 4,
+        [
+            pltpu.SMEM(source_index.shape, jnp.int32),
+            pltpu.VMEM(pool.shape, jnp.float32),
+            pltpu.SemaphoreType.DMA((6,)),
+        ],
+        moved=4 << 20,
+    )(target_row, *[pltpu.with_memory_space_constraint(x, pltpu.HBM) for x in (source_index, pool, metric, screening)])
     got = to_sibling(send)
     part = own[:NSRC] + got[:NSRC]
-    start = core * (planes - h)
-    near_z = core * (planes - h - 1)
-    half = functools.partial(lax.dynamic_slice_in_dim, start_index=start, slice_size=h, axis=0)
-    edge = jnp.concatenate(
-        [
-            half(screening),
-            half(metric[0]),
-            half(metric[1]),
-            lax.dynamic_slice_in_dim(metric[2], near_z, h + 1, axis=0),
-            own[NSRC],
-            got[NSRC],
-        ],
-        axis=0,
-    )
+    edge = edge.at[5 * h + 1 :].set(got[NSRC])
     near = to_slab(edge)
     for low, high in zip(bits, reversed(bits)):
         part = part + among(lambda o, z: (o ^ (high if o % 2 else low), z))(part)
     halo = to_slab(part)
     far = to_sibling(near[: 5 * h + 1])
+    total = planes + 2 * h
+    coef, scaled = call(
+        coefficient_kernel,
+        [(6, total * gx, gy), (total * gx, gy)],
+        [VMEM] * 5,
+        [pltpu.VMEM((total, gx, gy), jnp.float32)] * 2
+        + [pltpu.VMEM((total + 1, gx, gy), jnp.float32)]
+        + [pltpu.VMEM((total, gx, gy), jnp.float32)] * 2,
+        moved=8 << 20,
+    )(target, metric, screening, near, far)
+    halo, coef, scaled = lax.optimization_barrier((halo, coef, scaled))
     kept = planes - h
     lacks = jnp.where(
         core == 0,
@@ -212,22 +241,14 @@
         jnp.concatenate([part[:, h - kept :], halo], axis=1),
     )
     sibling = to_sibling(lacks)
-    total = planes + 2 * h
-    coef, scaled = call(
-        coefficient_kernel,
-        [(6, total * gx, gy), (total * gx, gy)],
-        [SMEM, SMEM] + [VMEM] * 5,
-        [pltpu.VMEM((total, gx, gy), jnp.float32)] * 2
-        + [pltpu.VMEM((total + 1, gx, gy), jnp.float32)]
-        + [pltpu.VMEM((total, gx, gy), jnp.float32)] * 2,
-    )(where, target_row, pool, metric, screening, near, far)
     field = pltpu.VMEM((NSRC, total * gx, gy), jnp.float32)
     (out,) = call(
         functools.partial(sweep_kernel, weights),
         [(1, planes, gx, gy)],
-        [SMEM] + [VMEM] * 5,
+        [VMEM] * 5,
         [field] * 4,
-    )(where, coef, scaled, part, halo, sibling)
+        moved=12 << 20,
+    )(coef, scaled, part, halo, sibling)
     return out
 
 

time: 36.8 us -> 32.4 us (0.88)
  Pallas kernels: 10.3 us -> 6.56 us
  local copies, waits for them, and re-layouts: 3.68 us -> 0.07 us
  starting transfers between devices: 14 us -> 15.7 us
  waiting for transfers between devices: 7.48 us -> 8.95 us
    pallas_call x3, Pallas kernels: 10.3 us -> 6.56 us  [the longest x1 3.76 us: shards(): call(functools.partial(sweep_kernel, weights), [(1, planes, gx, gy)], [VM...]
    unnamed x15 -> x4, local copies, waits for them, and re-layouts: 2.57 us -> 0.01 us
    ppermute x7, starting transfers between devices: 14 us -> 15.7 us  [among(): return lambda x: lax.ppermute(x, AXES, pairs)]
    ppermute x7, waiting for transfers between devices: 7.48 us -> 8.95 us  [among(): return lambda x: lax.ppermute(x, AXES, pairs)]
    slice x1 -> x0, local copies, waits for them, and re-layouts: 1.06 us -> none  [shards(): metric[2]]
  transfers between devices with their start and end apart: 7 -> 7, of which waited for: 2 -> 4; matrix products, arithmetic and copies ran while one was open for 6% -> 1% of each run, Pallas kernels for 6% -> 5%
where the time goes in v2:
time: 32.4 us; the launch traced here: 32.3 us
  starting transfers between devices  15.7 us (48%)
  waiting for transfers between devices  8.95 us (28%)
  Pallas kernels  6.56 us (20%)
  between operations  0.78 us (2%)
    ppermute x7, starting transfers between devices, among(): return lambda x: lax.ppermute(x, AXES, pairs)  15.7 us
    ppermute x7, waiting for transfers between devices, among(): return lambda x: lax.ppermute(x, AXES, pairs)  8.95 us
    pallas_call x1, Pallas kernels, shards(): call(functools.partial(sweep_kernel, weights), [(1, planes, gx, gy)], [VM...  3.76 us
    pallas_call x1, Pallas kernels, shards(): call(coefficient_kernel, [(6, total * gx, gy), (total * gx, gy)], [VMEM]...  1.65 us
    pallas_call x1, Pallas kernels, shards(): call(pick_kernel, [(NSRC + 1, h, gx, gy)] * 2 + [(6 * h + 1, gx, gy), (pl...  1.14 us
  transfers between devices with their start and end apart: 7, of which 4 were waited for; matrix products, arithmetic and copies ran while one was open for 1% of the time, Pallas kernels for 5%

profile of v2, /device:TPU:0, one launch (start us, length us, event | category | flops | bytes accessed | tf_op | source)
XLA Modules:
  0.0 32.3 jit_solution(775309610928272595)
XLA Ops:
  0.7 1.1 %shard_map.55 = (f32[4,5,32,128]{3,2,1,0:T(8,128)S(1)}, f32[4,5,32,128]{3,2,1,0:T(8,128)S(1)}, f32[31,32,128]{2,1,0:T(8,128)S(1)}, f32[8,32,128]{2,1,0:T(8,128)S(1)}) custom-call(s32[1]{0:T(128)S(6)} %copy.7.row, s32[3]{0:T(128)} %index_hbm.1, f32[2,8,32,128]{3,2,1,0:T(8,128)} %pool_hbm.1, f32[3,8,32,128]{3,2,1,0:T(8,128)} %metric.1, f32[8,32,128]{2,1,0:T(8,128)} %screening.1), custom_call_target="tpu_custom_call" | custom-call | bytes 4194304 | tf_op jit(solution)/shard_map/pallas_call | solution.py:207
  1.8 0.5 %collective-permute-start = (f32[4,5,32,128]{3,2,1,0:T(8,128)S(1)}, f32[4,5,32,128]{3,2,1,0:T(8,128)S(1)}, u32[]{:S(2)}, u32[]{:S(2)}) collective-permute-start(f32[4,5,32,128]{3,2,1,0:T(8,128)S(1)} %get-tuple-element.27), channel_id=1, source_target_pairs={{0,4},{1,5},{2,6},{3,7},{4,0},{5,1},{6,2},{7,3},{8,12},{9,13},{10,... | collective-permute-start | bytes 983048 | tf_op jit(solution)/shard_map/ppermute | solution.py:201
  2.3 1.3 %collective-permute-done = f32[4,5,32,128]{3,2,1,0:T(8,128)S(1)} collective-permute-done((f32[4,5,32,128]{3,2,1,0:T(8,128)S(1)}, f32[4,5,32,128]{3,2,1,0:T(8,128)S(1)}, u32[]{:S(2)}, u32[]{:S(2)}) %collective-permute-start) | collective-permute-done | bytes 327712 | tf_op jit(solution)/shard_map/ppermute | solution.py:201
  3.6 0.7 %collective-permute-start.4 = (f32[31,32,128]{2,1,0:T(8,128)S(1)}, f32[31,32,128]{2,1,0:T(8,128)S(1)}, u32[]{:S(2)}, u32[]{:S(2)}) collective-permute-start(f32[31,32,128]{2,1,0:T(8,128)S(1)} %fusion), channel_id=1, source_target_pairs={{1,4},{2,5},{3,6},{4,1},{5,2},{6,3},{9,12},{10,13},{11,14},{12,9},... | collective-permute-start | bytes 1523720 | tf_op jit(solution)/shard_map/ppermute | solution.py:201
  4.3 0.0 copy-start
  4.3 0.0 copy-start.1
  4.3 2.9 %collective-permute-start.1 = (f32[3,5,32,128]{3,2,1,0:T(8,128)S(1)}, f32[3,5,32,128]{3,2,1,0:T(8,128)S(1)}, u32[]{:S(2)}, u32[]{:S(2)}) collective-permute-start(f32[3,5,32,128]{3,2,1,0:T(8,128)S(1)} %slice_add_fusion), channel_id=1, source_target_pairs={{0,8},{1,9},{2,10},{3,11},{4,20},{5,21},{6,22},{7,23},{8,0},{9,1},... | collective-permute-start | bytes 737288 | tf_op jit(solution)/shard_map/ppermute | solution.py:201
  7.3 4.2 %collective-permute-done.1 = f32[3,5,32,128]{3,2,1,0:T(8,128)S(1)} collective-permute-done((f32[3,5,32,128]{3,2,1,0:T(8,128)S(1)}, f32[3,5,32,128]{3,2,1,0:T(8,128)S(1)}, u32[]{:S(2)}, u32[]{:S(2)}) %collective-permute-start.1) | collective-permute-done | bytes 245792 | tf_op jit(solution)/shard_map/ppermute | solution.py:201
  11.5 2.1 %collective-permute-start.2 = (f32[3,5,32,128]{3,2,1,0:T(8,128)S(1)}, f32[3,5,32,128]{3,2,1,0:T(8,128)S(1)}, u32[]{:S(2)}, u32[]{:S(2)}) collective-permute-start(f32[3,5,32,128]{3,2,1,0:T(8,128)S(1)} %add.16), channel_id=1, source_target_pairs={{0,16},{1,17},{2,18},{3,19},{4,12},{5,13},{6,14},{7,15},{8,24},{9,... | collective-permute-start | bytes 737288 | tf_op jit(solution)/shard_map/ppermute | solution.py:201
  13.6 0.0 collective-permute-done.4.near
  13.6 2.0 %collective-permute-start.5 = (f32[26,32,128]{2,1,0:T(8,128)S(1)}, f32[26,32,128]{2,1,0:T(8,128)S(1)}, u32[]{:S(2)}, u32[]{:S(2)}) collective-permute-start(f32[26,32,128]{2,1,0:T(8,128)S(1)} %slice.48), channel_id=1, source_target_pairs={{0,4},{1,5},{2,6},{3,7},{4,0},{5,1},{6,2},{7,3},{8,12},{9,13},{10,... | collective-permute-start | bytes 1277960 | tf_op jit(solution)/shard_map/ppermute | solution.py:201
  15.6 2.2 %collective-permute-done.2 = f32[3,5,32,128]{3,2,1,0:T(8,128)S(1)} collective-permute-done((f32[3,5,32,128]{3,2,1,0:T(8,128)S(1)}, f32[3,5,32,128]{3,2,1,0:T(8,128)S(1)}, u32[]{:S(2)}, u32[]{:S(2)}) %collective-permute-start.2) | collective-permute-done | bytes 245792 | tf_op jit(solution)/shard_map/ppermute | solution.py:201
  17.8 0.7 %collective-permute-start.3 = (f32[3,5,32,128]{3,2,1,0:T(8,128)S(1)}, f32[3,5,32,128]{3,2,1,0:T(8,128)S(1)}, u32[]{:S(2)}, u32[]{:S(2)}) collective-permute-start(f32[3,5,32,128]{3,2,1,0:T(8,128)S(1)} %add.17.middle), channel_id=1, source_target_pairs={{1,4},{2,5},{3,6},{4,1},{5,2},{6,3},{9,12},{10,13},{11,14},{12,9},... | collective-permute-start | bytes 737288 | tf_op jit(solution)/shard_map/ppermute | solution.py:201
  18.6 0.0 collective-permute-done.5.far
  18.6 0.0 copy-done
  18.6 0.0 copy-done.1
  18.6 1.7 %shard_map.56 = (f32[6,576,128]{2,1,0:T(8,128)S(1)}, f32[576,128]{1,0:T(8,128)S(1)}) custom-call(f32[8,32,128]{2,1,0:T(8,128)S(1)} %get-tuple-element.28.target, f32[3,8,32,128]{3,2,1,0:T(8,128)S(1)} %copy-done, f32[8,32,128]{2,1,0:T(8,128)S(1)} %copy-done.1, f32[31,32,128]{2,1,0:T(8,128)S(1)} %collective-permute-done.4.near, ...), custom_call_target="tpu_custom_call" | custom-call | bytes 8388608 | tf_op jit(solution)/shard_map/pallas_call | solution.py:227
  20.3 0.0 collective-permute-done.3.halo
  20.3 6.8 %collective-permute-start.6 = (f32[3,8,32,128]{3,2,1,0:T(8,128)S(1)}, f32[3,8,32,128]{3,2,1,0:T(8,128)S(1)}, u32[]{:S(2)}, u32[]{:S(2)}) collective-permute-start(f32[3,8,32,128]{3,2,1,0:T(8,128)S(1)} %maximum_select_fusion), channel_id=1, source_target_pairs={{0,4},{1,5},{2,6},{3,7},{4,0},{5,1},{6,2},{7,3},{8,12},{9,13},{10,... | collective-permute-start | bytes 1179656 | tf_op jit(solution)/shard_map/ppermute | solution.py:201
  27.1 1.3 %collective-permute-done.6.sibling = f32[3,8,32,128]{3,2,1,0:T(8,128)S(1)} collective-permute-done((f32[3,8,32,128]{3,2,1,0:T(8,128)S(1)}, f32[3,8,32,128]{3,2,1,0:T(8,128)S(1)}, u32[]{:S(2)}, u32[]{:S(2)}) %collective-permute-start.6) | collective-permute-done | bytes 393248 | tf_op jit(solution)/shard_map/ppermute | solution.py:201
  28.5 3.8 %shard_map.57 = f32[1,8,32,128]{3,2,1,0:T(8,128)} custom-call(f32[6,576,128]{2,1,0:T(8,128)S(1)} %get-tuple-element.32.coef, f32[576,128]{1,0:T(8,128)S(1)} %get-tuple-element.33.scaled, f32[3,5,32,128]{3,2,1,0:T(8,128)S(1)} %add.17.middle, f32[3,5,32,128]{3,2,1,0:T(8,128)S(1)} %collective-permute-done.3.halo, ...), custom_call_target="tpu_custom_call" | custom-call | bytes 12582912 | tf_op jit(solution)/shard_map/pallas_call | solution.py:245
  (7 shorter events, 0.2 us)
Async XLA Ops:
  1.8 1.8 %collective-permute-start = (f32[4,5,32,128]{3,2,1,0:T(8,128)S(1)}, f32[4,5,32,128]{3,2,1,0:T(8,128)S(1)}, u32[]{:S(2)}, u32[]{:S(2)}) collective-permute-start(f32[4,5,32,128]{3,2,1,0:T(8,128)S(1)} %get-tuple-element.27), channel_id=1, source_target_pairs={{0,4},{1,5},{2,6},{3,7},{4,0},{5,1},{6,2},{7,3},{8,12},{9,13},{10,... | collective-permute-start | bytes 983048 | tf_op jit(solution)/shard_map/ppermute | solution.py:201
  3.6 10.0 %collective-permute-start.4 = (f32[31,32,128]{2,1,0:T(8,128)S(1)}, f32[31,32,128]{2,1,0:T(8,128)S(1)}, u32[]{:S(2)}, u32[]{:S(2)}) collective-permute-start(f32[31,32,128]{2,1,0:T(8,128)S(1)} %fusion), channel_id=1, source_target_pairs={{1,4},{2,5},{3,6},{4,1},{5,2},{6,3},{9,12},{10,13},{11,14},{12,9},... | collective-permute-start | bytes 1523720 | tf_op jit(solution)/shard_map/ppermute | solution.py:201
  4.3 14.3 %copy-start = (f32[3,8,32,128]{3,2,1,0:T(8,128)S(1)}, f32[3,8,32,128]{3,2,1,0:T(8,128)}, u32[]{:S(2)}) copy-start(f32[3,8,32,128]{3,2,1,0:T(8,128)} %metric.1) | copy-start | bytes 1179652
  4.3 14.3 %copy-start.1 = (f32[8,32,128]{2,1,0:T(8,128)S(1)}, f32[8,32,128]{2,1,0:T(8,128)}, u32[]{:S(2)}) copy-start(f32[8,32,128]{2,1,0:T(8,128)} %screening.1) | copy-start | bytes 393220
  4.3 7.1 %collective-permute-start.1 = (f32[3,5,32,128]{3,2,1,0:T(8,128)S(1)}, f32[3,5,32,128]{3,2,1,0:T(8,128)S(1)}, u32[]{:S(2)}, u32[]{:S(2)}) collective-permute-start(f32[3,5,32,128]{3,2,1,0:T(8,128)S(1)} %slice_add_fusion), channel_id=1, source_target_pairs={{0,8},{1,9},{2,10},{3,11},{4,20},{5,21},{6,22},{7,23},{8,0},{9,1},... | collective-permute-start | bytes 737288 | tf_op jit(solution)/shard_map/ppermute | solution.py:201
  11.5 6.3 %collective-permute-start.2 = (f32[3,5,32,128]{3,2,1,0:T(8,128)S(1)}, f32[3,5,32,128]{3,2,1,0:T(8,128)S(1)}, u32[]{:S(2)}, u32[]{:S(2)}) collective-permute-start(f32[3,5,32,128]{3,2,1,0:T(8,128)S(1)} %add.16), channel_id=1, source_target_pairs={{0,16},{1,17},{2,18},{3,19},{4,12},{5,13},{6,14},{7,15},{8,24},{9,... | collective-permute-start | bytes 737288 | tf_op jit(solution)/shard_map/ppermute | solution.py:201
  13.6 4.9 %collective-permute-start.5 = (f32[26,32,128]{2,1,0:T(8,128)S(1)}, f32[26,32,128]{2,1,0:T(8,128)S(1)}, u32[]{:S(2)}, u32[]{:S(2)}) collective-permute-start(f32[26,32,128]{2,1,0:T(8,128)S(1)} %slice.48), channel_id=1, source_target_pairs={{0,4},{1,5},{2,6},{3,7},{4,0},{5,1},{6,2},{7,3},{8,12},{9,13},{10,... | collective-permute-start | bytes 1277960 | tf_op jit(solution)/shard_map/ppermute | solution.py:201
  17.8 2.4 %collective-permute-start.3 = (f32[3,5,32,128]{3,2,1,0:T(8,128)S(1)}, f32[3,5,32,128]{3,2,1,0:T(8,128)S(1)}, u32[]{:S(2)}, u32[]{:S(2)}) collective-permute-start(f32[3,5,32,128]{3,2,1,0:T(8,128)S(1)} %add.17.middle), channel_id=1, source_target_pairs={{1,4},{2,5},{3,6},{4,1},{5,2},{6,3},{9,12},{10,13},{11,14},{12,9},... | collective-permute-start | bytes 737288 | tf_op jit(solution)/shard_map/ppermute | solution.py:201
  20.3 8.2 %collective-permute-start.6 = (f32[3,8,32,128]{3,2,1,0:T(8,128)S(1)}, f32[3,8,32,128]{3,2,1,0:T(8,128)S(1)}, u32[]{:S(2)}, u32[]{:S(2)}) collective-permute-start(f32[3,8,32,128]{3,2,1,0:T(8,128)S(1)} %maximum_select_fusion), channel_id=1, source_target_pairs={{0,4},{1,5},{2,6},{3,7},{4,0},{5,1},{6,2},{7,3},{8,12},{9,13},{10,... | collective-permute-start | bytes 1179656 | tf_op jit(solution)/shard_map/ppermute | solution.py:201

commit v3 on v2

--- a/solution.py
+++ b/solution.py
@@ -12,6 +12,7 @@
 SWEEPS = 6
 HALO = SWEEPS - 1
 AXES = ("orb", "slab")
+HINT = 10**9
 VMEM = pl.BlockSpec(memory_space=pltpu.VMEM)
 SMEM = pl.BlockSpec(memory_space=pltpu.SMEM)
 HBM = pl.BlockSpec(memory_space=pltpu.HBM)
@@ -74,6 +75,10 @@
         copy.wait()
 
 
+def merge_kernel(mine, theirs, both):
+    both[...] = mine[...] + theirs[...]
+
+
 def coefficient_kernel(
     target, metric, screening, near, far, coef, scaled, fx, fy, fz, scr, tgt
 ):
@@ -202,6 +207,12 @@
 
     to_sibling = among(lambda o, z: (o ^ 1, z))
     to_slab = among(lambda o, z: (o ^ 1, z + 1 if o % 2 else z - 1))
+
+    def next_slab(o, z):
+        there = z + 1 if o % 2 else z - 1
+        return (o ^ 1, there) if 0 <= there < n_slab else (o ^ 2, z)
+
+    to_slab_all = among(next_slab)
     bits = [1 << b for b in range(1, n_orb.bit_length() - 1)]
 
     send, own, edge, target = call(
@@ -219,10 +230,13 @@
     part = own[:NSRC] + got[:NSRC]
     edge = edge.at[5 * h + 1 :].set(got[NSRC])
     near = to_slab(edge)
-    for low, high in zip(bits, reversed(bits)):
-        part = part + among(lambda o, z: (o ^ (high if o % 2 else low), z))(part)
-    halo = to_slab(part)
-    far = to_sibling(near[: 5 * h + 1])
+    for step, (low, high) in enumerate(zip(bits, reversed(bits))):
+        across = among(lambda o, z: (o ^ (high if o % 2 else low), z))
+        merge = call(merge_kernel, [part.shape], [VMEM] * 2, flops=0 if step else HINT)
+        (part,) = merge(part, across(part))
+    halo = to_slab_all(part)
+    cut = (5 * h + 1) // 2
+    far = jnp.concatenate([to_sibling(near[:cut]), to_sibling(near[cut : 5 * h + 1])], axis=0)
     total = planes + 2 * h
     coef, scaled = call(
         coefficient_kernel,
@@ -231,7 +245,7 @@
         [pltpu.VMEM((total, gx, gy), jnp.float32)] * 2
         + [pltpu.VMEM((total + 1, gx, gy), jnp.float32)]
         + [pltpu.VMEM((total, gx, gy), jnp.float32)] * 2,
-        moved=8 << 20,
+        moved=0,
     )(target, metric, screening, near, far)
     halo, coef, scaled = lax.optimization_barrier((halo, coef, scaled))
     kept = planes - h

time: 32.4 us -> 29.1 us (0.90)
  starting transfers between devices: 15.7 us -> 9.05 us
  waiting for transfers between devices: 8.95 us -> 12.4 us
    ppermute x7 -> x8, starting transfers between devices: 15.7 us -> 9.05 us  [among(): return lambda x: lax.ppermute(x, AXES, pairs)]
    ppermute x7 -> x8, waiting for transfers between devices: 8.95 us -> 12.4 us  [among(): return lambda x: lax.ppermute(x, AXES, pairs)]
  transfers between devices with their start and end apart: 7 -> 8, of which waited for: 4 -> 7; matrix products, arithmetic and copies ran while one was open for 1% -> 0% of each run, Pallas kernels for 5% -> 6%
where the time goes in v3:
time: 29.1 us; the launch traced here: 29 us
  waiting for transfers between devices  12.4 us (43%)
  starting transfers between devices  9.05 us (31%)
  Pallas kernels  6.61 us (23%)
  between operations  0.74 us (3%)
    ppermute x8, waiting for transfers between devices, among(): return lambda x: lax.ppermute(x, AXES, pairs)  12.4 us
    ppermute x8, starting transfers between devices, among(): return lambda x: lax.ppermute(x, AXES, pairs)  9.05 us
    pallas_call x1, Pallas kernels, shards(): call(functools.partial(sweep_kernel, weights), [(1, planes, gx, gy)], [VM...  3.76 us
    pallas_call x1, Pallas kernels, shards(): call(coefficient_kernel, [(6, total * gx, gy), (total * gx, gy)], [VMEM]...  1.65 us
    pallas_call x1, Pallas kernels, shards(): call(pick_kernel, [(NSRC + 1, h, gx, gy)] * 2 + [(6 * h + 1, gx, gy), (pl...  1.14 us
  transfers between devices with their start and end apart: 8, of which 7 were waited for; matrix products, arithmetic and copies ran while one was open for 0% of the time, Pallas kernels for 6%

profile of v3, /device:TPU:0, one launch (start us, length us, event | category | flops | bytes accessed | tf_op | source)
XLA Modules:
  0.0 29.0 jit_solution(15206544682889168819)
XLA Ops:
  0.7 1.1 %shard_map.55 = (f32[4,5,32,128]{3,2,1,0:T(8,128)S(1)}, f32[4,5,32,128]{3,2,1,0:T(8,128)S(1)}, f32[31,32,128]{2,1,0:T(8,128)S(1)}, f32[8,32,128]{2,1,0:T(8,128)S(1)}) custom-call(s32[1]{0:T(128)S(6)} %copy.7.row, s32[3]{0:T(128)} %index_hbm.1, f32[2,8,32,128]{3,2,1,0:T(8,128)} %pool_hbm.1, f32[3,8,32,128]{3,2,1,0:T(8,128)} %metric.1, f32[8,32,128]{2,1,0:T(8,128)} %screening.1), custom_call_target="tpu_custom_call" | custom-call | bytes 4194304 | tf_op jit(solution)/shard_map/pallas_call | solution.py:218
  1.8 0.5 %collective-permute-start = (f32[4,5,32,128]{3,2,1,0:T(8,128)S(1)}, f32[4,5,32,128]{3,2,1,0:T(8,128)S(1)}, u32[]{:S(2)}, u32[]{:S(2)}) collective-permute-start(f32[4,5,32,128]{3,2,1,0:T(8,128)S(1)} %get-tuple-element.27), channel_id=1, source_target_pairs={{0,4},{1,5},{2,6},{3,7},{4,0},{5,1},{6,2},{7,3},{8,12},{9,13},{10,... | collective-permute-start | bytes 983048 | tf_op jit(solution)/shard_map/ppermute | solution.py:206
  2.3 1.3 %collective-permute-done = f32[4,5,32,128]{3,2,1,0:T(8,128)S(1)} collective-permute-done((f32[4,5,32,128]{3,2,1,0:T(8,128)S(1)}, f32[4,5,32,128]{3,2,1,0:T(8,128)S(1)}, u32[]{:S(2)}, u32[]{:S(2)}) %collective-permute-start) | collective-permute-done | bytes 327712 | tf_op jit(solution)/shard_map/ppermute | solution.py:206
  3.6 2.9 %collective-permute-start.1 = (f32[3,5,32,128]{3,2,1,0:T(8,128)S(1)}, f32[3,5,32,128]{3,2,1,0:T(8,128)S(1)}, u32[]{:S(2)}, u32[]{:S(2)}) collective-permute-start(f32[3,5,32,128]{3,2,1,0:T(8,128)S(1)} %slice_add_fusion.mine), channel_id=1, source_target_pairs={{0,8},{1,9},{2,10},{3,11},{4,20},{5,21},{6,22},{7,23},{8,0},{9,1},... | collective-permute-start | bytes 737288 | tf_op jit(solution)/shard_map/ppermute | solution.py:206
  6.5 0.7 %collective-permute-start.4 = (f32[31,32,128]{2,1,0:T(8,128)S(1)}, f32[31,32,128]{2,1,0:T(8,128)S(1)}, u32[]{:S(2)}, u32[]{:S(2)}) collective-permute-start(f32[31,32,128]{2,1,0:T(8,128)S(1)} %fusion), channel_id=1, source_target_pairs={{1,4},{2,5},{3,6},{4,1},{5,2},{6,3},{9,12},{10,13},{11,14},{12,9},... | collective-permute-start | bytes 1523720 | tf_op jit(solution)/shard_map/ppermute | solution.py:206
  7.2 3.5 %collective-permute-done.1.theirs = f32[3,5,32,128]{3,2,1,0:T(8,128)S(1)} collective-permute-done((f32[3,5,32,128]{3,2,1,0:T(8,128)S(1)}, f32[3,5,32,128]{3,2,1,0:T(8,128)S(1)}, u32[]{:S(2)}, u32[]{:S(2)}) %collective-permute-start.1) | collective-permute-done | bytes 245792 | tf_op jit(solution)/shard_map/ppermute | solution.py:206
  10.7 0.0 copy-start
  10.8 0.0 copy-start.1
  10.8 2.1 %collective-permute-start.2 = (f32[3,5,32,128]{3,2,1,0:T(8,128)S(1)}, f32[3,5,32,128]{3,2,1,0:T(8,128)S(1)}, u32[]{:S(2)}, u32[]{:S(2)}) collective-permute-start(f32[3,5,32,128]{3,2,1,0:T(8,128)S(1)} %shard_map.56.mine), channel_id=1, source_target_pairs={{0,16},{1,17},{2,18},{3,19},{4,12},{5,13},{6,14},{7,15},{8,24},{9,... | collective-permute-start | bytes 737288 | tf_op jit(solution)/shard_map/ppermute | solution.py:206
  12.9 4.2 %collective-permute-done.2.theirs = f32[3,5,32,128]{3,2,1,0:T(8,128)S(1)} collective-permute-done((f32[3,5,32,128]{3,2,1,0:T(8,128)S(1)}, f32[3,5,32,128]{3,2,1,0:T(8,128)S(1)}, u32[]{:S(2)}, u32[]{:S(2)}) %collective-permute-start.2) | collective-permute-done | bytes 245792 | tf_op jit(solution)/shard_map/ppermute | solution.py:206
  17.1 2.1 %collective-permute-start.3 = (f32[3,5,32,128]{3,2,1,0:T(8,128)S(1)}, f32[3,5,32,128]{3,2,1,0:T(8,128)S(1)}, u32[]{:S(2)}, u32[]{:S(2)}) collective-permute-start(f32[3,5,32,128]{3,2,1,0:T(8,128)S(1)} %shard_map.57.middle), channel_id=1, source_target_pairs={{0,8},{1,4},{2,5},{3,6},{4,1},{5,2},{6,3},{7,15},{8,0},{9,12},{10,... | collective-permute-start | bytes 737288 | tf_op jit(solution)/shard_map/ppermute | solution.py:206
  19.1 0.0 collective-permute-done.4.near
  19.2 0.3 collective-permute-start.5
  19.5 0.3 %collective-permute-start.6 = (f32[13,32,128]{2,1,0:T(8,128)S(1)}, f32[13,32,128]{2,1,0:T(8,128)S(1)}, u32[]{:S(2)}, u32[]{:S(2)}) collective-permute-start(f32[13,32,128]{2,1,0:T(8,128)S(1)} %get-tuple-element.36), channel_id=1, source_target_pairs={{0,4},{1,5},{2,6},{3,7},{4,0},{5,1},{6,2},{7,3},{8,12},{9,13},{10,... | collective-permute-start | bytes 638984 | tf_op jit(solution)/shard_map/ppermute | solution.py:206
  19.8 0.9 %collective-permute-done.5 = f32[13,32,128]{2,1,0:T(8,128)S(1)} collective-permute-done((f32[13,32,128]{2,1,0:T(8,128)S(1)}, f32[13,32,128]{2,1,0:T(8,128)S(1)}, u32[]{:S(2)}, u32[]{:S(2)}) %collective-permute-start.5) | collective-permute-done | bytes 213024 | tf_op jit(solution)/shard_map/ppermute | solution.py:206
  20.7 0.3 %collective-permute-done.6 = f32[13,32,128]{2,1,0:T(8,128)S(1)} collective-permute-done((f32[13,32,128]{2,1,0:T(8,128)S(1)}, f32[13,32,128]{2,1,0:T(8,128)S(1)}, u32[]{:S(2)}, u32[]{:S(2)}) %collective-permute-start.6) | collective-permute-done | bytes 213024 | tf_op jit(solution)/shard_map/ppermute | solution.py:206
  21.1 0.0 copy-done
  21.1 0.0 copy-done.1
  21.1 1.7 %shard_map.58 = (f32[6,576,128]{2,1,0:T(8,128)S(1)}, f32[576,128]{1,0:T(8,128)S(1)}) custom-call(f32[8,32,128]{2,1,0:T(8,128)S(1)} %get-tuple-element.28.target, f32[3,8,32,128]{3,2,1,0:T(8,128)S(1)} %copy-done, f32[8,32,128]{2,1,0:T(8,128)S(1)} %copy-done.1, f32[31,32,128]{2,1,0:T(8,128)S(1)} %collective-permute-done.4.near, ...), custom_call_target="tpu_custom_call" | custom-call | tf_op jit(solution)/shard_map/pallas_call | solution.py:241
  22.7 0.6 %collective-permute-done.3.halo = f32[3,5,32,128]{3,2,1,0:T(8,128)S(1)} collective-permute-done((f32[3,5,32,128]{3,2,1,0:T(8,128)S(1)}, f32[3,5,32,128]{3,2,1,0:T(8,128)S(1)}, u32[]{:S(2)}, u32[]{:S(2)}) %collective-permute-start.3) | collective-permute-done | bytes 245792 | tf_op jit(solution)/shard_map/ppermute | solution.py:206
  23.4 0.2 collective-permute-start.7
  23.6 1.6 %collective-permute-done.7.sibling = f32[3,8,32,128]{3,2,1,0:T(8,128)S(1)} collective-permute-done((f32[3,8,32,128]{3,2,1,0:T(8,128)S(1)}, f32[3,8,32,128]{3,2,1,0:T(8,128)S(1)}, u32[]{:S(2)}, u32[]{:S(2)}) %collective-permute-start.7) | collective-permute-done | bytes 393248 | tf_op jit(solution)/shard_map/ppermute | solution.py:206
  25.2 3.8 %shard_map.59 = f32[1,8,32,128]{3,2,1,0:T(8,128)} custom-call(f32[6,576,128]{2,1,0:T(8,128)S(1)} %get-tuple-element.32.coef, f32[576,128]{1,0:T(8,128)S(1)} %get-tuple-element.33.scaled, f32[3,5,32,128]{3,2,1,0:T(8,128)S(1)} %shard_map.57.middle, f32[3,5,32,128]{3,2,1,0:T(8,128)S(1)} %collective-permute-done.3.halo, ...), custom_call_target="tpu_custom_call" | custom-call | bytes 12582912 | tf_op jit(solution)/shard_map/pallas_call | solution.py:259
  (8 shorter events, 0.2 us)
Async XLA Ops:
  1.8 1.8 %collective-permute-start = (f32[4,5,32,128]{3,2,1,0:T(8,128)S(1)}, f32[4,5,32,128]{3,2,1,0:T(8,128)S(1)}, u32[]{:S(2)}, u32[]{:S(2)}) collective-permute-start(f32[4,5,32,128]{3,2,1,0:T(8,128)S(1)} %get-tuple-element.27), channel_id=1, source_target_pairs={{0,4},{1,5},{2,6},{3,7},{4,0},{5,1},{6,2},{7,3},{8,12},{9,13},{10,... | collective-permute-start | bytes 983048 | tf_op jit(solution)/shard_map/ppermute | solution.py:206
  3.6 7.1 %collective-permute-start.1 = (f32[3,5,32,128]{3,2,1,0:T(8,128)S(1)}, f32[3,5,32,128]{3,2,1,0:T(8,128)S(1)}, u32[]{:S(2)}, u32[]{:S(2)}) collective-permute-start(f32[3,5,32,128]{3,2,1,0:T(8,128)S(1)} %slice_add_fusion.mine), channel_id=1, source_target_pairs={{0,8},{1,9},{2,10},{3,11},{4,20},{5,21},{6,22},{7,23},{8,0},{9,1},... | collective-permute-start | bytes 737288 | tf_op jit(solution)/shard_map/ppermute | solution.py:206
  6.5 12.6 %collective-permute-start.4 = (f32[31,32,128]{2,1,0:T(8,128)S(1)}, f32[31,32,128]{2,1,0:T(8,128)S(1)}, u32[]{:S(2)}, u32[]{:S(2)}) collective-permute-start(f32[31,32,128]{2,1,0:T(8,128)S(1)} %fusion), channel_id=1, source_target_pairs={{1,4},{2,5},{3,6},{4,1},{5,2},{6,3},{9,12},{10,13},{11,14},{12,9},... | collective-permute-start | bytes 1523720 | tf_op jit(solution)/shard_map/ppermute | solution.py:206
  10.7 10.3 %copy-start = (f32[3,8,32,128]{3,2,1,0:T(8,128)S(1)}, f32[3,8,32,128]{3,2,1,0:T(8,128)}, u32[]{:S(2)}) copy-start(f32[3,8,32,128]{3,2,1,0:T(8,128)} %metric.1) | copy-start | bytes 1179652
  10.8 10.3 %copy-start.1 = (f32[8,32,128]{2,1,0:T(8,128)S(1)}, f32[8,32,128]{2,1,0:T(8,128)}, u32[]{:S(2)}) copy-start(f32[8,32,128]{2,1,0:T(8,128)} %screening.1) | copy-start | bytes 393220
  10.8 6.3 %collective-permute-start.2 = (f32[3,5,32,128]{3,2,1,0:T(8,128)S(1)}, f32[3,5,32,128]{3,2,1,0:T(8,128)S(1)}, u32[]{:S(2)}, u32[]{:S(2)}) collective-permute-start(f32[3,5,32,128]{3,2,1,0:T(8,128)S(1)} %shard_map.56.mine), channel_id=1, source_target_pairs={{0,16},{1,17},{2,18},{3,19},{4,12},{5,13},{6,14},{7,15},{8,24},{9,... | collective-permute-start | bytes 737288 | tf_op jit(solution)/shard_map/ppermute | solution.py:206
  17.1 6.3 %collective-permute-start.3 = (f32[3,5,32,128]{3,2,1,0:T(8,128)S(1)}, f32[3,5,32,128]{3,2,1,0:T(8,128)S(1)}, u32[]{:S(2)}, u32[]{:S(2)}) collective-permute-start(f32[3,5,32,128]{3,2,1,0:T(8,128)S(1)} %shard_map.57.middle), channel_id=1, source_target_pairs={{0,8},{1,4},{2,5},{3,6},{4,1},{5,2},{6,3},{7,15},{8,0},{9,12},{10,... | collective-permute-start | bytes 737288 | tf_op jit(solution)/shard_map/ppermute | solution.py:206
  19.2 1.5 %collective-permute-start.5 = (f32[13,32,128]{2,1,0:T(8,128)S(1)}, f32[13,32,128]{2,1,0:T(8,128)S(1)}, u32[]{:S(2)}, u32[]{:S(2)}) collective-permute-start(f32[13,32,128]{2,1,0:T(8,128)S(1)} %get-tuple-element.35), channel_id=1, source_target_pairs={{0,4},{1,5},{2,6},{3,7},{4,0},{5,1},{6,2},{7,3},{8,12},{9,13},{10,... | collective-permute-start | bytes 638984 | tf_op jit(solution)/shard_map/ppermute | solution.py:206
  19.5 1.6 %collective-permute-start.6 = (f32[13,32,128]{2,1,0:T(8,128)S(1)}, f32[13,32,128]{2,1,0:T(8,128)S(1)}, u32[]{:S(2)}, u32[]{:S(2)}) collective-permute-start(f32[13,32,128]{2,1,0:T(8,128)S(1)} %get-tuple-element.36), channel_id=1, source_target_pairs={{0,4},{1,5},{2,6},{3,7},{4,0},{5,1},{6,2},{7,3},{8,12},{9,13},{10,... | collective-permute-start | bytes 638984 | tf_op jit(solution)/shard_map/ppermute | solution.py:206
  23.4 1.8 %collective-permute-start.7 = (f32[3,8,32,128]{3,2,1,0:T(8,128)S(1)}, f32[3,8,32,128]{3,2,1,0:T(8,128)S(1)}, u32[]{:S(2)}, u32[]{:S(2)}) collective-permute-start(f32[3,8,32,128]{3,2,1,0:T(8,128)S(1)} %maximum_select_fusion), channel_id=1, source_target_pairs={{0,4},{1,5},{2,6},{3,7},{4,0},{5,1},{6,2},{7,3},{8,12},{9,13},{10,... | collective-permute-start | bytes 1179656 | tf_op jit(solution)/shard_map/ppermute | solution.py:206

commit v4 on v3

--- a/solution.py
+++ b/solution.py
@@ -12,7 +12,7 @@
 SWEEPS = 6
 HALO = SWEEPS - 1
 AXES = ("orb", "slab")
-HINT = 10**9
+HINT = 10**10
 VMEM = pl.BlockSpec(memory_space=pltpu.VMEM)
 SMEM = pl.BlockSpec(memory_space=pltpu.SMEM)
 HBM = pl.BlockSpec(memory_space=pltpu.HBM)
@@ -38,12 +38,13 @@
 
 def pick_kernel(
     row, index_hbm, pool_hbm, metric_hbm, screening_hbm,
-    send, own, edge, target, index, pool, sems,
+    own, aim, edge, target, pick, index, pool, sems,
 ):
     h = HALO
     held, planes = pool.shape[0], pool.shape[1]
     orb = lax.axis_index("orb")
     core = lax.rem(orb, 2)
+    sibling = orb + 1 - 2 * core
     mine = core * (planes - h)
     other = (1 - core) * (planes - h)
     parts = [
@@ -62,17 +63,29 @@
         copy.start()
     for copy in copies[:2]:
         copy.wait()
-    for out, start in ((send, other), (own, mine)):
-        for s in range(NSRC):
-            held_here = index[s] // held == orb
-            cells = pool[lax.rem(index[s], held), pl.ds(start, h)]
-            out[s] = jnp.where(held_here, cells, 0.0)
-        out[NSRC] = pool[row[0], pl.ds(start, h)]
+    for s in range(NSRC):
+        group, place = index[s] // held, lax.rem(index[s], held)
+        own[s] = jnp.where(group == orb, pool[place, pl.ds(mine, h)], 0.0)
+        for r in range(held):
+            there = jnp.logical_and(group == sibling, place == r)
+            pick[s, r] = jnp.where(there, jnp.ones(pick.shape[2:], jnp.float32), 0.0)
+    aim[...] = pool[row[0], pl.ds(other, h)]
     target[...] = pool[row[0]]
     edge[pl.ds(4 * h + 1, h)] = pool[row[0], pl.ds(mine, h)]
     edge[pl.ds(5 * h + 1, h)] = jnp.zeros((h,) + edge.shape[1:], jnp.float32)
     for copy in copies[2:]:
         copy.wait()
+
+
+def gather_kernel(own, pick, pool, part):
+    h = HALO
+    held, planes, gx = pool.shape[:3]
+    mine = lax.rem(lax.axis_index("orb"), 2) * (planes - h)
+    for s in range(NSRC):
+        total = own[s]
+        for r in range(held):
+            total += jnp.tile(pick[s, r], (gx // pick.shape[2], 1)) * pool[r, pl.ds(mine, h)]
+        part[s] = total
 
 
 def merge_kernel(mine, theirs, both):
@@ -215,9 +228,16 @@
     to_slab_all = among(next_slab)
     bits = [1 << b for b in range(1, n_orb.bit_length() - 1)]
 
-    send, own, edge, target = call(
+    theirs = to_sibling(pool)
+    own, aim, edge, target, pick = call(
         pick_kernel,
-        [(NSRC + 1, h, gx, gy)] * 2 + [(6 * h + 1, gx, gy), (planes, gx, gy)],
+        [
+            (NSRC, h, gx, gy),
+            (h, gx, gy),
+            (6 * h + 1, gx, gy),
+            (planes, gx, gy),
+            (NSRC, held, 8, gy),
+        ],
         [SMEM] + [HBM] * 4,
         [
             pltpu.SMEM(source_index.shape, jnp.int32),
@@ -225,10 +245,13 @@
             pltpu.SemaphoreType.DMA((6,)),
         ],
         moved=4 << 20,
-    )(target_row, *[pltpu.with_memory_space_constraint(x, pltpu.HBM) for x in (source_index, pool, metric, screening)])
-    got = to_sibling(send)
-    part = own[:NSRC] + got[:NSRC]
-    edge = edge.at[5 * h + 1 :].set(got[NSRC])
+    )(target_row, *[
+        pltpu.with_memory_space_constraint(x, pltpu.HBM)
+        for x in (source_index, pool, metric, screening)
+    ])
+    (part,) = call(gather_kernel, [own.shape], [VMEM] * 3)(own, pick, theirs)
+    part, aim = lax.optimization_barrier((part, aim))
+    edge = edge.at[5 * h + 1 :].set(to_sibling(aim))
     near = to_slab(edge)
     for step, (low, high) in enumerate(zip(bits, reversed(bits))):
         across = among(lambda o, z: (o ^ (high if o % 2 else low), z))

time: 29.1 us -> 27.4 us (0.942)
  waiting for transfers between devices: 12.4 us -> 10.9 us
    ppermute x8 -> x9, waiting for transfers between devices: 12.4 us -> 10.9 us  [among(): return lambda x: lax.ppermute(x, AXES, pairs)]
    ppermute x8 -> x9, starting transfers between devices: 9.05 us -> 8.88 us  [among(): return lambda x: lax.ppermute(x, AXES, pairs)]
    pallas_call x1 -> x2, Pallas kernels: 1.14 us -> 1.2 us  [the longest x1 1.14 us: shards(): call(pick_kernel, [(NSRC, h, gx, gy), (h, gx, gy), (6 * h + 1, gx, gy), (...]
  transfers between devices with their start and end apart: 8 -> 9, of which waited for: 7 -> 7; matrix products, arithmetic and copies ran while one was open for 0% -> 0% of each run, Pallas kernels for 6% -> 10%
where the time goes in v4:
time: 27.4 us; the launch traced here: 27.3 us
  waiting for transfers between devices  10.9 us (40%)
  starting transfers between devices  8.88 us (32%)
  Pallas kernels  6.67 us (24%)
  between operations  0.75 us (3%)
    ppermute x9, waiting for transfers between devices, among(): return lambda x: lax.ppermute(x, AXES, pairs)  10.9 us
    ppermute x9, starting transfers between devices, among(): return lambda x: lax.ppermute(x, AXES, pairs)  8.88 us
    pallas_call x1, Pallas kernels, shards(): call(functools.partial(sweep_kernel, weights), [(1, planes, gx, gy)], [VM...  3.76 us
    pallas_call x1, Pallas kernels, shards(): call(coefficient_kernel, [(6, total * gx, gy), (total * gx, gy)], [VMEM]...  1.65 us
    pallas_call x1, Pallas kernels, shards(): call(pick_kernel, [(NSRC, h, gx, gy), (h, gx, gy), (6 * h + 1, gx, gy), (...  1.14 us
  transfers between devices with their start and end apart: 9, of which 7 were waited for; matrix products, arithmetic and copies ran while one was open for 0% of the time, Pallas kernels for 10%

profile of v4, /device:TPU:0, one launch (start us, length us, event | category | flops | bytes accessed | tf_op | source)
XLA Modules:
  0.0 27.3 jit_solution(1885385035537434889)
XLA Ops:
  0.0 0.5 %collective-permute-start = (f32[2,8,32,128]{3,2,1,0:T(8,128)}, f32[2,8,32,128]{3,2,1,0:T(8,128)S(1)}, u32[]{:S(2)}, u32[]{:S(2)}) collective-permute-start(f32[2,8,32,128]{3,2,1,0:T(8,128)} %pool_hbm.1), channel_id=1, source_target_pairs={{0,4},{1,5},{2,6},{3,7},{4,0},{5,1},{6,2},{7,3},{8,12},{9,13},{10,... | collective-permute-start | bytes 786440 | tf_op jit(solution)/shard_map/ppermute | solution.py:219
  1.1 1.1 %shard_map.55 = (f32[3,5,32,128]{3,2,1,0:T(8,128)S(1)}, f32[5,32,128]{2,1,0:T(8,128)S(1)}, f32[31,32,128]{2,1,0:T(8,128)S(1)}, f32[8,32,128]{2,1,0:T(8,128)S(1)}, f32[3,2,8,128]{3,2,1,0:T(8,128)S(1)}) custom-call(s32[1]{0:T(128)S(6)} %copy.7.row, s32[3]{0:T(128)} %index_hbm.1, f32[2,8,32,128]{3,2,1,0:T(8,128)} %pool_hbm.1, f32[3,8,32,128]{3,2,1,0:T(8,128)} %metric.1, ...), custom_call_target="tpu_custom_call" | custom-call | bytes 4194304 | tf_op jit(solution)/shard_map/pallas_call | solution.py:232
  2.3 0.0 collective-permute-done.pool
  2.3 0.1 shard_map.56.mine
  2.3 2.6 %collective-permute-start.1 = (f32[3,5,32,128]{3,2,1,0:T(8,128)S(1)}, f32[3,5,32,128]{3,2,1,0:T(8,128)S(1)}, u32[]{:S(2)}, u32[]{:S(2)}) collective-permute-start(f32[3,5,32,128]{3,2,1,0:T(8,128)S(1)} %shard_map.56.mine), channel_id=1, source_target_pairs={{0,8},{1,9},{2,10},{3,11},{4,20},{5,21},{6,22},{7,23},{8,0},{9,1},... | collective-permute-start | bytes 737288 | tf_op jit(solution)/shard_map/ppermute | solution.py:219
  4.9 0.3 collective-permute-start.4
  5.1 1.0 %collective-permute-done.4 = f32[5,32,128]{2,1,0:T(8,128)S(1)} collective-permute-done((f32[5,32,128]{2,1,0:T(8,128)S(1)}, f32[5,32,128]{2,1,0:T(8,128)S(1)}, u32[]{:S(2)}, u32[]{:S(2)}) %collective-permute-start.4) | collective-permute-done | bytes 81952 | tf_op jit(solution)/shard_map/ppermute | solution.py:219
  6.2 0.7 %collective-permute-start.5 = (f32[31,32,128]{2,1,0:T(8,128)S(1)}, f32[31,32,128]{2,1,0:T(8,128)S(1)}, u32[]{:S(2)}, u32[]{:S(2)}) collective-permute-start(f32[31,32,128]{2,1,0:T(8,128)S(1)} %constant_dynamic-update-slice_fusion), channel_id=1, source_target_pairs={{1,4},{2,5},{3,6},{4,1},{5,2},{6,3},{9,12},{10,13},{11,14},{12,9},... | collective-permute-start | bytes 1523720 | tf_op jit(solution)/shard_map/ppermute | solution.py:219
  6.9 2.2 %collective-permute-done.1.theirs = f32[3,5,32,128]{3,2,1,0:T(8,128)S(1)} collective-permute-done((f32[3,5,32,128]{3,2,1,0:T(8,128)S(1)}, f32[3,5,32,128]{3,2,1,0:T(8,128)S(1)}, u32[]{:S(2)}, u32[]{:S(2)}) %collective-permute-start.1) | collective-permute-done | bytes 245792 | tf_op jit(solution)/shard_map/ppermute | solution.py:219
  9.1 0.0 copy-start
  9.1 0.0 copy-start.1
  9.1 2.1 %collective-permute-start.2 = (f32[3,5,32,128]{3,2,1,0:T(8,128)S(1)}, f32[3,5,32,128]{3,2,1,0:T(8,128)S(1)}, u32[]{:S(2)}, u32[]{:S(2)}) collective-permute-start(f32[3,5,32,128]{3,2,1,0:T(8,128)S(1)} %shard_map.57.mine), channel_id=1, source_target_pairs={{0,16},{1,17},{2,18},{3,19},{4,12},{5,13},{6,14},{7,15},{8,24},{9,... | collective-permute-start | bytes 737288 | tf_op jit(solution)/shard_map/ppermute | solution.py:219
  11.2 4.2 %collective-permute-done.2.theirs = f32[3,5,32,128]{3,2,1,0:T(8,128)S(1)} collective-permute-done((f32[3,5,32,128]{3,2,1,0:T(8,128)S(1)}, f32[3,5,32,128]{3,2,1,0:T(8,128)S(1)}, u32[]{:S(2)}, u32[]{:S(2)}) %collective-permute-start.2) | collective-permute-done | bytes 245792 | tf_op jit(solution)/shard_map/ppermute | solution.py:219
  15.4 2.1 %collective-permute-start.3 = (f32[3,5,32,128]{3,2,1,0:T(8,128)S(1)}, f32[3,5,32,128]{3,2,1,0:T(8,128)S(1)}, u32[]{:S(2)}, u32[]{:S(2)}) collective-permute-start(f32[3,5,32,128]{3,2,1,0:T(8,128)S(1)} %shard_map.58.middle), channel_id=1, source_target_pairs={{0,8},{1,4},{2,5},{3,6},{4,1},{5,2},{6,3},{7,15},{8,0},{9,12},{10,... | collective-permute-start | bytes 737288 | tf_op jit(solution)/shard_map/ppermute | solution.py:219
  17.5 0.0 collective-permute-done.5.near
  17.5 0.3 collective-permute-start.6
  17.8 0.3 %collective-permute-start.7 = (f32[13,32,128]{2,1,0:T(8,128)S(1)}, f32[13,32,128]{2,1,0:T(8,128)S(1)}, u32[]{:S(2)}, u32[]{:S(2)}) collective-permute-start(f32[13,32,128]{2,1,0:T(8,128)S(1)} %get-tuple-element.42), channel_id=1, source_target_pairs={{0,4},{1,5},{2,6},{3,7},{4,0},{5,1},{6,2},{7,3},{8,12},{9,13},{10,... | collective-permute-start | bytes 638984 | tf_op jit(solution)/shard_map/ppermute | solution.py:219
  18.1 0.9 %collective-permute-done.6 = f32[13,32,128]{2,1,0:T(8,128)S(1)} collective-permute-done((f32[13,32,128]{2,1,0:T(8,128)S(1)}, f32[13,32,128]{2,1,0:T(8,128)S(1)}, u32[]{:S(2)}, u32[]{:S(2)}) %collective-permute-start.6) | collective-permute-done | bytes 213024 | tf_op jit(solution)/shard_map/ppermute | solution.py:219
  19.1 0.3 %collective-permute-done.7 = f32[13,32,128]{2,1,0:T(8,128)S(1)} collective-permute-done((f32[13,32,128]{2,1,0:T(8,128)S(1)}, f32[13,32,128]{2,1,0:T(8,128)S(1)}, u32[]{:S(2)}, u32[]{:S(2)}) %collective-permute-start.7) | collective-permute-done | bytes 213024 | tf_op jit(solution)/shard_map/ppermute | solution.py:219
  19.4 0.0 copy-done
  19.4 0.0 copy-done.1
  19.4 1.7 %shard_map.59 = (f32[6,576,128]{2,1,0:T(8,128)S(1)}, f32[576,128]{1,0:T(8,128)S(1)}) custom-call(f32[8,32,128]{2,1,0:T(8,128)S(1)} %get-tuple-element.33.target, f32[3,8,32,128]{3,2,1,0:T(8,128)S(1)} %copy-done, f32[8,32,128]{2,1,0:T(8,128)S(1)} %copy-done.1, f32[31,32,128]{2,1,0:T(8,128)S(1)} %collective-permute-done.5.near, ...), custom_call_target="tpu_custom_call" | custom-call | tf_op jit(solution)/shard_map/pallas_call | solution.py:264
  21.1 0.6 %collective-permute-done.3.halo = f32[3,5,32,128]{3,2,1,0:T(8,128)S(1)} collective-permute-done((f32[3,5,32,128]{3,2,1,0:T(8,128)S(1)}, f32[3,5,32,128]{3,2,1,0:T(8,128)S(1)}, u32[]{:S(2)}, u32[]{:S(2)}) %collective-permute-start.3) | collective-permute-done | bytes 245792 | tf_op jit(solution)/shard_map/ppermute | solution.py:219
  21.7 0.2 collective-permute-start.8
  21.9 1.6 %collective-permute-done.8.sibling = f32[3,8,32,128]{3,2,1,0:T(8,128)S(1)} collective-permute-done((f32[3,8,32,128]{3,2,1,0:T(8,128)S(1)}, f32[3,8,32,128]{3,2,1,0:T(8,128)S(1)}, u32[]{:S(2)}, u32[]{:S(2)}) %collective-permute-start.8) | collective-permute-done | bytes 393248 | tf_op jit(solution)/shard_map/ppermute | solution.py:219
  23.5 3.8 %shard_map.60 = f32[1,8,32,128]{3,2,1,0:T(8,128)} custom-call(f32[6,576,128]{2,1,0:T(8,128)S(1)} %get-tuple-element.38.coef, f32[576,128]{1,0:T(8,128)S(1)} %get-tuple-element.39.scaled, f32[3,5,32,128]{3,2,1,0:T(8,128)S(1)} %shard_map.58.middle, f32[3,5,32,128]{3,2,1,0:T(8,128)S(1)} %collective-permute-done.3.halo, ...), custom_call_target="tpu_custom_call" | custom-call | bytes 12582912 | tf_op jit(solution)/shard_map/pallas_call | solution.py:282
  (7 shorter events, 0.2 us)
Async XLA Ops:
  0.0 2.3 %collective-permute-start = (f32[2,8,32,128]{3,2,1,0:T(8,128)}, f32[2,8,32,128]{3,2,1,0:T(8,128)S(1)}, u32[]{:S(2)}, u32[]{:S(2)}) collective-permute-start(f32[2,8,32,128]{3,2,1,0:T(8,128)} %pool_hbm.1), channel_id=1, source_target_pairs={{0,4},{1,5},{2,6},{3,7},{4,0},{5,1},{6,2},{7,3},{8,12},{9,13},{10,... | collective-permute-start | bytes 786440 | tf_op jit(solution)/shard_map/ppermute | solution.py:219
  2.3 6.7 %collective-permute-start.1 = (f32[3,5,32,128]{3,2,1,0:T(8,128)S(1)}, f32[3,5,32,128]{3,2,1,0:T(8,128)S(1)}, u32[]{:S(2)}, u32[]{:S(2)}) collective-permute-start(f32[3,5,32,128]{3,2,1,0:T(8,128)S(1)} %shard_map.56.mine), channel_id=1, source_target_pairs={{0,8},{1,9},{2,10},{3,11},{4,20},{5,21},{6,22},{7,23},{8,0},{9,1},... | collective-permute-start | bytes 737288 | tf_op jit(solution)/shard_map/ppermute | solution.py:219
  4.9 1.3 %collective-permute-start.4 = (f32[5,32,128]{2,1,0:T(8,128)S(1)}, f32[5,32,128]{2,1,0:T(8,128)S(1)}, u32[]{:S(2)}, u32[]{:S(2)}) collective-permute-start(f32[5,32,128]{2,1,0:T(8,128)S(1)} %get-tuple-element.35), channel_id=1, source_target_pairs={{0,4},{1,5},{2,6},{3,7},{4,0},{5,1},{6,2},{7,3},{8,12},{9,13},{10,... | collective-permute-start | bytes 245768 | tf_op jit(solution)/shard_map/ppermute | solution.py:219
  6.2 11.3 %collective-permute-start.5 = (f32[31,32,128]{2,1,0:T(8,128)S(1)}, f32[31,32,128]{2,1,0:T(8,128)S(1)}, u32[]{:S(2)}, u32[]{:S(2)}) collective-permute-start(f32[31,32,128]{2,1,0:T(8,128)S(1)} %constant_dynamic-update-slice_fusion), channel_id=1, source_target_pairs={{1,4},{2,5},{3,6},{4,1},{5,2},{6,3},{9,12},{10,13},{11,14},{12,9},... | collective-permute-start | bytes 1523720 | tf_op jit(solution)/shard_map/ppermute | solution.py:219
  9.1 10.3 %copy-start = (f32[3,8,32,128]{3,2,1,0:T(8,128)S(1)}, f32[3,8,32,128]{3,2,1,0:T(8,128)}, u32[]{:S(2)}) copy-start(f32[3,8,32,128]{3,2,1,0:T(8,128)} %metric.1) | copy-start | bytes 1179652
  9.1 10.3 %copy-start.1 = (f32[8,32,128]{2,1,0:T(8,128)S(1)}, f32[8,32,128]{2,1,0:T(8,128)}, u32[]{:S(2)}) copy-start(f32[8,32,128]{2,1,0:T(8,128)} %screening.1) | copy-start | bytes 393220
  9.1 6.3 %collective-permute-start.2 = (f32[3,5,32,128]{3,2,1,0:T(8,128)S(1)}, f32[3,5,32,128]{3,2,1,0:T(8,128)S(1)}, u32[]{:S(2)}, u32[]{:S(2)}) collective-permute-start(f32[3,5,32,128]{3,2,1,0:T(8,128)S(1)} %shard_map.57.mine), channel_id=1, source_target_pairs={{0,16},{1,17},{2,18},{3,19},{4,12},{5,13},{6,14},{7,15},{8,24},{9,... | collective-permute-start | bytes 737288 | tf_op jit(solution)/shard_map/ppermute | solution.py:219
  15.4 6.3 %collective-permute-start.3 = (f32[3,5,32,128]{3,2,1,0:T(8,128)S(1)}, f32[3,5,32,128]{3,2,1,0:T(8,128)S(1)}, u32[]{:S(2)}, u32[]{:S(2)}) collective-permute-start(f32[3,5,32,128]{3,2,1,0:T(8,128)S(1)} %shard_map.58.middle), channel_id=1, source_target_pairs={{0,8},{1,4},{2,5},{3,6},{4,1},{5,2},{6,3},{7,15},{8,0},{9,12},{10,... | collective-permute-start | bytes 737288 | tf_op jit(solution)/shard_map/ppermute | solution.py:219
  17.5 1.5 %collective-permute-start.6 = (f32[13,32,128]{2,1,0:T(8,128)S(1)}, f32[13,32,128]{2,1,0:T(8,128)S(1)}, u32[]{:S(2)}, u32[]{:S(2)}) collective-permute-start(f32[13,32,128]{2,1,0:T(8,128)S(1)} %get-tuple-element.41), channel_id=1, source_target_pairs={{0,4},{1,5},{2,6},{3,7},{4,0},{5,1},{6,2},{7,3},{8,12},{9,13},{10,... | collective-permute-start | bytes 638984 | tf_op jit(solution)/shard_map/ppermute | solution.py:219
  17.8 1.6 %collective-permute-start.7 = (f32[13,32,128]{2,1,0:T(8,128)S(1)}, f32[13,32,128]{2,1,0:T(8,128)S(1)}, u32[]{:S(2)}, u32[]{:S(2)}) collective-permute-start(f32[13,32,128]{2,1,0:T(8,128)S(1)} %get-tuple-element.42), channel_id=1, source_target_pairs={{0,4},{1,5},{2,6},{3,7},{4,0},{5,1},{6,2},{7,3},{8,12},{9,13},{10,... | collective-permute-start | bytes 638984 | tf_op jit(solution)/shard_map/ppermute | solution.py:219
  21.7 1.8 %collective-permute-start.8 = (f32[3,8,32,128]{3,2,1,0:T(8,128)S(1)}, f32[3,8,32,128]{3,2,1,0:T(8,128)S(1)}, u32[]{:S(2)}, u32[]{:S(2)}) collective-permute-start(f32[3,8,32,128]{3,2,1,0:T(8,128)S(1)} %maximum_select_fusion), channel_id=1, source_target_pairs={{0,4},{1,5},{2,6},{3,7},{4,0},{5,1},{6,2},{7,3},{8,12},{9,13},{10,... | collective-permute-start | bytes 1179656 | tf_op jit(solution)/shard_map/ppermute | solution.py:219

commit v5 on v4

v5 whole, which is shorter than its diff:
```python
import functools
import math

import jax
import jax.numpy as jnp
from jax import lax
from jax.experimental import pallas as pl
from jax.experimental.pallas import tpu as pltpu
from jax.sharding import PartitionSpec as P

NSRC = 3
SWEEPS = 6
HALO = SWEEPS - 1
AXES = ("orb", "slab")
HINT = 10**10
VMEM = pl.BlockSpec(memory_space=pltpu.VMEM)
SMEM = pl.BlockSpec(memory_space=pltpu.SMEM)
HBM = pl.BlockSpec(memory_space=pltpu.HBM)


def step_sizes(count):
    return [
        1.0 / (1.025 + 0.975 * math.cos(math.pi * (2 * k + 1) / (2 * count))) for k in range(count)
    ]


def upper_side():
    return 1 - lax.rem(lax.axis_index("orb"), 2)


def call(kernel, out_shapes, in_specs, scratch=(), flops=0, moved=0, alias=None):
    return pl.pallas_call(
        kernel,
        out_shape=[jax.ShapeDtypeStruct(s, jnp.float32) for s in out_shapes],
        in_specs=in_specs,
        out_specs=[VMEM] * len(out_shapes),
        scratch_shapes=list(scratch),
        compiler_params=pltpu.CompilerParams(vmem_limit_bytes=16 << 20),
        input_output_aliases=alias or {},
        cost_estimate=pl.CostEstimate(flops=flops, transcendentals=0, bytes_accessed=moved),
    )


def pick_kernel(
    row, index_hbm, pool_hbm, metric_hbm, screening_hbm,
    own, edge, target, pick, index, pool, sems,
):
    h = HALO
    held, planes = pool.shape[0], pool.shape[1]
    orb = lax.axis_index("orb")
    side = upper_side()
    sibling = orb - 1 + 2 * side
    mine = side * (planes - h)
    parts = [
        (index_hbm, index),
        (pool_hbm, pool),
        (screening_hbm.at[pl.ds(mine, h)], edge.at[pl.ds(0, h)]),
        (metric_hbm.at[0, pl.ds(mine, h)], edge.at[pl.ds(h, h)]),
        (metric_hbm.at[1, pl.ds(mine, h)], edge.at[pl.ds(2 * h, h)]),
        (
            metric_hbm.at[2, pl.ds(side * (planes - h - 1), h + 1)],
            edge.at[pl.ds(3 * h, h + 1)],
        ),
    ]
    copies = [pltpu.make_async_copy(a, b, sems.at[i]) for i, (a, b) in enumerate(parts)]
    for copy in copies:
        copy.start()
    for copy in copies[:2]:
        copy.wait()
    for s in range(NSRC):
        group, place = index[s] // held, lax.rem(index[s], held)
        own[s] = jnp.where(group == orb, pool[place, pl.ds(mine, h)], 0.0)
        for r in range(held):
            there = jnp.logical_and(group == sibling, place == r)
            pick[s, r] = jnp.where(there, jnp.ones(pick.shape[2:], jnp.float32), 0.0)
    target[...] = pool[row[0]]
    edge[pl.ds(4 * h + 1, h)] = pool[row[0], pl.ds(mine, h)]
    rest = (edge.shape[0] - 5 * h - 1,) + edge.shape[1:]
    edge[pl.ds(5 * h + 1, rest[0])] = jnp.zeros(rest, jnp.float32)
    for copy in copies[2:]:
        copy.wait()


def gather_kernel(own, pick, pool, blank, part, edge):
    del blank
    h = HALO
    held, planes, gx = pool.shape[:3]
    mine = upper_side() * (planes - h)
    for s in range(NSRC):
        total = own[s]
        for r in range(held):
            total += jnp.tile(pick[s, r], (gx // pick.shape[2], 1)) * pool[r, pl.ds(mine, h)]
        part[s] = total
    for r in range(held):
        edge[pl.ds((5 + r) * h + 1, h)] = pool[r, pl.ds(mine, h)]


def merge_kernel(mine, theirs, both):
    both[...] = mine[...] + theirs[...]


def coefficient_kernel(
    row, target, metric, screening, near, far, coef, scaled, fx, fy, fz, scr, tgt
):
    side = upper_side()
    slab, slabs = lax.axis_index("slab"), lax.axis_size("slab")
    planes, gx, gy = screening.shape
    total = planes + 2 * HALO
    lower = side * (HALO + planes)
    upper = (1 - side) * (HALO + planes)
    h = HALO
    for halo, at, own_slot in ((near, lower, (5 + row[0]) * h + 1), (far, upper, 4 * h + 1)):
        scr[pl.ds(at, h)] = halo[0:h]
        fx[pl.ds(at, h)] = halo[h : 2 * h]
        fy[pl.ds(at, h)] = halo[2 * h : 3 * h]
        tgt[pl.ds(at, h)] = halo[pl.ds(own_slot, h)]
    low_z = jnp.where(side == 0, near[3 * h : 4 * h + 1], far[3 * h : 4 * h + 1])
    high_z = jnp.where(side == 0, far[3 * h : 4 * h], near[3 * h : 4 * h])
    fz[0 : h + 1] = low_z
    fz[h + 1 : h + 1 + planes] = metric[2]
    fz[h + 1 + planes :] = high_z
    scr[h : h + planes] = screening[...]
    fx[h : h + planes] = metric[0]
    fy[h : h + planes] = metric[1]
    tgt[h : h + planes] = target[...]
    first = jnp.where(slab == 0, h, 0)
    last = jnp.where(slab == slabs - 1, h + planes, total)
    x_id = lax.broadcasted_iota(jnp.int32, (gx, gy), 0)
    y_id = lax.broadcasted_iota(jnp.int32, (gx, gy), 1)

    @pl.loop(0, total)
    def _(e):
        z_hi, z_lo = fz[e + 1], fz[e]
        x_hi, y_hi = fx[e], fy[e]
        x_lo = jnp.where(x_id == 0, 0.0, pltpu.roll(x_hi, 1, 0))
        y_lo = jnp.where(y_id == 0, 0.0, pltpu.roll(y_hi, 1, 1))
        diag = scr[e] + z_hi + z_lo + x_hi + x_lo + y_hi + y_lo
        inside = jnp.logical_and(e >= first, e < last)
        inverse = 1.0 / jnp.where(inside, diag, 1.0)
        inverse = jnp.where(inside, inverse, 0.0)
        rows = pl.ds(pl.multiple_of(e * gx, gx), gx)
        coef[0, rows] = z_hi * inverse
        coef[1, rows] = z_lo * inverse
        coef[2, rows] = jnp.where(x_id == gx - 1, 0.0, x_hi * inverse)
        coef[3, rows] = x_lo * inverse
        coef[4, rows] = jnp.where(y_id == gy - 1, 0.0, y_hi * inverse)
        coef[5, rows] = y_lo * inverse
        scaled[rows] = tgt[e] * inverse


def sweep_rows(weight, coef, base, old, at, there, back, gy):
    c = [coef[i, pl.ds(at, 8)] for i in range(6)]
    for s in range(NSRC):
        v = old[s, pl.ds(there, 8)]
        total = base[s, pl.ds(there, 8)]
        total += c[0] * old[s, pl.ds(there + back, 8)]
        total += c[1] * old[s, pl.ds(there - back, 8)]
        total += c[2] * old[s, pl.ds(there + 1, 8)]
        total += c[3] * old[s, pl.ds(there - 1, 8)]
        total += c[4] * pltpu.roll(v, gy - 1, 1)
        total += c[5] * pltpu.roll(v, 1, 1)
        yield s, (1.0 - weight) * v + weight * total


def early_kernel(weights, coef, scaled, middle, halo, level, src, base, first):
    side = upper_side()
    h = HALO
    gx, gy = middle.shape[-2:]
    count = middle.shape[1] + halo.shape[1]
    planes = scaled.shape[0] // gx - 2 * h
    offset = side * (planes + 2 * h - count)
    for part, at in ((halo, side * h), (middle, (1 - side) * h)):
        for s in range(NSRC):
            src[s, pl.ds(pl.multiple_of(at * gx, gx), h * gx)] = part[s].reshape(h * gx, gy)

    @pl.loop(0, count, unroll=2)
    def _(i):
        here = pl.ds(pl.multiple_of(i * gx, gx), gx)
        t = scaled[pl.ds(pl.multiple_of((i + offset) * gx, gx), gx)]
        for s in range(NSRC):
            b = t * src[s, here]
            base[s, here] = b
            first[s, here] = weights[0] * b

    for k in range(1, h):
        old = first if k == 1 else level.at[k - 2]

        @pl.loop(k, count - k, unroll=min(4, count - 2 * k))
        def _(i):
            for j in range(0, gx, 8):
                there = pl.multiple_of(i * gx, gx) + j
                at = pl.multiple_of((i + offset) * gx, gx) + j
                for s, v in sweep_rows(weights[k], coef, base, old, at, there, gx, gy):
                    level[k - 1, s, pl.ds(there, 8)] = v


def sweep_kernel(weights, coef, scaled, middle, halo, sibling, level, out, src, base, field):
    side = upper_side()
    h = HALO
    gx, gy = out.shape[-2:]
    planes = out.shape[1]
    total = planes + 2 * h
    extra = middle.shape[1]
    count = extra + h
    halo_at = side * (h + planes)
    middle_at = h + side * (planes - extra)
    sibling_at = (1 - side) * (h + extra)
    for part, at in ((halo, halo_at), (middle, middle_at), (sibling, sibling_at)):
        size = part.shape[1]
        for s in range(NSRC):
            src[s, pl.ds(pl.multiple_of(at * gx, gx), size * gx)] = part[s].reshape(size * gx, gy)
    for k in range(2, SWEEPS):
        local = jnp.where(side == 0, count - k - 1, k - 1)
        taken = pl.ds(pl.multiple_of(local * gx, gx), 2 * gx)
        placed = pl.multiple_of((local + side * (total - count)) * gx, gx)
        for s in range(NSRC):
            field[k - 1, s, pl.ds(placed, 2 * gx)] = level[k - 2, s, taken]

    @pl.loop(0, total - h, unroll=2)
    def _(i):
        rows = pl.ds(pl.multiple_of((i + (1 - side) * h) * gx, gx), gx)
        t = scaled[rows]
        for s in range(NSRC):
            b = t * src[s, rows]
            base[s, rows] = b
            field[0, s, rows] = weights[0] * b

    for k in range(1, SWEEPS):
        begin = jnp.where(side == 0, count - k, k)

        @pl.loop(0, total - count, unroll=4)
        def _(i):
            for j in range(0, gx, 8):
                at = pl.multiple_of((begin + i) * gx, gx) + j
                acc = None
                for s, v in sweep_rows(weights[k], coef, base, field.at[k - 1], at, at, gx, gy):
                    if k < SWEEPS - 1:
                        field[k, s, pl.ds(at, 8)] = v
                    else:
                        term = v * src[s, pl.ds(at, 8)]
                        acc = term if acc is None else acc + term
                if k == SWEEPS - 1:
                    out[0, begin + i - h, j : j + 8] = acc


def shards(pool, target_row, source_index, metric, screening):
    held, planes, gx, gy = pool.shape
    n_orb, n_slab = lax.axis_size("orb"), lax.axis_size("slab")
    h = HALO
    weights = step_sizes(SWEEPS)
    side = upper_side()

    def place(o, z):
        return o * n_slab + z

    def among(moved):
        pairs = [
            (place(o, z), place(*moved(o, z)))
            for o in range(n_orb)
            for z in range(n_slab)
            if 0 <= moved(o, z)[1] < n_slab
        ]
        return lambda x: lax.ppermute(x, AXES, pairs)

    to_sibling = among(lambda o, z: (o ^ 1, z))
    to_slab = among(lambda o, z: (o ^ 1, z - 1 if o % 2 else z + 1))

    def next_slab(o, z):
        there = z - 1 if o % 2 else z + 1
        return (o ^ 1, there) if 0 <= there < n_slab else (o ^ 2, z)

    to_slab_all = among(next_slab)
    bits = [1 << b for b in range(1, n_orb.bit_length() - 1)]

    theirs = to_sibling(pool)
    own, edge, target, pick = call(
        pick_kernel,
        [
            (NSRC, h, gx, gy),
            ((5 + held) * h + 1, gx, gy),
            (planes, gx, gy),
            (NSRC, held, 8, gy),
        ],
        [SMEM] + [HBM] * 4,
        [
            pltpu.SMEM(source_index.shape, jnp.int32),
            pltpu.VMEM(pool.shape, jnp.float32),
            pltpu.SemaphoreType.DMA((6,)),
        ],
        moved=4 << 20,
    )(target_row, *[
        pltpu.with_memory_space_constraint(x, pltpu.HBM)
        for x in (source_index, pool, metric, screening)
    ])
    part, edge = call(gather_kernel, [own.shape, edge.shape], [VMEM] * 4, alias={3: 1})(
        own, pick, theirs, edge
    )
    near = to_slab(edge)
    for step, (low, high) in enumerate(zip(bits, reversed(bits))):
        across = among(lambda o, z: (o ^ (high if o % 2 else low), z))
        merge = call(merge_kernel, [part.shape], [VMEM] * 2, flops=0 if step else HINT)
        (part,) = merge(part, across(part))
    halo = to_slab_all(part)
    cut = (5 * h + 1) // 2
    far = jnp.concatenate([to_sibling(near[:cut]), to_sibling(near[cut : 5 * h + 1])], axis=0)
    total = planes + 2 * h
    coef, scaled = call(
        coefficient_kernel,
        [(6, total * gx, gy), (total * gx, gy)],
        [SMEM] + [VMEM] * 5,
        [pltpu.VMEM((total, gx, gy), jnp.float32)] * 2
        + [pltpu.VMEM((total + 1, gx, gy), jnp.float32)]
        + [pltpu.VMEM((total, gx, gy), jnp.float32)] * 2,
        moved=0,
    )(target_row, target, metric, screening, near, far)
    halo, coef, scaled = lax.optimization_barrier((halo, coef, scaled))
    kept = planes - h
    lacks = jnp.where(
        side == 0,
        jnp.concatenate([halo, part[:, :kept]], axis=1),
        jnp.concatenate([part[:, h - kept :], halo], axis=1),
    )
    sibling = to_sibling(lacks)
    count = 2 * h
    own_field = pltpu.VMEM((NSRC, count * gx, gy), jnp.float32)
    (level,) = call(
        functools.partial(early_kernel, weights),
        [(SWEEPS - 2, NSRC, count * gx, gy)],
        [VMEM] * 4,
        [own_field] * 3,
    )(coef, scaled, part, halo)
    field = pltpu.VMEM((NSRC, total * gx, gy), jnp.float32)
    (out,) = call(
        functools.partial(sweep_kernel, weights),
        [(1, planes, gx, gy)],
        [VMEM] * 6,
        [field] * 2 + [pltpu.VMEM((SWEEPS - 1, NSRC, total * gx, gy), jnp.float32)],
    )(coef, scaled, part, halo, sibling, level)
    return out


def solution(mesh):
    in_specs = (
        P("orb", "slab", None, None),
        P("orb"),
        P(),
        P(None, "slab", None, None),
        P("slab", None, None),
    )
    out_specs = P("orb", "slab", None, None)
    return jax.shard_map(shards, mesh=mesh, in_specs=in_specs, out_specs=out_specs, check_vma=False)
```

time: 27.4 us -> 25.7 us (0.938)
  waiting for transfers between devices: 10.9 us -> 8.41 us
  starting transfers between devices: 8.88 us -> 9.64 us
    ppermute x9 -> x8, waiting for transfers between devices: 10.9 us -> 8.41 us  [among(): return lambda x: lax.ppermute(x, AXES, pairs)]
    pallas_call x1, Pallas kernels: 3.76 us -> 2.6 us  [shards(): call(functools.partial(sweep_kernel, weights), [(1, planes, gx, gy)], [VM...]
    pallas_call x3 -> x4, Pallas kernels: 2.85 us -> 3.95 us  [the longest x1 1.66 us: shards(): call(coefficient_kernel, [(6, total * gx, gy), (total * gx, gy)], [SMEM]...]
    ppermute x9 -> x8, starting transfers between devices: 8.88 us -> 9.64 us  [among(): return lambda x: lax.ppermute(x, AXES, pairs)]
  transfers between devices with their start and end apart: 9 -> 8, of which waited for: 7 -> 7; matrix products, arithmetic and copies ran while one was open for 0% -> 0% of each run, Pallas kernels for 10% -> 15%
where the time goes in v5:
time: 25.7 us; the launch traced here: 25.6 us
  starting transfers between devices  9.64 us (38%)
  waiting for transfers between devices  8.41 us (33%)
  Pallas kernels  6.61 us (26%)
  between operations  0.78 us (3%)
    ppermute x8, starting transfers between devices, among(): return lambda x: lax.ppermute(x, AXES, pairs)  9.64 us
    ppermute x8, waiting for transfers between devices, among(): return lambda x: lax.ppermute(x, AXES, pairs)  8.41 us
    pallas_call x1, Pallas kernels, shards(): call(functools.partial(sweep_kernel, weights), [(1, planes, gx, gy)], [VM...  2.6 us
    pallas_call x1, Pallas kernels, shards(): call(coefficient_kernel, [(6, total * gx, gy), (total * gx, gy)], [SMEM]...  1.66 us
    pallas_call x1, Pallas kernels, shards(): call(pick_kernel, [(NSRC, h, gx, gy), ((5 + held) * h + 1, gx, gy), (plan...  1.14 us
    pallas_call x1, Pallas kernels, shards(): call(functools.partial(early_kernel, weights), [(SWEEPS - 2, NSRC, count...  1.09 us
  transfers between devices with their start and end apart: 8, of which 7 were waited for; matrix products, arithmetic and copies ran while one was open for 0% of the time, Pallas kernels for 15%

profile of v5, /device:TPU:0, one launch (start us, length us, event | category | flops | bytes accessed | tf_op | source)
XLA Modules:
  0.0 25.6 jit_solution(11395391871654276327)
XLA Ops:
  0.0 0.5 %collective-permute-start = (f32[2,8,32,128]{3,2,1,0:T(8,128)}, f32[2,8,32,128]{3,2,1,0:T(8,128)S(1)}, u32[]{:S(2)}, u32[]{:S(2)}) collective-permute-start(f32[2,8,32,128]{3,2,1,0:T(8,128)} %pool_hbm.1), channel_id=1, source_target_pairs={{0,4},{1,5},{2,6},{3,7},{4,0},{5,1},{6,2},{7,3},{8,12},{9,13},{10,... | collective-permute-start | bytes 786440 | tf_op jit(solution)/shard_map/ppermute | solution.py:263
  1.1 1.1 %shard_map.55 = (f32[3,5,32,128]{3,2,1,0:T(8,128)S(1)}, f32[36,32,128]{2,1,0:T(8,128)S(1)}, f32[8,32,128]{2,1,0:T(8,128)S(1)}, f32[3,2,8,128]{3,2,1,0:T(8,128)S(1)}) custom-call(s32[1]{0:T(128)S(6)} %copy.8.row, s32[3]{0:T(128)} %index_hbm.1, f32[2,8,32,128]{3,2,1,0:T(8,128)} %pool_hbm.1, f32[3,8,32,128]{3,2,1,0:T(8,128)} %metric.1, f32[8,32,128]{2,1,0:T(8,128)} %screening.1), custom_call_target="tpu_custom_call" | custom-call | bytes 4194304 | tf_op jit(solution)/shard_map/pallas_call | solution.py:276
  2.3 0.0 collective-permute-done.pool
  2.3 0.1 shard_map.56
  2.3 2.6 %collective-permute-start.1 = (f32[3,5,32,128]{3,2,1,0:T(8,128)S(1)}, f32[3,5,32,128]{3,2,1,0:T(8,128)S(1)}, u32[]{:S(2)}, u32[]{:S(2)}) collective-permute-start(f32[3,5,32,128]{3,2,1,0:T(8,128)S(1)} %get-tuple-element.19.mine), channel_id=1, source_target_pairs={{0,8},{1,9},{2,10},{3,11},{4,20},{5,21},{6,22},{7,23},{8,0},{9,1},... | collective-permute-start | bytes 737288 | tf_op jit(solution)/shard_map/ppermute | solution.py:263
  4.9 3.3 %collective-permute-start.4 = (f32[36,32,128]{2,1,0:T(8,128)S(1)}, f32[36,32,128]{2,1,0:T(8,128)S(1)}, u32[]{:S(2)}, u32[]{:S(2)}) collective-permute-start(f32[36,32,128]{2,1,0:T(8,128)S(1)} %get-tuple-element.21), channel_id=1, source_target_pairs={{0,5},{1,6},{2,7},{5,0},{6,1},{7,2},{8,13},{9,14},{10,15},{13,8},{... | collective-permute-start | bytes 1769480 | tf_op jit(solution)/shard_map/ppermute | solution.py:263
  8.2 0.8 %collective-permute-done.1.theirs = f32[3,5,32,128]{3,2,1,0:T(8,128)S(1)} collective-permute-done((f32[3,5,32,128]{3,2,1,0:T(8,128)S(1)}, f32[3,5,32,128]{3,2,1,0:T(8,128)S(1)}, u32[]{:S(2)}, u32[]{:S(2)}) %collective-permute-start.1) | collective-permute-done | bytes 245792 | tf_op jit(solution)/shard_map/ppermute | solution.py:263
  9.1 0.0 copy-start
  9.1 0.0 copy-start.1
  9.1 2.1 %collective-permute-start.2 = (f32[3,5,32,128]{3,2,1,0:T(8,128)S(1)}, f32[3,5,32,128]{3,2,1,0:T(8,128)S(1)}, u32[]{:S(2)}, u32[]{:S(2)}) collective-permute-start(f32[3,5,32,128]{3,2,1,0:T(8,128)S(1)} %shard_map.57.mine), channel_id=1, source_target_pairs={{0,16},{1,17},{2,18},{3,19},{4,12},{5,13},{6,14},{7,15},{8,24},{9,... | collective-permute-start | bytes 737288 | tf_op jit(solution)/shard_map/ppermute | solution.py:263
  11.2 4.2 %collective-permute-done.2.theirs = f32[3,5,32,128]{3,2,1,0:T(8,128)S(1)} collective-permute-done((f32[3,5,32,128]{3,2,1,0:T(8,128)S(1)}, f32[3,5,32,128]{3,2,1,0:T(8,128)S(1)}, u32[]{:S(2)}, u32[]{:S(2)}) %collective-permute-start.2) | collective-permute-done | bytes 245792 | tf_op jit(solution)/shard_map/ppermute | solution.py:263
  15.4 0.5 %collective-permute-start.3 = (f32[3,5,32,128]{3,2,1,0:T(8,128)S(1)}, f32[3,5,32,128]{3,2,1,0:T(8,128)S(1)}, u32[]{:S(2)}, u32[]{:S(2)}) collective-permute-start(f32[3,5,32,128]{3,2,1,0:T(8,128)S(1)} %shard_map.58.middle), channel_id=1, source_target_pairs={{0,5},{1,6},{2,7},{3,11},{4,12},{5,0},{6,1},{7,2},{8,13},{9,14},{1... | collective-permute-start | bytes 737288 | tf_op jit(solution)/shard_map/ppermute | solution.py:263
  16.0 0.1 collective-permute-done.4.near
  16.1 0.1 collective-permute-start.5
  16.2 0.5 %collective-permute-start.6 = (f32[13,32,128]{2,1,0:T(8,128)S(1)}, f32[13,32,128]{2,1,0:T(8,128)S(1)}, u32[]{:S(2)}, u32[]{:S(2)}) collective-permute-start(f32[13,32,128]{2,1,0:T(8,128)S(1)} %get-tuple-element.28), channel_id=1, source_target_pairs={{0,4},{1,5},{2,6},{3,7},{4,0},{5,1},{6,2},{7,3},{8,12},{9,13},{10,... | collective-permute-start | bytes 638984 | tf_op jit(solution)/shard_map/ppermute | solution.py:263
  16.7 0.9 %collective-permute-done.5 = f32[13,32,128]{2,1,0:T(8,128)S(1)} collective-permute-done((f32[13,32,128]{2,1,0:T(8,128)S(1)}, f32[13,32,128]{2,1,0:T(8,128)S(1)}, u32[]{:S(2)}, u32[]{:S(2)}) %collective-permute-start.5) | collective-permute-done | bytes 213024 | tf_op jit(solution)/shard_map/ppermute | solution.py:263
  17.6 0.3 %collective-permute-done.6 = f32[13,32,128]{2,1,0:T(8,128)S(1)} collective-permute-done((f32[13,32,128]{2,1,0:T(8,128)S(1)}, f32[13,32,128]{2,1,0:T(8,128)S(1)}, u32[]{:S(2)}, u32[]{:S(2)}) %collective-permute-start.6) | collective-permute-done | bytes 213024 | tf_op jit(solution)/shard_map/ppermute | solution.py:263
  18.0 0.0 copy-done
  18.0 0.0 copy-done.1
  18.0 1.7 %shard_map.59 = (f32[6,576,128]{2,1,0:T(8,128)S(1)}, f32[576,128]{1,0:T(8,128)S(1)}) custom-call(s32[1]{0:T(128)S(6)} %copy.8.row, f32[8,32,128]{2,1,0:T(8,128)S(1)} %get-tuple-element.20.target, f32[3,8,32,128]{3,2,1,0:T(8,128)S(1)} %copy-done, f32[8,32,128]{2,1,0:T(8,128)S(1)} %copy-done.1, f32[36,32,128]{2,1,0:T(8,128)S(1)} %collective-permute-done.4.near, ...), custom_call_target="tpu_custom_call" | custom-call | tf_op jit(solution)/shard_map/pallas_call | solution.py:307
  19.7 1.5 %collective-permute-done.3.halo = f32[3,5,32,128]{3,2,1,0:T(8,128)S(1)} collective-permute-done((f32[3,5,32,128]{3,2,1,0:T(8,128)S(1)}, f32[3,5,32,128]{3,2,1,0:T(8,128)S(1)}, u32[]{:S(2)}, u32[]{:S(2)}) %collective-permute-start.3) | collective-permute-done | bytes 245792 | tf_op jit(solution)/shard_map/ppermute | solution.py:263
  21.2 0.1 collective-permute-start.7
  21.2 1.1 %shard_map.60.level = f32[4,3,320,128]{3,2,1,0:T(8,128)S(1)} custom-call(f32[6,576,128]{2,1,0:T(8,128)S(1)} %get-tuple-element.24.coef, f32[576,128]{1,0:T(8,128)S(1)} %get-tuple-element.25.scaled, f32[3,5,32,128]{3,2,1,0:T(8,128)S(1)} %shard_map.58.middle, f32[3,5,32,128]{3,2,1,0:T(8,128)S(1)} %collective-permute-done.3.halo), custom_call_target="tpu_custom_call" | custom-call | tf_op jit(solution)/shard_map/pallas_call | solution.py:326
  22.4 0.6 %collective-permute-done.7.sibling = f32[3,8,32,128]{3,2,1,0:T(8,128)S(1)} collective-permute-done((f32[3,8,32,128]{3,2,1,0:T(8,128)S(1)}, f32[3,8,32,128]{3,2,1,0:T(8,128)S(1)}, u32[]{:S(2)}, u32[]{:S(2)}) %collective-permute-start.7) | collective-permute-done | bytes 393248 | tf_op jit(solution)/shard_map/ppermute | solution.py:263
  23.0 2.6 %shard_map.61 = f32[1,8,32,128]{3,2,1,0:T(8,128)} custom-call(f32[6,576,128]{2,1,0:T(8,128)S(1)} %get-tuple-element.24.coef, f32[576,128]{1,0:T(8,128)S(1)} %get-tuple-element.25.scaled, f32[3,5,32,128]{3,2,1,0:T(8,128)S(1)} %shard_map.58.middle, f32[3,5,32,128]{3,2,1,0:T(8,128)S(1)} %collective-permute-done.3.halo, ...), custom_call_target="tpu_custom_call" | custom-call | tf_op jit(solution)/shard_map/pallas_call | solution.py:333
  (6 shorter events, 0.2 us)
Async XLA Ops:
  0.0 2.3 %collective-permute-start = (f32[2,8,32,128]{3,2,1,0:T(8,128)}, f32[2,8,32,128]{3,2,1,0:T(8,128)S(1)}, u32[]{:S(2)}, u32[]{:S(2)}) collective-permute-start(f32[2,8,32,128]{3,2,1,0:T(8,128)} %pool_hbm.1), channel_id=1, source_target_pairs={{0,4},{1,5},{2,6},{3,7},{4,0},{5,1},{6,2},{7,3},{8,12},{9,13},{10,... | collective-permute-start | bytes 786440 | tf_op jit(solution)/shard_map/ppermute | solution.py:263
  2.3 6.7 %collective-permute-start.1 = (f32[3,5,32,128]{3,2,1,0:T(8,128)S(1)}, f32[3,5,32,128]{3,2,1,0:T(8,128)S(1)}, u32[]{:S(2)}, u32[]{:S(2)}) collective-permute-start(f32[3,5,32,128]{3,2,1,0:T(8,128)S(1)} %get-tuple-element.19.mine), channel_id=1, source_target_pairs={{0,8},{1,9},{2,10},{3,11},{4,20},{5,21},{6,22},{7,23},{8,0},{9,1},... | collective-permute-start | bytes 737288 | tf_op jit(solution)/shard_map/ppermute | solution.py:263
  4.9 11.2 %collective-permute-start.4 = (f32[36,32,128]{2,1,0:T(8,128)S(1)}, f32[36,32,128]{2,1,0:T(8,128)S(1)}, u32[]{:S(2)}, u32[]{:S(2)}) collective-permute-start(f32[36,32,128]{2,1,0:T(8,128)S(1)} %get-tuple-element.21), channel_id=1, source_target_pairs={{0,5},{1,6},{2,7},{5,0},{6,1},{7,2},{8,13},{9,14},{10,15},{13,8},{... | collective-permute-start | bytes 1769480 | tf_op jit(solution)/shard_map/ppermute | solution.py:263
  9.1 8.9 %copy-start = (f32[3,8,32,128]{3,2,1,0:T(8,128)S(1)}, f32[3,8,32,128]{3,2,1,0:T(8,128)}, u32[]{:S(2)}) copy-start(f32[3,8,32,128]{3,2,1,0:T(8,128)} %metric.1) | copy-start | bytes 1179652
  9.1 8.9 %copy-start.1 = (f32[8,32,128]{2,1,0:T(8,128)S(1)}, f32[8,32,128]{2,1,0:T(8,128)}, u32[]{:S(2)}) copy-start(f32[8,32,128]{2,1,0:T(8,128)} %screening.1) | copy-start | bytes 393220
  9.1 6.3 %collective-permute-start.2 = (f32[3,5,32,128]{3,2,1,0:T(8,128)S(1)}, f32[3,5,32,128]{3,2,1,0:T(8,128)S(1)}, u32[]{:S(2)}, u32[]{:S(2)}) collective-permute-start(f32[3,5,32,128]{3,2,1,0:T(8,128)S(1)} %shard_map.57.mine), channel_id=1, source_target_pairs={{0,16},{1,17},{2,18},{3,19},{4,12},{5,13},{6,14},{7,15},{8,24},{9,... | collective-permute-start | bytes 737288 | tf_op jit(solution)/shard_map/ppermute | solution.py:263
  15.4 5.7 %collective-permute-start.3 = (f32[3,5,32,128]{3,2,1,0:T(8,128)S(1)}, f32[3,5,32,128]{3,2,1,0:T(8,128)S(1)}, u32[]{:S(2)}, u32[]{:S(2)}) collective-permute-start(f32[3,5,32,128]{3,2,1,0:T(8,128)S(1)} %shard_map.58.middle), channel_id=1, source_target_pairs={{0,5},{1,6},{2,7},{3,11},{4,12},{5,0},{6,1},{7,2},{8,13},{9,14},{1... | collective-permute-start | bytes 737288 | tf_op jit(solution)/shard_map/ppermute | solution.py:263
  16.1 1.5 %collective-permute-start.5 = (f32[13,32,128]{2,1,0:T(8,128)S(1)}, f32[13,32,128]{2,1,0:T(8,128)S(1)}, u32[]{:S(2)}, u32[]{:S(2)}) collective-permute-start(f32[13,32,128]{2,1,0:T(8,128)S(1)} %get-tuple-element.27), channel_id=1, source_target_pairs={{0,4},{1,5},{2,6},{3,7},{4,0},{5,1},{6,2},{7,3},{8,12},{9,13},{10,... | collective-permute-start | bytes 638984 | tf_op jit(solution)/shard_map/ppermute | solution.py:263
  16.2 1.8 %collective-permute-start.6 = (f32[13,32,128]{2,1,0:T(8,128)S(1)}, f32[13,32,128]{2,1,0:T(8,128)S(1)}, u32[]{:S(2)}, u32[]{:S(2)}) collective-permute-start(f32[13,32,128]{2,1,0:T(8,128)S(1)} %get-tuple-element.28), channel_id=1, source_target_pairs={{0,4},{1,5},{2,6},{3,7},{4,0},{5,1},{6,2},{7,3},{8,12},{9,13},{10,... | collective-permute-start | bytes 638984 | tf_op jit(solution)/shard_map/ppermute | solution.py:263
  21.2 1.8 %collective-permute-start.7 = (f32[3,8,32,128]{3,2,1,0:T(8,128)S(1)}, f32[3,8,32,128]{3,2,1,0:T(8,128)S(1)}, u32[]{:S(2)}, u32[]{:S(2)}) collective-permute-start(f32[3,8,32,128]{3,2,1,0:T(8,128)S(1)} %maximum_select_fusion), channel_id=1, source_target_pairs={{0,4},{1,5},{2,6},{3,7},{4,0},{5,1},{6,2},{7,3},{8,12},{9,13},{10,... | collective-permute-start | bytes 1179656 | tf_op jit(solution)/shard_map/ppermute | solution.py:263

commit v6 on v5

--- a/solution.py
+++ b/solution.py
@@ -13,6 +13,7 @@
 HALO = SWEEPS - 1
 AXES = ("orb", "slab")
 HINT = 10**10
+PIECES = 3
 VMEM = pl.BlockSpec(memory_space=pltpu.VMEM)
 SMEM = pl.BlockSpec(memory_space=pltpu.SMEM)
 HBM = pl.BlockSpec(memory_space=pltpu.HBM)
@@ -42,8 +43,7 @@
 
 
 def pick_kernel(
-    row, index_hbm, pool_hbm, metric_hbm, screening_hbm,
-    own, edge, target, pick, index, pool, sems,
+    index_hbm, pool_hbm, metric_hbm, screening_hbm, own, edge, pick, pool, index, sems
 ):
     h = HALO
     held, planes = pool.shape[0], pool.shape[1]
@@ -69,30 +69,32 @@
         copy.wait()
     for s in range(NSRC):
         group, place = index[s] // held, lax.rem(index[s], held)
-        own[s] = jnp.where(group == orb, pool[place, pl.ds(mine, h)], 0.0)
+        own[s] = jnp.where(group == orb, pool[place], 0.0)
         for r in range(held):
             there = jnp.logical_and(group == sibling, place == r)
             pick[s, r] = jnp.where(there, jnp.ones(pick.shape[2:], jnp.float32), 0.0)
-    target[...] = pool[row[0]]
-    edge[pl.ds(4 * h + 1, h)] = pool[row[0], pl.ds(mine, h)]
-    rest = (edge.shape[0] - 5 * h - 1,) + edge.shape[1:]
-    edge[pl.ds(5 * h + 1, rest[0])] = jnp.zeros(rest, jnp.float32)
+    rest = (edge.shape[0] - 4 * h - 1,) + edge.shape[1:]
+    edge[pl.ds(4 * h + 1, rest[0])] = jnp.zeros(rest, jnp.float32)
     for copy in copies[2:]:
         copy.wait()
 
 
-def gather_kernel(own, pick, pool, blank, part, edge):
+def gather_kernel(own, pick, pool, theirs, blank, keep, send, edge):
     del blank
     h = HALO
     held, planes, gx = pool.shape[:3]
-    mine = upper_side() * (planes - h)
-    for s in range(NSRC):
-        total = own[s]
-        for r in range(held):
-            total += jnp.tile(pick[s, r], (gx // pick.shape[2], 1)) * pool[r, pl.ds(mine, h)]
-        part[s] = total
+    side = upper_side()
+    mine = side * (planes - h)
+    for part, start in ((send, (1 - side) * (planes - h)), (keep, mine)):
+        for s in range(NSRC):
+            total = own[s, pl.ds(start, h)]
+            for r in range(held):
+                factor = jnp.tile(pick[s, r], (gx // pick.shape[2], 1))
+                total += factor * theirs[r, pl.ds(start, h)]
+            part[s] = total
     for r in range(held):
-        edge[pl.ds((5 + r) * h + 1, h)] = pool[r, pl.ds(mine, h)]
+        edge[pl.ds((4 + r) * h + 1, h)] = pool[r, pl.ds(mine, h)]
+        edge[pl.ds((4 + held + r) * h + 1, h)] = theirs[r, pl.ds(mine, h)]
 
 
 def merge_kernel(mine, theirs, both):
@@ -100,7 +102,7 @@
 
 
 def coefficient_kernel(
-    row, target, metric, screening, near, far, coef, scaled, fx, fy, fz, scr, tgt
+    row, pool, metric, screening, near, far, coef, scaled, fx, fy, fz, scr, tgt
 ):
     side = upper_side()
     slab, slabs = lax.axis_index("slab"), lax.axis_size("slab")
@@ -109,7 +111,10 @@
     lower = side * (HALO + planes)
     upper = (1 - side) * (HALO + planes)
     h = HALO
-    for halo, at, own_slot in ((near, lower, (5 + row[0]) * h + 1), (far, upper, 4 * h + 1)):
+    held = pool.shape[0]
+    near_row = (4 + held + row[0]) * h + 1
+    far_row = (4 + row[0]) * h + 1
+    for halo, at, own_slot in ((near, lower, near_row), (far, upper, far_row)):
         scr[pl.ds(at, h)] = halo[0:h]
         fx[pl.ds(at, h)] = halo[h : 2 * h]
         fy[pl.ds(at, h)] = halo[2 * h : 3 * h]
@@ -122,13 +127,13 @@
     scr[h : h + planes] = screening[...]
     fx[h : h + planes] = metric[0]
     fy[h : h + planes] = metric[1]
-    tgt[h : h + planes] = target[...]
+    tgt[h : h + planes] = pool[row[0]]
     first = jnp.where(slab == 0, h, 0)
     last = jnp.where(slab == slabs - 1, h + planes, total)
     x_id = lax.broadcasted_iota(jnp.int32, (gx, gy), 0)
     y_id = lax.broadcasted_iota(jnp.int32, (gx, gy), 1)
 
-    @pl.loop(0, total)
+    @pl.loop(0, total, unroll=6)
     def _(e):
         z_hi, z_lo = fz[e + 1], fz[e]
         x_hi, y_hi = fx[e], fy[e]
@@ -273,36 +278,39 @@
     bits = [1 << b for b in range(1, n_orb.bit_length() - 1)]
 
     theirs = to_sibling(pool)
-    own, edge, target, pick = call(
+    own, edge, pick, pool_here = call(
         pick_kernel,
         [
-            (NSRC, h, gx, gy),
-            ((5 + held) * h + 1, gx, gy),
-            (planes, gx, gy),
+            (NSRC,) + pool.shape[1:],
+            ((4 + 2 * held) * h + 1, gx, gy),
             (NSRC, held, 8, gy),
+            pool.shape,
         ],
-        [SMEM] + [HBM] * 4,
-        [
-            pltpu.SMEM(source_index.shape, jnp.int32),
-            pltpu.VMEM(pool.shape, jnp.float32),
-            pltpu.SemaphoreType.DMA((6,)),
-        ],
+        [HBM] * 4,
+        [pltpu.SMEM(source_index.shape, jnp.int32), pltpu.SemaphoreType.DMA((6,))],
         moved=4 << 20,
-    )(target_row, *[
+    )(*[
         pltpu.with_memory_space_constraint(x, pltpu.HBM)
         for x in (source_index, pool, metric, screening)
     ])
-    part, edge = call(gather_kernel, [own.shape, edge.shape], [VMEM] * 4, alias={3: 1})(
-        own, pick, theirs, edge
-    )
+    keep, send, edge = call(
+        gather_kernel,
+        [(NSRC, h, gx, gy)] * 2 + [edge.shape],
+        [VMEM] * 5,
+        alias={4: 2},
+    )(own, pick, pool_here, theirs, edge)
     near = to_slab(edge)
-    for step, (low, high) in enumerate(zip(bits, reversed(bits))):
-        across = among(lambda o, z: (o ^ (high if o % 2 else low), z))
+    part = keep
+    for step in range(len(bits)):
+        low, high = (bits[0], bits[-1]) if step == 0 else (bits[-1 - step], bits[step])
+        swap = 1 if step == 0 else 0
+        across = among(lambda o, z: (o ^ swap ^ (high if o % 2 else low), z))
         merge = call(merge_kernel, [part.shape], [VMEM] * 2, flops=0 if step else HINT)
-        (part,) = merge(part, across(part))
+        (part,) = merge(part, across(send if step == 0 else part))
     halo = to_slab_all(part)
-    cut = (5 * h + 1) // 2
-    far = jnp.concatenate([to_sibling(near[:cut]), to_sibling(near[cut : 5 * h + 1])], axis=0)
+    last = (4 + held) * h + 1
+    cuts = [last * i // PIECES for i in range(PIECES + 1)]
+    far = jnp.concatenate([to_sibling(near[a:b]) for a, b in zip(cuts, cuts[1:])], axis=0)
     total = planes + 2 * h
     coef, scaled = call(
         coefficient_kernel,
@@ -312,7 +320,7 @@
         + [pltpu.VMEM((total + 1, gx, gy), jnp.float32)]
         + [pltpu.VMEM((total, gx, gy), jnp.float32)] * 2,
         moved=0,
-    )(target_row, target, metric, screening, near, far)
+    )(target_row, pool_here, metric, screening, near, far)
     halo, coef, scaled = lax.optimization_barrier((halo, coef, scaled))
     kept = planes - h
     lacks = jnp.where(

time: 25.7 us -> 25.1 us (0.977)
  Pallas kernels: 6.61 us -> 5.49 us
  starting transfers between devices: 9.64 us -> 10.4 us
  waiting for transfers between devices: 8.41 us -> 8.15 us
    pallas_call x1, Pallas kernels: 1.66 us -> 0.5 us  [shards(): call(coefficient_kernel, [(6, total * gx, gy), (total * gx, gy)], [SMEM]...]
    ppermute x8 -> x9, starting transfers between devices: 9.64 us -> 10.4 us  [among(): return lambda x: lax.ppermute(x, AXES, pairs)]
    ppermute x8 -> x9, waiting for transfers between devices: 8.41 us -> 8.15 us  [among(): return lambda x: lax.ppermute(x, AXES, pairs)]
  transfers between devices with their start and end apart: 8 -> 9, of which waited for: 7 -> 8; matrix products, arithmetic and copies ran while one was open for 0% -> 0% of each run, Pallas kernels for 15% -> 11%
where the time goes in v6:
time: 25.1 us; the launch traced here: 25 us
  starting transfers between devices  10.4 us (41%)
  waiting for transfers between devices  8.15 us (32%)
  Pallas kernels  5.49 us (22%)
  between operations  0.77 us (3%)
    ppermute x9, starting transfers between devices, among(): return lambda x: lax.ppermute(x, AXES, pairs)  10.4 us
    ppermute x9, waiting for transfers between devices, among(): return lambda x: lax.ppermute(x, AXES, pairs)  8.15 us
    pallas_call x1, Pallas kernels, shards(): call(functools.partial(sweep_kernel, weights), [(1, planes, gx, gy)], [VM...  2.6 us
    pallas_call x1, Pallas kernels, shards(): call(pick_kernel, [(NSRC,) + pool.shape[1:], ((4 + 2 * held) * h + 1, gx,...  1.14 us
    pallas_call x1, Pallas kernels, shards(): call(functools.partial(early_kernel, weights), [(SWEEPS - 2, NSRC, count...  1.09 us
  transfers between devices with their start and end apart: 9, of which 8 were waited for; matrix products, arithmetic and copies ran while one was open for 0% of the time, Pallas kernels for 11%

profile of v6, /device:TPU:0, one launch (start us, length us, event | category | flops | bytes accessed | tf_op | source)
XLA Modules:
  0.0 25.0 jit_solution(7498494779543561305)
XLA Ops:
  0.0 0.5 %collective-permute-start = (f32[2,8,32,128]{3,2,1,0:T(8,128)}, f32[2,8,32,128]{3,2,1,0:T(8,128)S(1)}, u32[]{:S(2)}, u32[]{:S(2)}) collective-permute-start(f32[2,8,32,128]{3,2,1,0:T(8,128)} %pool_hbm.1), channel_id=1, source_target_pairs={{0,4},{1,5},{2,6},{3,7},{4,0},{5,1},{6,2},{7,3},{8,12},{9,13},{10,... | collective-permute-start | bytes 786440 | tf_op jit(solution)/shard_map/ppermute | solution.py:268
  0.5 1.1 %shard_map.55 = (f32[3,8,32,128]{3,2,1,0:T(8,128)S(1)}, f32[41,32,128]{2,1,0:T(8,128)S(1)}, f32[3,2,8,128]{3,2,1,0:T(8,128)S(1)}, f32[2,8,32,128]{3,2,1,0:T(8,128)S(1)}) custom-call(s32[3]{0:T(128)} %index_hbm.1, f32[2,8,32,128]{3,2,1,0:T(8,128)} %pool_hbm.1, f32[3,8,32,128]{3,2,1,0:T(8,128)} %metric.1, f32[8,32,128]{2,1,0:T(8,128)} %screening.1), custom_call_target="tpu_custom_call" | custom-call | bytes 4194304 | tf_op jit(solution)/shard_map/pallas_call | solution.py:281
  1.6 0.2 collective-permute-done.theirs
  1.8 0.1 shard_map.56
  1.9 2.7 %collective-permute-start.1 = (f32[3,5,32,128]{3,2,1,0:T(8,128)S(1)}, f32[3,5,32,128]{3,2,1,0:T(8,128)S(1)}, u32[]{:S(2)}, u32[]{:S(2)}) collective-permute-start(f32[3,5,32,128]{3,2,1,0:T(8,128)S(1)} %get-tuple-element.22), channel_id=1, source_target_pairs={{0,12},{1,13},{2,14},{3,15},{4,16},{5,17},{6,18},{7,19},{8,4},{9,5... | collective-permute-start | bytes 737288 | tf_op jit(solution)/shard_map/ppermute | solution.py:268
  4.6 3.5 %collective-permute-start.4 = (f32[41,32,128]{2,1,0:T(8,128)S(1)}, f32[41,32,128]{2,1,0:T(8,128)S(1)}, u32[]{:S(2)}, u32[]{:S(2)}) collective-permute-start(f32[41,32,128]{2,1,0:T(8,128)S(1)} %get-tuple-element.23), channel_id=1, source_target_pairs={{0,5},{1,6},{2,7},{5,0},{6,1},{7,2},{8,13},{9,14},{10,15},{13,8},{... | collective-permute-start | bytes 2015240 | tf_op jit(solution)/shard_map/ppermute | solution.py:268
  8.1 0.4 %collective-permute-done.1.theirs = f32[3,5,32,128]{3,2,1,0:T(8,128)S(1)} collective-permute-done((f32[3,5,32,128]{3,2,1,0:T(8,128)S(1)}, f32[3,5,32,128]{3,2,1,0:T(8,128)S(1)}, u32[]{:S(2)}, u32[]{:S(2)}) %collective-permute-start.1) | collective-permute-done | bytes 245792 | tf_op jit(solution)/shard_map/ppermute | solution.py:268
  8.5 0.0 copy-start
  8.5 0.0 copy-start.1
  8.5 2.0 %collective-permute-start.2 = (f32[3,5,32,128]{3,2,1,0:T(8,128)S(1)}, f32[3,5,32,128]{3,2,1,0:T(8,128)S(1)}, u32[]{:S(2)}, u32[]{:S(2)}) collective-permute-start(f32[3,5,32,128]{3,2,1,0:T(8,128)S(1)} %shard_map.57.mine), channel_id=1, source_target_pairs={{0,8},{1,9},{2,10},{3,11},{4,20},{5,21},{6,22},{7,23},{8,0},{9,1},... | collective-permute-start | bytes 737288 | tf_op jit(solution)/shard_map/ppermute | solution.py:268
  11.2 3.6 %collective-permute-done.2.theirs = f32[3,5,32,128]{3,2,1,0:T(8,128)S(1)} collective-permute-done((f32[3,5,32,128]{3,2,1,0:T(8,128)S(1)}, f32[3,5,32,128]{3,2,1,0:T(8,128)S(1)}, u32[]{:S(2)}, u32[]{:S(2)}) %collective-permute-start.2) | collective-permute-done | bytes 245792 | tf_op jit(solution)/shard_map/ppermute | solution.py:268
  14.8 1.0 %collective-permute-start.3 = (f32[3,5,32,128]{3,2,1,0:T(8,128)S(1)}, f32[3,5,32,128]{3,2,1,0:T(8,128)S(1)}, u32[]{:S(2)}, u32[]{:S(2)}) collective-permute-start(f32[3,5,32,128]{3,2,1,0:T(8,128)S(1)} %shard_map.58.middle), channel_id=1, source_target_pairs={{0,5},{1,6},{2,7},{3,11},{4,12},{5,0},{6,1},{7,2},{8,13},{9,14},{1... | collective-permute-start | bytes 737288 | tf_op jit(solution)/shard_map/ppermute | solution.py:268
  15.8 0.8 %collective-permute-done.4.near = f32[41,32,128]{2,1,0:T(8,128)S(1)} collective-permute-done((f32[41,32,128]{2,1,0:T(8,128)S(1)}, f32[41,32,128]{2,1,0:T(8,128)S(1)}, u32[]{:S(2)}, u32[]{:S(2)}) %collective-permute-start.4) | collective-permute-done | bytes 671776 | tf_op jit(solution)/shard_map/ppermute | solution.py:268
  16.7 0.1 collective-permute-start.7
  16.8 0.6 %collective-permute-start.5 = (f32[10,32,128]{2,1,0:T(8,128)S(1)}, f32[10,32,128]{2,1,0:T(8,128)S(1)}, u32[]{:S(2)}, u32[]{:S(2)}) collective-permute-start(f32[10,32,128]{2,1,0:T(8,128)S(1)} %get-tuple-element.29), channel_id=1, source_target_pairs={{0,4},{1,5},{2,6},{3,7},{4,0},{5,1},{6,2},{7,3},{8,12},{9,13},{10,... | collective-permute-start | bytes 491528 | tf_op jit(solution)/shard_map/ppermute | solution.py:268
  17.3 0.1 collective-permute-start.6
  17.4 0.9 %collective-permute-done.5 = f32[10,32,128]{2,1,0:T(8,128)S(1)} collective-permute-done((f32[10,32,128]{2,1,0:T(8,128)S(1)}, f32[10,32,128]{2,1,0:T(8,128)S(1)}, u32[]{:S(2)}, u32[]{:S(2)}) %collective-permute-start.5) | collective-permute-done | bytes 163872 | tf_op jit(solution)/shard_map/ppermute | solution.py:268
  18.4 0.3 %collective-permute-done.6 = f32[10,32,128]{2,1,0:T(8,128)S(1)} collective-permute-done((f32[10,32,128]{2,1,0:T(8,128)S(1)}, f32[10,32,128]{2,1,0:T(8,128)S(1)}, u32[]{:S(2)}, u32[]{:S(2)}) %collective-permute-start.6) | collective-permute-done | bytes 163872 | tf_op jit(solution)/shard_map/ppermute | solution.py:268
  18.7 0.0 collective-permute-done.7
  18.8 0.0 copy-done
  18.8 0.0 copy-done.1
  18.8 0.5 %shard_map.59 = (f32[6,576,128]{2,1,0:T(8,128)S(1)}, f32[576,128]{1,0:T(8,128)S(1)}) custom-call(s32[1]{0:T(128)S(6)} %copy.8.row, f32[2,8,32,128]{3,2,1,0:T(8,128)S(1)} %get-tuple-element.19.pool, f32[3,8,32,128]{3,2,1,0:T(8,128)S(1)} %copy-done, f32[8,32,128]{2,1,0:T(8,128)S(1)} %copy-done.1, f32[41,32,128]{2,1,0:T(8,128)S(1)} %collective-permute-done.4.near, ...), custom_call_target="tpu_custom_call" | custom-call | tf_op jit(solution)/shard_map/pallas_call | solution.py:315
  19.3 1.2 %collective-permute-done.3.halo = f32[3,5,32,128]{3,2,1,0:T(8,128)S(1)} collective-permute-done((f32[3,5,32,128]{3,2,1,0:T(8,128)S(1)}, f32[3,5,32,128]{3,2,1,0:T(8,128)S(1)}, u32[]{:S(2)}, u32[]{:S(2)}) %collective-permute-start.3) | collective-permute-done | bytes 245792 | tf_op jit(solution)/shard_map/ppermute | solution.py:268
  20.6 0.1 collective-permute-start.8
  20.6 1.1 %shard_map.60.level = f32[4,3,320,128]{3,2,1,0:T(8,128)S(1)} custom-call(f32[6,576,128]{2,1,0:T(8,128)S(1)} %get-tuple-element.26.coef, f32[576,128]{1,0:T(8,128)S(1)} %get-tuple-element.27.scaled, f32[3,5,32,128]{3,2,1,0:T(8,128)S(1)} %shard_map.58.middle, f32[3,5,32,128]{3,2,1,0:T(8,128)S(1)} %collective-permute-done.3.halo), custom_call_target="tpu_custom_call" | custom-call | tf_op jit(solution)/shard_map/pallas_call | solution.py:334
  21.7 0.6 %collective-permute-done.8.sibling = f32[3,8,32,128]{3,2,1,0:T(8,128)S(1)} collective-permute-done((f32[3,8,32,128]{3,2,1,0:T(8,128)S(1)}, f32[3,8,32,128]{3,2,1,0:T(8,128)S(1)}, u32[]{:S(2)}, u32[]{:S(2)}) %collective-permute-start.8) | collective-permute-done | bytes 393248 | tf_op jit(solution)/shard_map/ppermute | solution.py:268
  22.4 2.6 %shard_map.61 = f32[1,8,32,128]{3,2,1,0:T(8,128)} custom-call(f32[6,576,128]{2,1,0:T(8,128)S(1)} %get-tuple-element.26.coef, f32[576,128]{1,0:T(8,128)S(1)} %get-tuple-element.27.scaled, f32[3,5,32,128]{3,2,1,0:T(8,128)S(1)} %shard_map.58.middle, f32[3,5,32,128]{3,2,1,0:T(8,128)S(1)} %collective-permute-done.3.halo, ...), custom_call_target="tpu_custom_call" | custom-call | tf_op jit(solution)/shard_map/pallas_call | solution.py:341
  (7 shorter events, 0.2 us)
Async XLA Ops:
  0.0 1.8 %collective-permute-start = (f32[2,8,32,128]{3,2,1,0:T(8,128)}, f32[2,8,32,128]{3,2,1,0:T(8,128)S(1)}, u32[]{:S(2)}, u32[]{:S(2)}) collective-permute-start(f32[2,8,32,128]{3,2,1,0:T(8,128)} %pool_hbm.1), channel_id=1, source_target_pairs={{0,4},{1,5},{2,6},{3,7},{4,0},{5,1},{6,2},{7,3},{8,12},{9,13},{10,... | collective-permute-start | bytes 786440 | tf_op jit(solution)/shard_map/ppermute | solution.py:268
  1.9 6.6 %collective-permute-start.1 = (f32[3,5,32,128]{3,2,1,0:T(8,128)S(1)}, f32[3,5,32,128]{3,2,1,0:T(8,128)S(1)}, u32[]{:S(2)}, u32[]{:S(2)}) collective-permute-start(f32[3,5,32,128]{3,2,1,0:T(8,128)S(1)} %get-tuple-element.22), channel_id=1, source_target_pairs={{0,12},{1,13},{2,14},{3,15},{4,16},{5,17},{6,18},{7,19},{8,4},{9,5... | collective-permute-start | bytes 737288 | tf_op jit(solution)/shard_map/ppermute | solution.py:268
  4.6 12.1 %collective-permute-start.4 = (f32[41,32,128]{2,1,0:T(8,128)S(1)}, f32[41,32,128]{2,1,0:T(8,128)S(1)}, u32[]{:S(2)}, u32[]{:S(2)}) collective-permute-start(f32[41,32,128]{2,1,0:T(8,128)S(1)} %get-tuple-element.23), channel_id=1, source_target_pairs={{0,5},{1,6},{2,7},{5,0},{6,1},{7,2},{8,13},{9,14},{10,15},{13,8},{... | collective-permute-start | bytes 2015240 | tf_op jit(solution)/shard_map/ppermute | solution.py:268
  8.5 10.3 %copy-start = (f32[3,8,32,128]{3,2,1,0:T(8,128)S(1)}, f32[3,8,32,128]{3,2,1,0:T(8,128)}, u32[]{:S(2)}) copy-start(f32[3,8,32,128]{3,2,1,0:T(8,128)} %metric.1) | copy-start | bytes 1179652
  8.5 10.2 %copy-start.1 = (f32[8,32,128]{2,1,0:T(8,128)S(1)}, f32[8,32,128]{2,1,0:T(8,128)}, u32[]{:S(2)}) copy-start(f32[8,32,128]{2,1,0:T(8,128)} %screening.1) | copy-start | bytes 393220
  8.5 6.3 %collective-permute-start.2 = (f32[3,5,32,128]{3,2,1,0:T(8,128)S(1)}, f32[3,5,32,128]{3,2,1,0:T(8,128)S(1)}, u32[]{:S(2)}, u32[]{:S(2)}) collective-permute-start(f32[3,5,32,128]{3,2,1,0:T(8,128)S(1)} %shard_map.57.mine), channel_id=1, source_target_pairs={{0,8},{1,9},{2,10},{3,11},{4,20},{5,21},{6,22},{7,23},{8,0},{9,1},... | collective-permute-start | bytes 737288 | tf_op jit(solution)/shard_map/ppermute | solution.py:268
  14.8 5.7 %collective-permute-start.3 = (f32[3,5,32,128]{3,2,1,0:T(8,128)S(1)}, f32[3,5,32,128]{3,2,1,0:T(8,128)S(1)}, u32[]{:S(2)}, u32[]{:S(2)}) collective-permute-start(f32[3,5,32,128]{3,2,1,0:T(8,128)S(1)} %shard_map.58.middle), channel_id=1, source_target_pairs={{0,5},{1,6},{2,7},{3,11},{4,12},{5,0},{6,1},{7,2},{8,13},{9,14},{1... | collective-permute-start | bytes 737288 | tf_op jit(solution)/shard_map/ppermute | solution.py:268
  16.7 2.1 %collective-permute-start.7 = (f32[11,32,128]{2,1,0:T(8,128)S(1)}, f32[11,32,128]{2,1,0:T(8,128)S(1)}, u32[]{:S(2)}, u32[]{:S(2)}) collective-permute-start(f32[11,32,128]{2,1,0:T(8,128)S(1)} %slice.22), channel_id=1, source_target_pairs={{0,4},{1,5},{2,6},{3,7},{4,0},{5,1},{6,2},{7,3},{8,12},{9,13},{10,... | collective-permute-start | bytes 540680 | tf_op jit(solution)/shard_map/ppermute | solution.py:268
  16.8 1.6 %collective-permute-start.5 = (f32[10,32,128]{2,1,0:T(8,128)S(1)}, f32[10,32,128]{2,1,0:T(8,128)S(1)}, u32[]{:S(2)}, u32[]{:S(2)}) collective-permute-start(f32[10,32,128]{2,1,0:T(8,128)S(1)} %get-tuple-element.29), channel_id=1, source_target_pairs={{0,4},{1,5},{2,6},{3,7},{4,0},{5,1},{6,2},{7,3},{8,12},{9,13},{10,... | collective-permute-start | bytes 491528 | tf_op jit(solution)/shard_map/ppermute | solution.py:268
  17.3 1.4 %collective-permute-start.6 = (f32[10,32,128]{2,1,0:T(8,128)S(1)}, f32[10,32,128]{2,1,0:T(8,128)S(1)}, u32[]{:S(2)}, u32[]{:S(2)}) collective-permute-start(f32[10,32,128]{2,1,0:T(8,128)S(1)} %get-tuple-element.30), channel_id=1, source_target_pairs={{0,4},{1,5},{2,6},{3,7},{4,0},{5,1},{6,2},{7,3},{8,12},{9,13},{10,... | collective-permute-start | bytes 491528 | tf_op jit(solution)/shard_map/ppermute | solution.py:268
  20.6 1.8 %collective-permute-start.8 = (f32[3,8,32,128]{3,2,1,0:T(8,128)S(1)}, f32[3,8,32,128]{3,2,1,0:T(8,128)S(1)}, u32[]{:S(2)}, u32[]{:S(2)}) collective-permute-start(f32[3,8,32,128]{3,2,1,0:T(8,128)S(1)} %maximum_select_fusion), channel_id=1, source_target_pairs={{0,4},{1,5},{2,6},{3,7},{4,0},{5,1},{6,2},{7,3},{8,12},{9,13},{10,... | collective-permute-start | bytes 1179656 | tf_op jit(solution)/shard_map/ppermute | solution.py:268

commit v7 on v6

v7 whole, which is shorter than its diff:
```python
import functools
import math

import jax
import jax.numpy as jnp
from jax import lax
from jax.experimental import pallas as pl
from jax.experimental.pallas import tpu as pltpu
from jax.sharding import PartitionSpec as P

NSRC = 3
SWEEPS = 6
HALO = SWEEPS - 1
AXES = ("orb", "slab")
HINT = 10**10
PIECES = 4
VMEM = pl.BlockSpec(memory_space=pltpu.VMEM)
SMEM = pl.BlockSpec(memory_space=pltpu.SMEM)
HBM = pl.BlockSpec(memory_space=pltpu.HBM)


def step_sizes(count):
    return [
        1.0 / (1.025 + 0.975 * math.cos(math.pi * (2 * k + 1) / (2 * count))) for k in range(count)
    ]


def upper_side():
    return 1 - lax.rem(lax.axis_index("orb"), 2)


def call(kernel, out_shapes, in_specs, scratch=(), flops=0, moved=0, alias=None):
    return pl.pallas_call(
        kernel,
        out_shape=[jax.ShapeDtypeStruct(s, jnp.float32) for s in out_shapes],
        in_specs=in_specs,
        out_specs=[VMEM] * len(out_shapes),
        scratch_shapes=list(scratch),
        compiler_params=pltpu.CompilerParams(vmem_limit_bytes=16 << 20),
        input_output_aliases=alias or {},
        cost_estimate=pl.CostEstimate(flops=flops, transcendentals=0, bytes_accessed=moved),
    )


def pick_kernel(
    index_hbm, pool_hbm, metric_hbm, screening_hbm, own, edge, pick, pool, index, screen, face, sems
):
    h = HALO
    held, planes, gx, gy = pool.shape
    orb = lax.axis_index("orb")
    side = upper_side()
    sibling = orb - 1 + 2 * side
    mine = side * (planes - h)
    parts = [
        (index_hbm, index),
        (pool_hbm, pool),
        (screening_hbm.at[pl.ds(mine, h)], screen),
        (metric_hbm.at[0, pl.ds(mine, h)], face.at[0, pl.ds(1, h)]),
        (metric_hbm.at[1, pl.ds(mine, h)], face.at[1, pl.ds(1, h)]),
        (
            metric_hbm.at[2, pl.ds(side * (planes - h - 1), h + 1)],
            face.at[2, pl.ds(1 - side, h + 1)],
        ),
    ]
    copies = [pltpu.make_async_copy(a, b, sems.at[i]) for i, (a, b) in enumerate(parts)]
    for copy in copies:
        copy.start()
    for copy in copies[:2]:
        copy.wait()
    for s in range(NSRC):
        group, place = index[s] // held, lax.rem(index[s], held)
        own[s] = jnp.where(group == orb, pool[place], 0.0)
        for r in range(held):
            there = jnp.logical_and(group == sibling, place == r)
            pick[s, r] = jnp.where(there, jnp.ones(pick.shape[2:], jnp.float32), 0.0)
    rest = (edge.shape[0] - 4 * h + 2,) + edge.shape[1:]
    edge[pl.ds(4 * h - 2, rest[0])] = jnp.zeros(rest, jnp.float32)
    for copy in copies[2:]:
        copy.wait()
    x_id = lax.broadcasted_iota(jnp.int32, (gx, gy), 0)
    y_id = lax.broadcasted_iota(jnp.int32, (gx, gy), 1)
    for i in range(h):
        x_hi, y_hi, z_hi = face[0, i + 1], face[1, i + 1], face[2, i + 1]
        z_lo = face[2, i] if i else jnp.where(side == 0, 0.0, face[2, i])
        x_lo = jnp.where(x_id == 0, 0.0, pltpu.roll(x_hi, 1, 0))
        y_lo = jnp.where(y_id == 0, 0.0, pltpu.roll(y_hi, 1, 1))
        edge[i] = screen[i] + z_hi + z_lo + x_hi + x_lo + y_hi + y_lo
        edge[h + i] = z_hi
    edge[2 * h : 3 * h - 1] = face[0, pl.ds(1 + side, h - 1)]
    edge[3 * h - 1 : 4 * h - 2] = face[1, pl.ds(1 + side, h - 1)]


def gather_kernel(own, pick, pool, theirs, blank, keep, send, edge):
    del blank
    h = HALO
    held, planes, gx = pool.shape[:3]
    side = upper_side()
    mine = side * (planes - h)
    for part, start in ((send, (1 - side) * (planes - h)), (keep, mine)):
        for s in range(NSRC):
            total = own[s, pl.ds(start, h)]
            for r in range(held):
                factor = jnp.tile(pick[s, r], (gx // pick.shape[2], 1))
                total += factor * theirs[r, pl.ds(start, h)]
            part[s] = total
    for r in range(held):
        edge[pl.ds((4 + r) * h - 2, h)] = pool[r, pl.ds(mine, h)]
        edge[pl.ds((4 + held + r) * h - 2, h)] = theirs[r, pl.ds(mine, h)]


def merge_kernel(mine, theirs, both):
    both[...] = mine[...] + theirs[...]


def coefficient_kernel(
    row, pool, metric, screening, near, far, coef, scaled, fx, fy, fz, scr, tgt
):
    side = upper_side()
    slab, slabs = lax.axis_index("slab"), lax.axis_size("slab")
    planes, gx, gy = screening.shape
    total = planes + 2 * HALO
    lower = side * (HALO + planes)
    upper = (1 - side) * (HALO + planes)
    h = HALO
    held = pool.shape[0]
    near_row = (4 + held + row[0]) * h - 2
    far_row = (4 + row[0]) * h - 2
    blank = jnp.zeros((gx, gy), jnp.float32)
    for e in (0, total - 1):
        fx[e] = blank
        fy[e] = blank
    fz[0] = blank
    for halo, at, inner, above, own_slot in (
        (near, lower, lower + 1 - side, lower + 1, near_row),
        (far, upper, upper + side, upper + 1, far_row),
    ):
        scr[pl.ds(at, h)] = halo[0:h]
        fz[pl.ds(above, h)] = halo[h : 2 * h]
        fx[pl.ds(inner, h - 1)] = halo[2 * h : 3 * h - 1]
        fy[pl.ds(inner, h - 1)] = halo[3 * h - 1 : 4 * h - 2]
        tgt[pl.ds(at, h)] = halo[pl.ds(own_slot, h)]
    fz[h + 1 : h + 1 + planes] = metric[2]
    scr[h : h + planes] = screening[...]
    fx[h : h + planes] = metric[0]
    fy[h : h + planes] = metric[1]
    tgt[h : h + planes] = pool[row[0]]
    first = jnp.where(slab == 0, h, 0)
    last = jnp.where(slab == slabs - 1, h + planes, total)
    x_id = lax.broadcasted_iota(jnp.int32, (gx, gy), 0)
    y_id = lax.broadcasted_iota(jnp.int32, (gx, gy), 1)

    @pl.loop(0, total, unroll=6)
    def _(e):
        z_hi, z_lo = fz[e + 1], fz[e]
        x_hi, y_hi = fx[e], fy[e]
        x_lo = jnp.where(x_id == 0, 0.0, pltpu.roll(x_hi, 1, 0))
        y_lo = jnp.where(y_id == 0, 0.0, pltpu.roll(y_hi, 1, 1))
        here = jnp.logical_and(e >= h, e < h + planes)
        rest = jnp.where(e == h + planes, z_lo, 0.0)
        diag = scr[e] + jnp.where(here, z_hi + z_lo + x_hi + x_lo + y_hi + y_lo, rest)
        inside = jnp.logical_and(e >= first, e < last)
        inverse = 1.0 / jnp.where(inside, diag, 1.0)
        inverse = jnp.where(inside, inverse, 0.0)
        rows = pl.ds(pl.multiple_of(e * gx, gx), gx)
        coef[0, rows] = z_hi * inverse
        coef[1, rows] = z_lo * inverse
        coef[2, rows] = jnp.where(x_id == gx - 1, 0.0, x_hi * inverse)
        coef[3, rows] = x_lo * inverse
        coef[4, rows] = jnp.where(y_id == gy - 1, 0.0, y_hi * inverse)
        coef[5, rows] = y_lo * inverse
        scaled[rows] = tgt[e] * inverse


SOURCE, DENSITY, START = 0, 1, 2


def take_planes(weight, scaled, state, part, at):
    count, gx, gy = part.shape[1:]
    for i in range(count):
        rows = pl.ds(pl.multiple_of((at + i) * gx, gx), gx)
        t = scaled[rows]
        for s in range(NSRC):
            cells = part[s, i]
            b = t * cells
            state[SOURCE, s, rows] = cells
            state[DENSITY, s, rows] = b
            state[START, s, rows] = weight * b


def sweep_planes(k, weight, coef, state, begin, count, gx, out=None, shift=0):
    gy = state.shape[-1]
    old = START + k - 1

    @pl.loop(0, count, unroll=count)
    def _(i):
        for j in range(0, gx, 8):
            at = pl.multiple_of((begin + i) * gx, gx) + j
            here = pl.ds(at, 8)
            c = [coef[n, here] for n in range(6)]
            acc = None
            for s in range(NSRC):
                v = state[old, s, here]
                total = state[DENSITY, s, here]
                total += c[0] * state[old, s, pl.ds(at + gx, 8)]
                total += c[1] * state[old, s, pl.ds(at - gx, 8)]
                total += c[2] * state[old, s, pl.ds(at + 1, 8)]
                total += c[3] * state[old, s, pl.ds(at - 1, 8)]
                total += c[4] * pltpu.roll(v, gy - 1, 1)
                total += c[5] * pltpu.roll(v, 1, 1)
                v = (1.0 - weight) * v + weight * total
                if out is None:
                    state[old + 1, s, here] = v
                else:
                    term = v * state[SOURCE, s, here]
                    acc = term if acc is None else acc + term
            if out is not None:
                out[begin + i - shift, j : j + 8] = acc


def inner_kernel(weights, coef, scaled, middle, inner, state):
    side = upper_side()
    h = HALO
    gx = middle.shape[2]
    extra, rest = middle.shape[1], inner.shape[1]
    planes = extra + rest
    take_planes(weights[0], scaled, state, middle, h + side * rest)
    take_planes(weights[0], scaled, state, inner, h + (1 - side) * extra)
    for k in range(1, SWEEPS):
        if planes > 2 * k:
            sweep_planes(k, weights[k], coef, state, h + k, planes - 2 * k, gx)


def near_kernel(weights, coef, scaled, halo, known, state, early):
    del known
    side = upper_side()
    h = HALO
    gx = halo.shape[2]
    total = state.shape[2] // gx
    planes = total - 2 * h
    take_planes(weights[0], scaled, state, halo, side * (h + planes))
    for k in range(1, SWEEPS):
        count = min(h, h + planes - 2 * k)
        begin = jnp.where(side == 0, k, total - k - count)
        if k < SWEEPS - 1:
            sweep_planes(k, weights[k], coef, state, begin, count, gx)
        else:
            sweep_planes(k, weights[k], coef, state, begin, count, gx, early, begin)


def far_kernel(weights, coef, scaled, halo, known, early, state, out):
    del known
    side = upper_side()
    h = HALO
    gx = halo.shape[2]
    planes = out.shape[1]
    total = planes + 2 * h
    take_planes(weights[0], scaled, state, halo, (1 - side) * (h + planes))
    for k in range(1, SWEEPS):
        begin = jnp.where(side == 0, h + planes - k, k)
        if k < SWEEPS - 1:
            sweep_planes(k, weights[k], coef, state, begin, h, gx)
        else:
            sweep_planes(k, weights[k], coef, state, begin, h, gx, out.at[0], h)
    done = early.shape[0]
    out[0, pl.ds(side * (planes - done), done)] = early[...]


def shards(pool, target_row, source_index, metric, screening):
    held, planes, gx, gy = pool.shape
    n_orb, n_slab = lax.axis_size("orb"), lax.axis_size("slab")
    h = HALO
    weights = step_sizes(SWEEPS)
    side = upper_side()

    def place(o, z):
        return o * n_slab + z

    def among(moved):
        pairs = [
            (place(o, z), place(*moved(o, z)))
            for o in range(n_orb)
            for z in range(n_slab)
            if 0 <= moved(o, z)[1] < n_slab
        ]
        return lambda x: lax.ppermute(x, AXES, pairs)

    to_sibling = among(lambda o, z: (o ^ 1, z))
    to_slab = among(lambda o, z: (o ^ 1, z - 1 if o % 2 else z + 1))

    def next_slab(o, z):
        there = z - 1 if o % 2 else z + 1
        return (o ^ 1, there) if 0 <= there < n_slab else (o ^ 2, z)

    to_slab_all = among(next_slab)
    bits = [1 << b for b in range(1, n_orb.bit_length() - 1)]

    theirs = to_sibling(pool)
    own, edge, pick, pool_here = call(
        pick_kernel,
        [
            (NSRC,) + pool.shape[1:],
            ((4 + 2 * held) * h - 2, gx, gy),
            (NSRC, held, 8, gy),
            pool.shape,
        ],
        [HBM] * 4,
        [
            pltpu.SMEM(source_index.shape, jnp.int32),
            pltpu.VMEM((h, gx, gy), jnp.float32),
            pltpu.VMEM((3, h + 2, gx, gy), jnp.float32),
            pltpu.SemaphoreType.DMA((6,)),
        ],
        moved=4 << 20,
    )(*[
        pltpu.with_memory_space_constraint(x, pltpu.HBM)
        for x in (source_index, pool, metric, screening)
    ])
    keep, send, edge = call(
        gather_kernel,
        [(NSRC, h, gx, gy)] * 2 + [edge.shape],
        [VMEM] * 5,
        alias={4: 2},
    )(own, pick, pool_here, theirs, edge)
    near = to_slab(edge)
    part = keep
    for step in range(len(bits)):
        low, high = (bits[0], bits[-1]) if step == 0 else (bits[-1 - step], bits[step])
        swap = 1 if step == 0 else 0
        across = among(lambda o, z: (o ^ swap ^ (high if o % 2 else low), z))
        merge = call(merge_kernel, [part.shape], [VMEM] * 2, flops=0 if step else HINT)
        (part,) = merge(part, across(send if step == 0 else part))
    halo = to_slab_all(part)
    last = (4 + held) * h - 2
    cuts = [last * i // PIECES for i in range(PIECES + 1)]
    far = jnp.concatenate([to_sibling(near[a:b]) for a, b in zip(cuts, cuts[1:])], axis=0)
    total = planes + 2 * h
    coef, scaled = call(
        coefficient_kernel,
        [(6, total * gx, gy), (total * gx, gy)],
        [SMEM] + [VMEM] * 5,
        [pltpu.VMEM((total, gx, gy), jnp.float32)] * 2
        + [pltpu.VMEM((total + 1, gx, gy), jnp.float32)]
        + [pltpu.VMEM((total, gx, gy), jnp.float32)] * 2,
        moved=0,
    )(target_row, pool_here, metric, screening, near, far)
    rest = planes - h
    inner = to_sibling(lax.dynamic_slice_in_dim(part, side * (h - rest), rest, axis=1))
    (state,) = call(
        functools.partial(inner_kernel, weights),
        [(START + SWEEPS - 1, NSRC, total * gx, gy)],
        [VMEM] * 4,
    )(coef, scaled, part, inner)
    halo, state, coef, scaled = lax.optimization_barrier((halo, state, coef, scaled))
    state, early = call(
        functools.partial(near_kernel, weights),
        [state.shape, (rest, gx, gy)],
        [VMEM] * 4,
        alias={3: 0},
    )(coef, scaled, halo, state)
    state, out = call(
        functools.partial(far_kernel, weights),
        [state.shape, (1, planes, gx, gy)],
        [VMEM] * 5,
        alias={3: 0},
    )(coef, scaled, to_sibling(halo), state, early)
    return out


def solution(mesh):
    in_specs = (
        P("orb", "slab", None, None),
        P("orb"),
        P(),
        P(None, "slab", None, None),
        P("slab", None, None),
    )
    out_specs = P("orb", "slab", None, None)
    return jax.shard_map(shards, mesh=mesh, in_specs=in_specs, out_specs=out_specs, check_vma=False)
```

time: 25.1 us -> 23.9 us (0.952)
  waiting for transfers between devices: 8.15 us -> 6.88 us
  starting transfers between devices: 10.4 us -> 10.9 us
  Pallas kernels: 5.49 us -> 5.11 us
    ppermute x9 -> x11, waiting for transfers between devices: 8.15 us -> 6.88 us  [among(): return lambda x: lax.ppermute(x, AXES, pairs)]
    ppermute x9 -> x11, starting transfers between devices: 10.4 us -> 10.9 us  [among(): return lambda x: lax.ppermute(x, AXES, pairs)]
    pallas_call x3 -> x4, Pallas kernels: 4.84 us -> 4.46 us  [the longest x1 1.7 us: shards(): call(functools.partial(far_kernel, weights), [state.shape, (1, planes, gx...]
  transfers between devices with their start and end apart: 9 -> 11, of which waited for: 8 -> 7; matrix products, arithmetic and copies ran while one was open for 0% -> 0% of each run, Pallas kernels for 11% -> 14%
where the time goes in v7:
time: 23.9 us; the launch traced here: 23.7 us
  starting transfers between devices  10.9 us (46%)
  waiting for transfers between devices  6.88 us (29%)
  Pallas kernels  5.11 us (21%)
  between operations  0.78 us (3%)
    ppermute x11, starting transfers between devices, among(): return lambda x: lax.ppermute(x, AXES, pairs)  10.9 us
    ppermute x11, waiting for transfers between devices, among(): return lambda x: lax.ppermute(x, AXES, pairs)  6.88 us
    pallas_call x1, Pallas kernels, shards(): call(functools.partial(far_kernel, weights), [state.shape, (1, planes, gx...  1.7 us
    pallas_call x1, Pallas kernels, shards(): call(pick_kernel, [(NSRC,) + pool.shape[1:], ((4 + 2 * held) * h - 2, gx,...  1.24 us
    pallas_call x1, Pallas kernels, shards(): call(functools.partial(near_kernel, weights), [state.shape, (rest, gx, gy...  1.01 us
    pallas_call x1, Pallas kernels, shards(): call(functools.partial(inner_kernel, weights), [(START + SWEEPS - 1, NSRC...  0.51 us
    pallas_call x1, Pallas kernels, shards(): call(coefficient_kernel, [(6, total * gx, gy), (total * gx, gy)], [SMEM]...  0.51 us
  transfers between devices with their start and end apart: 11, of which 7 were waited for; matrix products, arithmetic and copies ran while one was open for 0% of the time, Pallas kernels for 14%

profile of v7, /device:TPU:0, one launch (start us, length us, event | category | flops | bytes accessed | tf_op | source)
XLA Modules:
  0.0 23.7 jit_solution(7051298824487407883)
XLA Ops:
  0.0 0.5 %collective-permute-start = (f32[2,8,32,128]{3,2,1,0:T(8,128)}, f32[2,8,32,128]{3,2,1,0:T(8,128)S(1)}, u32[]{:S(2)}, u32[]{:S(2)}) collective-permute-start(f32[2,8,32,128]{3,2,1,0:T(8,128)} %pool_hbm.1), channel_id=1, source_target_pairs={{0,4},{1,5},{2,6},{3,7},{4,0},{5,1},{6,2},{7,3},{8,12},{9,13},{10,... | collective-permute-start | bytes 786440 | tf_op jit(solution)/shard_map/ppermute | solution.py:285
  0.5 1.2 %shard_map.55 = (f32[3,8,32,128]{3,2,1,0:T(8,128)S(1)}, f32[38,32,128]{2,1,0:T(8,128)S(1)}, f32[3,2,8,128]{3,2,1,0:T(8,128)S(1)}, f32[2,8,32,128]{3,2,1,0:T(8,128)S(1)}) custom-call(s32[3]{0:T(128)} %index_hbm.1, f32[2,8,32,128]{3,2,1,0:T(8,128)} %pool_hbm.1, f32[3,8,32,128]{3,2,1,0:T(8,128)} %metric.1, f32[8,32,128]{2,1,0:T(8,128)} %screening.1), custom_call_target="tpu_custom_call" | custom-call | bytes 4194304 | tf_op jit(solution)/shard_map/pallas_call | solution.py:298
  1.7 0.1 collective-permute-done.theirs
  1.8 0.1 shard_map.56
  1.9 2.7 %collective-permute-start.1 = (f32[3,5,32,128]{3,2,1,0:T(8,128)S(1)}, f32[3,5,32,128]{3,2,1,0:T(8,128)S(1)}, u32[]{:S(2)}, u32[]{:S(2)}) collective-permute-start(f32[3,5,32,128]{3,2,1,0:T(8,128)S(1)} %get-tuple-element.26), channel_id=1, source_target_pairs={{0,12},{1,13},{2,14},{3,15},{4,16},{5,17},{6,18},{7,19},{8,4},{9,5... | collective-permute-start | bytes 737288 | tf_op jit(solution)/shard_map/ppermute | solution.py:285
  4.6 3.5 %collective-permute-start.4 = (f32[38,32,128]{2,1,0:T(8,128)S(1)}, f32[38,32,128]{2,1,0:T(8,128)S(1)}, u32[]{:S(2)}, u32[]{:S(2)}) collective-permute-start(f32[38,32,128]{2,1,0:T(8,128)S(1)} %get-tuple-element.27), channel_id=1, source_target_pairs={{0,5},{1,6},{2,7},{5,0},{6,1},{7,2},{8,13},{9,14},{10,15},{13,8},{... | collective-permute-start | bytes 1867784 | tf_op jit(solution)/shard_map/ppermute | solution.py:285
  8.1 0.4 %collective-permute-done.1.theirs = f32[3,5,32,128]{3,2,1,0:T(8,128)S(1)} collective-permute-done((f32[3,5,32,128]{3,2,1,0:T(8,128)S(1)}, f32[3,5,32,128]{3,2,1,0:T(8,128)S(1)}, u32[]{:S(2)}, u32[]{:S(2)}) %collective-permute-start.1) | collective-permute-done | bytes 245792 | tf_op jit(solution)/shard_map/ppermute | solution.py:285
  8.5 0.0 copy-start
  8.5 0.0 copy-start.1
  8.5 2.0 %collective-permute-start.2 = (f32[3,5,32,128]{3,2,1,0:T(8,128)S(1)}, f32[3,5,32,128]{3,2,1,0:T(8,128)S(1)}, u32[]{:S(2)}, u32[]{:S(2)}) collective-permute-start(f32[3,5,32,128]{3,2,1,0:T(8,128)S(1)} %shard_map.57.mine), channel_id=1, source_target_pairs={{0,8},{1,9},{2,10},{3,11},{4,20},{5,21},{6,22},{7,23},{8,0},{9,1},... | collective-permute-start | bytes 737288 | tf_op jit(solution)/shard_map/ppermute | solution.py:285
  10.6 4.2 %collective-permute-done.2.theirs = f32[3,5,32,128]{3,2,1,0:T(8,128)S(1)} collective-permute-done((f32[3,5,32,128]{3,2,1,0:T(8,128)S(1)}, f32[3,5,32,128]{3,2,1,0:T(8,128)S(1)}, u32[]{:S(2)}, u32[]{:S(2)}) %collective-permute-start.2) | collective-permute-done | bytes 245792 | tf_op jit(solution)/shard_map/ppermute | solution.py:285
  14.8 1.0 %collective-permute-start.3 = (f32[3,5,32,128]{3,2,1,0:T(8,128)S(1)}, f32[3,5,32,128]{3,2,1,0:T(8,128)S(1)}, u32[]{:S(2)}, u32[]{:S(2)}) collective-permute-start(f32[3,5,32,128]{3,2,1,0:T(8,128)S(1)} %shard_map.58.middle), channel_id=1, source_target_pairs={{0,5},{1,6},{2,7},{3,11},{4,12},{5,0},{6,1},{7,2},{8,13},{9,14},{1... | collective-permute-start | bytes 737288 | tf_op jit(solution)/shard_map/ppermute | solution.py:285
  15.8 0.3 %collective-permute-done.4.near = f32[38,32,128]{2,1,0:T(8,128)S(1)} collective-permute-done((f32[38,32,128]{2,1,0:T(8,128)S(1)}, f32[38,32,128]{2,1,0:T(8,128)S(1)}, u32[]{:S(2)}, u32[]{:S(2)}) %collective-permute-start.4) | collective-permute-done | bytes 622624 | tf_op jit(solution)/shard_map/ppermute | solution.py:285
  16.2 0.1 collective-permute-start.5
  16.2 0.5 %collective-permute-start.8 = (f32[7,32,128]{2,1,0:T(8,128)S(1)}, f32[7,32,128]{2,1,0:T(8,128)S(1)}, u32[]{:S(2)}, u32[]{:S(2)}) collective-permute-start(f32[7,32,128]{2,1,0:T(8,128)S(1)} %get-tuple-element.38), channel_id=1, source_target_pairs={{0,4},{1,5},{2,6},{3,7},{4,0},{5,1},{6,2},{7,3},{8,12},{9,13},{10,... | collective-permute-start | bytes 344072 | tf_op jit(solution)/shard_map/ppermute | solution.py:285
  16.7 0.1 collective-permute-start.7
  16.8 0.4 %collective-permute-start.6 = (f32[7,32,128]{2,1,0:T(8,128)S(1)}, f32[7,32,128]{2,1,0:T(8,128)S(1)}, u32[]{:S(2)}, u32[]{:S(2)}) collective-permute-start(f32[7,32,128]{2,1,0:T(8,128)S(1)} %get-tuple-element.40), channel_id=1, source_target_pairs={{0,4},{1,5},{2,6},{3,7},{4,0},{5,1},{6,2},{7,3},{8,12},{9,13},{10,... | collective-permute-start | bytes 344072 | tf_op jit(solution)/shard_map/ppermute | solution.py:285
  17.3 0.3 %collective-permute-done.5 = f32[7,32,128]{2,1,0:T(8,128)S(1)} collective-permute-done((f32[7,32,128]{2,1,0:T(8,128)S(1)}, f32[7,32,128]{2,1,0:T(8,128)S(1)}, u32[]{:S(2)}, u32[]{:S(2)}) %collective-permute-start.5) | collective-permute-done | bytes 114720 | tf_op jit(solution)/shard_map/ppermute | solution.py:285
  17.5 0.2 collective-permute-start.9
  18.3 0.0 collective-permute-done.8
  18.4 0.0 collective-permute-done.7
  18.4 0.0 collective-permute-done.6
  18.4 0.0 copy-done
  18.4 0.0 copy-done.1
  18.4 0.5 %shard_map.59 = (f32[6,576,128]{2,1,0:T(8,128)S(1)}, f32[576,128]{1,0:T(8,128)S(1)}) custom-call(s32[1]{0:T(128)S(6)} %copy.12.row, f32[2,8,32,128]{3,2,1,0:T(8,128)S(1)} %get-tuple-element.23.pool, f32[3,8,32,128]{3,2,1,0:T(8,128)S(1)} %copy-done, f32[8,32,128]{2,1,0:T(8,128)S(1)} %copy-done.1, f32[38,32,128]{2,1,0:T(8,128)S(1)} %collective-permute-done.4.near, ...), custom_call_target="tpu_custom_call" | custom-call | tf_op jit(solution)/shard_map/pallas_call | solution.py:337
  19.0 0.0 collective-permute-done.9.inner
  19.0 0.5 %shard_map.60.known = f32[7,3,576,128]{3,2,1,0:T(8,128)S(1)} custom-call(f32[6,576,128]{2,1,0:T(8,128)S(1)} %get-tuple-element.30.coef, f32[576,128]{1,0:T(8,128)S(1)} %get-tuple-element.31.scaled, f32[3,5,32,128]{3,2,1,0:T(8,128)S(1)} %shard_map.58.middle, f32[3,3,32,128]{3,2,1,0:T(8,128)S(1)} %collective-permute-done.9.inner), custom_call_target="tpu_custom_call" | custom-call | tf_op jit(solution)/shard_map/pallas_call | solution.py:348
  19.5 1.0 %collective-permute-done.3.halo = f32[3,5,32,128]{3,2,1,0:T(8,128)S(1)} collective-permute-done((f32[3,5,32,128]{3,2,1,0:T(8,128)S(1)}, f32[3,5,32,128]{3,2,1,0:T(8,128)S(1)}, u32[]{:S(2)}, u32[]{:S(2)}) %collective-permute-start.3) | collective-permute-done | bytes 245792 | tf_op jit(solution)/shard_map/ppermute | solution.py:285
  20.5 0.0 collective-permute-start.10
  20.5 1.0 %shard_map.61 = (f32[7,3,576,128]{3,2,1,0:T(8,128)S(1)}, f32[3,32,128]{2,1,0:T(8,128)S(1)}) custom-call(f32[6,576,128]{2,1,0:T(8,128)S(1)} %get-tuple-element.30.coef, f32[576,128]{1,0:T(8,128)S(1)} %get-tuple-element.31.scaled, f32[3,5,32,128]{3,2,1,0:T(8,128)S(1)} %collective-permute-done.3.halo, ...), custom_call_target="tpu_custom_call", output_to_operand_aliasing={{0}: (3, {})} | custom-call | tf_op jit(solution)/shard_map/pallas_call | solution.py:354
  21.5 0.5 %collective-permute-done.10.halo = f32[3,5,32,128]{3,2,1,0:T(8,128)S(1)} collective-permute-done((f32[3,5,32,128]{3,2,1,0:T(8,128)S(1)}, f32[3,5,32,128]{3,2,1,0:T(8,128)S(1)}, u32[]{:S(2)}, u32[]{:S(2)}) %collective-permute-start.10) | collective-permute-done | bytes 245792 | tf_op jit(solution)/shard_map/ppermute | solution.py:285
  22.0 1.7 %shard_map.62 = (f32[7,3,576,128]{3,2,1,0:T(8,128)S(1)}, f32[1,8,32,128]{3,2,1,0:T(8,128)}) custom-call(f32[6,576,128]{2,1,0:T(8,128)S(1)} %get-tuple-element.30.coef, f32[576,128]{1,0:T(8,128)S(1)} %get-tuple-element.31.scaled, f32[3,5,32,128]{3,2,1,0:T(8,128)S(1)} %collective-permute-done.10.halo, ...), custom_call_target="tpu_custom_call", output_to_operand_aliasing={{0}: (3, {})} | custom-call | tf_op jit(solution)/shard_map/pallas_call | solution.py:360
  (5 shorter events, 0.1 us)
Async XLA Ops:
  0.0 1.8 %collective-permute-start = (f32[2,8,32,128]{3,2,1,0:T(8,128)}, f32[2,8,32,128]{3,2,1,0:T(8,128)S(1)}, u32[]{:S(2)}, u32[]{:S(2)}) collective-permute-start(f32[2,8,32,128]{3,2,1,0:T(8,128)} %pool_hbm.1), channel_id=1, source_target_pairs={{0,4},{1,5},{2,6},{3,7},{4,0},{5,1},{6,2},{7,3},{8,12},{9,13},{10,... | collective-permute-start | bytes 786440 | tf_op jit(solution)/shard_map/ppermute | solution.py:285
  1.9 6.6 %collective-permute-start.1 = (f32[3,5,32,128]{3,2,1,0:T(8,128)S(1)}, f32[3,5,32,128]{3,2,1,0:T(8,128)S(1)}, u32[]{:S(2)}, u32[]{:S(2)}) collective-permute-start(f32[3,5,32,128]{3,2,1,0:T(8,128)S(1)} %get-tuple-element.26), channel_id=1, source_target_pairs={{0,12},{1,13},{2,14},{3,15},{4,16},{5,17},{6,18},{7,19},{8,4},{9,5... | collective-permute-start | bytes 737288 | tf_op jit(solution)/shard_map/ppermute | solution.py:285
  4.6 11.5 %collective-permute-start.4 = (f32[38,32,128]{2,1,0:T(8,128)S(1)}, f32[38,32,128]{2,1,0:T(8,128)S(1)}, u32[]{:S(2)}, u32[]{:S(2)}) collective-permute-start(f32[38,32,128]{2,1,0:T(8,128)S(1)} %get-tuple-element.27), channel_id=1, source_target_pairs={{0,5},{1,6},{2,7},{5,0},{6,1},{7,2},{8,13},{9,14},{10,15},{13,8},{... | collective-permute-start | bytes 1867784 | tf_op jit(solution)/shard_map/ppermute | solution.py:285
  8.5 9.9 %copy-start = (f32[3,8,32,128]{3,2,1,0:T(8,128)S(1)}, f32[3,8,32,128]{3,2,1,0:T(8,128)}, u32[]{:S(2)}) copy-start(f32[3,8,32,128]{3,2,1,0:T(8,128)} %metric.1) | copy-start | bytes 1179652
  8.5 9.9 %copy-start.1 = (f32[8,32,128]{2,1,0:T(8,128)S(1)}, f32[8,32,128]{2,1,0:T(8,128)}, u32[]{:S(2)}) copy-start(f32[8,32,128]{2,1,0:T(8,128)} %screening.1) | copy-start | bytes 393220
  8.5 6.3 %collective-permute-start.2 = (f32[3,5,32,128]{3,2,1,0:T(8,128)S(1)}, f32[3,5,32,128]{3,2,1,0:T(8,128)S(1)}, u32[]{:S(2)}, u32[]{:S(2)}) collective-permute-start(f32[3,5,32,128]{3,2,1,0:T(8,128)S(1)} %shard_map.57.mine), channel_id=1, source_target_pairs={{0,8},{1,9},{2,10},{3,11},{4,20},{5,21},{6,22},{7,23},{8,0},{9,1},... | collective-permute-start | bytes 737288 | tf_op jit(solution)/shard_map/ppermute | solution.py:285
  14.8 5.7 %collective-permute-start.3 = (f32[3,5,32,128]{3,2,1,0:T(8,128)S(1)}, f32[3,5,32,128]{3,2,1,0:T(8,128)S(1)}, u32[]{:S(2)}, u32[]{:S(2)}) collective-permute-start(f32[3,5,32,128]{3,2,1,0:T(8,128)S(1)} %shard_map.58.middle), channel_id=1, source_target_pairs={{0,5},{1,6},{2,7},{3,11},{4,12},{5,0},{6,1},{7,2},{8,13},{9,14},{1... | collective-permute-start | bytes 737288 | tf_op jit(solution)/shard_map/ppermute | solution.py:285
  16.2 1.4 %collective-permute-start.5 = (f32[7,32,128]{2,1,0:T(8,128)S(1)}, f32[7,32,128]{2,1,0:T(8,128)S(1)}, u32[]{:S(2)}, u32[]{:S(2)}) collective-permute-start(f32[7,32,128]{2,1,0:T(8,128)S(1)} %get-tuple-element.37), channel_id=1, source_target_pairs={{0,4},{1,5},{2,6},{3,7},{4,0},{5,1},{6,2},{7,3},{8,12},{9,13},{10,... | collective-permute-start | bytes 344072 | tf_op jit(solution)/shard_map/ppermute | solution.py:285
  16.2 2.1 %collective-permute-start.8 = (f32[7,32,128]{2,1,0:T(8,128)S(1)}, f32[7,32,128]{2,1,0:T(8,128)S(1)}, u32[]{:S(2)}, u32[]{:S(2)}) collective-permute-start(f32[7,32,128]{2,1,0:T(8,128)S(1)} %get-tuple-element.38), channel_id=1, source_target_pairs={{0,4},{1,5},{2,6},{3,7},{4,0},{5,1},{6,2},{7,3},{8,12},{9,13},{10,... | collective-permute-start | bytes 344072 | tf_op jit(solution)/shard_map/ppermute | solution.py:285
  16.7 1.6 %collective-permute-start.7 = (f32[7,32,128]{2,1,0:T(8,128)S(1)}, f32[7,32,128]{2,1,0:T(8,128)S(1)}, u32[]{:S(2)}, u32[]{:S(2)}) collective-permute-start(f32[7,32,128]{2,1,0:T(8,128)S(1)} %get-tuple-element.39), channel_id=1, source_target_pairs={{0,4},{1,5},{2,6},{3,7},{4,0},{5,1},{6,2},{7,3},{8,12},{9,13},{10,... | collective-permute-start | bytes 344072 | tf_op jit(solution)/shard_map/ppermute | solution.py:285
  16.8 1.6 %collective-permute-start.6 = (f32[7,32,128]{2,1,0:T(8,128)S(1)}, f32[7,32,128]{2,1,0:T(8,128)S(1)}, u32[]{:S(2)}, u32[]{:S(2)}) collective-permute-start(f32[7,32,128]{2,1,0:T(8,128)S(1)} %get-tuple-element.40), channel_id=1, source_target_pairs={{0,4},{1,5},{2,6},{3,7},{4,0},{5,1},{6,2},{7,3},{8,12},{9,13},{10,... | collective-permute-start | bytes 344072 | tf_op jit(solution)/shard_map/ppermute | solution.py:285
  17.5 1.4 %collective-permute-start.9 = (f32[3,3,32,128]{3,2,1,0:T(8,128)S(1)}, f32[3,3,32,128]{3,2,1,0:T(8,128)S(1)}, u32[]{:S(2)}, u32[]{:S(2)}) collective-permute-start(f32[3,3,32,128]{3,2,1,0:T(8,128)S(1)} %constant_dynamic-slice_fusion), channel_id=1, source_target_pairs={{0,4},{1,5},{2,6},{3,7},{4,0},{5,1},{6,2},{7,3},{8,12},{9,13},{10,... | collective-permute-start | bytes 442376 | tf_op jit(solution)/shard_map/ppermute | solution.py:285
  20.5 1.5 %collective-permute-start.10 = (f32[3,5,32,128]{3,2,1,0:T(8,128)S(1)}, f32[3,5,32,128]{3,2,1,0:T(8,128)S(1)}, u32[]{:S(2)}, u32[]{:S(2)}) collective-permute-start(f32[3,5,32,128]{3,2,1,0:T(8,128)S(1)} %collective-permute-done.3.halo), channel_id=1, source_target_pairs={{0,4},{1,5},{2,6},{3,7},{4,0},{5,1},{6,2},{7,3},{8,12},{9,13},{10,... | collective-permute-start | bytes 737288 | tf_op jit(solution)/shard_map/ppermute | solution.py:285

commit v8 on v7

--- a/solution.py
+++ b/solution.py
@@ -27,6 +27,12 @@
 
 def upper_side():
     return 1 - lax.rem(lax.axis_index("orb"), 2)
+
+
+def on_each_side(body):
+    side = upper_side()
+    for constant in (0, 1):
+        pl.when(side == constant)(functools.partial(body, constant))
 
 
 def call(kernel, out_shapes, in_specs, scratch=(), flops=0, moved=0, alias=None):
@@ -177,7 +183,8 @@
 def take_planes(weight, scaled, state, part, at):
     count, gx, gy = part.shape[1:]
     for i in range(count):
-        rows = pl.ds(pl.multiple_of((at + i) * gx, gx), gx)
+        first = (at + i) * gx
+        rows = pl.ds(first if isinstance(at, int) else pl.multiple_of(first, gx), gx)
         t = scaled[rows]
         for s in range(NSRC):
             cells = part[s, i]
@@ -191,10 +198,11 @@
     gy = state.shape[-1]
     old = START + k - 1
 
-    @pl.loop(0, count, unroll=count)
-    def _(i):
+    for i in range(count):
         for j in range(0, gx, 8):
-            at = pl.multiple_of((begin + i) * gx, gx) + j
+            at = (begin + i) * gx + j
+            if not isinstance(begin, int):
+                at = pl.multiple_of(at, 8)
             here = pl.ds(at, 8)
             c = [coef[n, here] for n in range(6)]
             acc = None
@@ -232,37 +240,40 @@
 
 def near_kernel(weights, coef, scaled, halo, known, state, early):
     del known
-    side = upper_side()
     h = HALO
     gx = halo.shape[2]
     total = state.shape[2] // gx
     planes = total - 2 * h
-    take_planes(weights[0], scaled, state, halo, side * (h + planes))
-    for k in range(1, SWEEPS):
-        count = min(h, h + planes - 2 * k)
-        begin = jnp.where(side == 0, k, total - k - count)
-        if k < SWEEPS - 1:
-            sweep_planes(k, weights[k], coef, state, begin, count, gx)
-        else:
-            sweep_planes(k, weights[k], coef, state, begin, count, gx, early, begin)
+
+    @on_each_side
+    def _(side):
+        take_planes(weights[0], scaled, state, halo, side * (h + planes))
+        for k in range(1, SWEEPS):
+            count = min(h, h + planes - 2 * k)
+            begin = k if side == 0 else total - k - count
+            if k < SWEEPS - 1:
+                sweep_planes(k, weights[k], coef, state, begin, count, gx)
+            else:
+                sweep_planes(k, weights[k], coef, state, begin, count, gx, early, begin)
 
 
 def far_kernel(weights, coef, scaled, halo, known, early, state, out):
     del known
-    side = upper_side()
     h = HALO
     gx = halo.shape[2]
     planes = out.shape[1]
-    total = planes + 2 * h
-    take_planes(weights[0], scaled, state, halo, (1 - side) * (h + planes))
-    for k in range(1, SWEEPS):
-        begin = jnp.where(side == 0, h + planes - k, k)
-        if k < SWEEPS - 1:
-            sweep_planes(k, weights[k], coef, state, begin, h, gx)
-        else:
-            sweep_planes(k, weights[k], coef, state, begin, h, gx, out.at[0], h)
     done = early.shape[0]
-    out[0, pl.ds(side * (planes - done), done)] = early[...]
+
+    @on_each_side
+    def _(side):
+        take_planes(weights[0], scaled, state, halo, (1 - side) * (h + planes))
+        out[0, pl.ds(side * (planes - done), done)] = early[...]
+        for k in range(1, SWEEPS):
+            begin = k if side else h + planes - k
+            if k < SWEEPS - 1:
+                sweep_planes(k, weights[k], coef, state, begin, h, gx)
+            else:
+                sweep_planes(k, weights[k], coef, state, begin, h, gx, out.at[0], h)
 
 
 def shards(pool, target_row, source_index, metric, screening):

time: 23.9 us -> 23.6 us (0.987)
  Pallas kernels: 5.11 us -> 4.45 us
  waiting for transfers between devices: 6.88 us -> 7.22 us
    ppermute x11, waiting for transfers between devices: 6.88 us -> 7.22 us  [among(): return lambda x: lax.ppermute(x, AXES, pairs)]
    pallas_call x1, Pallas kernels: 1.01 us -> 0.66 us  [shards(): call(functools.partial(near_kernel, weights), [state.shape, (rest, gx, gy...]
    pallas_call x1, Pallas kernels: 1.7 us -> 1.38 us  [shards(): call(functools.partial(far_kernel, weights), [state.shape, (1, planes, gx...]
  transfers between devices with their start and end apart: 11 -> 11, of which waited for: 7 -> 7; matrix products, arithmetic and copies ran while one was open for 0% -> 0% of each run, Pallas kernels for 14% -> 13%
where the time goes in v8:
time: 23.6 us; the launch traced here: 23.4 us
  starting transfers between devices  10.9 us (46%)
  waiting for transfers between devices  7.22 us (31%)
  Pallas kernels  4.45 us (19%)
  between operations  0.78 us (3%)
    ppermute x11, starting transfers between devices, among(): return lambda x: lax.ppermute(x, AXES, pairs)  10.9 us
    ppermute x11, waiting for transfers between devices, among(): return lambda x: lax.ppermute(x, AXES, pairs)  7.22 us
    pallas_call x1, Pallas kernels, shards(): call(functools.partial(far_kernel, weights), [state.shape, (1, planes, gx...  1.38 us
    pallas_call x1, Pallas kernels, shards(): call(pick_kernel, [(NSRC,) + pool.shape[1:], ((4 + 2 * held) * h - 2, gx,...  1.24 us
    pallas_call x1, Pallas kernels, shards(): call(functools.partial(near_kernel, weights), [state.shape, (rest, gx, gy...  0.66 us
    pallas_call x1, Pallas kernels, shards(): call(functools.partial(inner_kernel, weights), [(START + SWEEPS - 1, NSRC...  0.51 us
    pallas_call x1, Pallas kernels, shards(): call(coefficient_kernel, [(6, total * gx, gy), (total * gx, gy)], [SMEM]...  0.51 us
  transfers between devices with their start and end apart: 11, of which 7 were waited for; matrix products, arithmetic and copies ran while one was open for 0% of the time, Pallas kernels for 13%

profile of v8, /device:TPU:0, one launch (start us, length us, event | category | flops | bytes accessed | tf_op | source)
XLA Modules:
  0.0 23.4 jit_solution(6874390709182269228)
XLA Ops:
  0.0 0.5 %collective-permute-start = (f32[2,8,32,128]{3,2,1,0:T(8,128)}, f32[2,8,32,128]{3,2,1,0:T(8,128)S(1)}, u32[]{:S(2)}, u32[]{:S(2)}) collective-permute-start(f32[2,8,32,128]{3,2,1,0:T(8,128)} %pool_hbm.1), channel_id=1, source_target_pairs={{0,4},{1,5},{2,6},{3,7},{4,0},{5,1},{6,2},{7,3},{8,12},{9,13},{10,... | collective-permute-start | bytes 786440 | tf_op jit(solution)/shard_map/ppermute | solution.py:296
  0.5 1.2 %shard_map.55 = (f32[3,8,32,128]{3,2,1,0:T(8,128)S(1)}, f32[38,32,128]{2,1,0:T(8,128)S(1)}, f32[3,2,8,128]{3,2,1,0:T(8,128)S(1)}, f32[2,8,32,128]{3,2,1,0:T(8,128)S(1)}) custom-call(s32[3]{0:T(128)} %index_hbm.1, f32[2,8,32,128]{3,2,1,0:T(8,128)} %pool_hbm.1, f32[3,8,32,128]{3,2,1,0:T(8,128)} %metric.1, f32[8,32,128]{2,1,0:T(8,128)} %screening.1), custom_call_target="tpu_custom_call" | custom-call | bytes 4194304 | tf_op jit(solution)/shard_map/pallas_call | solution.py:309
  1.7 0.1 collective-permute-done.theirs
  1.8 0.1 shard_map.56
  1.9 2.7 %collective-permute-start.1 = (f32[3,5,32,128]{3,2,1,0:T(8,128)S(1)}, f32[3,5,32,128]{3,2,1,0:T(8,128)S(1)}, u32[]{:S(2)}, u32[]{:S(2)}) collective-permute-start(f32[3,5,32,128]{3,2,1,0:T(8,128)S(1)} %get-tuple-element.26), channel_id=1, source_target_pairs={{0,12},{1,13},{2,14},{3,15},{4,16},{5,17},{6,18},{7,19},{8,4},{9,5... | collective-permute-start | bytes 737288 | tf_op jit(solution)/shard_map/ppermute | solution.py:296
  4.6 3.5 %collective-permute-start.4 = (f32[38,32,128]{2,1,0:T(8,128)S(1)}, f32[38,32,128]{2,1,0:T(8,128)S(1)}, u32[]{:S(2)}, u32[]{:S(2)}) collective-permute-start(f32[38,32,128]{2,1,0:T(8,128)S(1)} %get-tuple-element.27), channel_id=1, source_target_pairs={{0,5},{1,6},{2,7},{5,0},{6,1},{7,2},{8,13},{9,14},{10,15},{13,8},{... | collective-permute-start | bytes 1867784 | tf_op jit(solution)/shard_map/ppermute | solution.py:296
  8.1 0.4 %collective-permute-done.1.theirs = f32[3,5,32,128]{3,2,1,0:T(8,128)S(1)} collective-permute-done((f32[3,5,32,128]{3,2,1,0:T(8,128)S(1)}, f32[3,5,32,128]{3,2,1,0:T(8,128)S(1)}, u32[]{:S(2)}, u32[]{:S(2)}) %collective-permute-start.1) | collective-permute-done | bytes 245792 | tf_op jit(solution)/shard_map/ppermute | solution.py:296
  8.5 0.0 copy-start
  8.5 0.0 copy-start.1
  8.5 2.0 %collective-permute-start.2 = (f32[3,5,32,128]{3,2,1,0:T(8,128)S(1)}, f32[3,5,32,128]{3,2,1,0:T(8,128)S(1)}, u32[]{:S(2)}, u32[]{:S(2)}) collective-permute-start(f32[3,5,32,128]{3,2,1,0:T(8,128)S(1)} %shard_map.57.mine), channel_id=1, source_target_pairs={{0,8},{1,9},{2,10},{3,11},{4,20},{5,21},{6,22},{7,23},{8,0},{9,1},... | collective-permute-start | bytes 737288 | tf_op jit(solution)/shard_map/ppermute | solution.py:296
  10.6 4.2 %collective-permute-done.2.theirs = f32[3,5,32,128]{3,2,1,0:T(8,128)S(1)} collective-permute-done((f32[3,5,32,128]{3,2,1,0:T(8,128)S(1)}, f32[3,5,32,128]{3,2,1,0:T(8,128)S(1)}, u32[]{:S(2)}, u32[]{:S(2)}) %collective-permute-start.2) | collective-permute-done | bytes 245792 | tf_op jit(solution)/shard_map/ppermute | solution.py:296
  14.8 1.0 %collective-permute-start.3 = (f32[3,5,32,128]{3,2,1,0:T(8,128)S(1)}, f32[3,5,32,128]{3,2,1,0:T(8,128)S(1)}, u32[]{:S(2)}, u32[]{:S(2)}) collective-permute-start(f32[3,5,32,128]{3,2,1,0:T(8,128)S(1)} %shard_map.58.middle), channel_id=1, source_target_pairs={{0,5},{1,6},{2,7},{3,11},{4,12},{5,0},{6,1},{7,2},{8,13},{9,14},{1... | collective-permute-start | bytes 737288 | tf_op jit(solution)/shard_map/ppermute | solution.py:296
  15.8 0.3 %collective-permute-done.4.near = f32[38,32,128]{2,1,0:T(8,128)S(1)} collective-permute-done((f32[38,32,128]{2,1,0:T(8,128)S(1)}, f32[38,32,128]{2,1,0:T(8,128)S(1)}, u32[]{:S(2)}, u32[]{:S(2)}) %collective-permute-start.4) | collective-permute-done | bytes 622624 | tf_op jit(solution)/shard_map/ppermute | solution.py:296
  16.2 0.1 collective-permute-start.5
  16.2 0.5 %collective-permute-start.8 = (f32[7,32,128]{2,1,0:T(8,128)S(1)}, f32[7,32,128]{2,1,0:T(8,128)S(1)}, u32[]{:S(2)}, u32[]{:S(2)}) collective-permute-start(f32[7,32,128]{2,1,0:T(8,128)S(1)} %get-tuple-element.38), channel_id=1, source_target_pairs={{0,4},{1,5},{2,6},{3,7},{4,0},{5,1},{6,2},{7,3},{8,12},{9,13},{10,... | collective-permute-start | bytes 344072 | tf_op jit(solution)/shard_map/ppermute | solution.py:296
  16.7 0.1 collective-permute-start.7
  16.8 0.4 %collective-permute-start.6 = (f32[7,32,128]{2,1,0:T(8,128)S(1)}, f32[7,32,128]{2,1,0:T(8,128)S(1)}, u32[]{:S(2)}, u32[]{:S(2)}) collective-permute-start(f32[7,32,128]{2,1,0:T(8,128)S(1)} %get-tuple-element.40), channel_id=1, source_target_pairs={{0,4},{1,5},{2,6},{3,7},{4,0},{5,1},{6,2},{7,3},{8,12},{9,13},{10,... | collective-permute-start | bytes 344072 | tf_op jit(solution)/shard_map/ppermute | solution.py:296
  17.3 0.3 %collective-permute-done.5 = f32[7,32,128]{2,1,0:T(8,128)S(1)} collective-permute-done((f32[7,32,128]{2,1,0:T(8,128)S(1)}, f32[7,32,128]{2,1,0:T(8,128)S(1)}, u32[]{:S(2)}, u32[]{:S(2)}) %collective-permute-start.5) | collective-permute-done | bytes 114720 | tf_op jit(solution)/shard_map/ppermute | solution.py:296
  17.5 0.2 collective-permute-start.9
  18.3 0.0 collective-permute-done.8
  18.4 0.0 collective-permute-done.7
  18.4 0.0 collective-permute-done.6
  18.4 0.0 copy-done
  18.4 0.0 copy-done.1
  18.4 0.5 %shard_map.59 = (f32[6,576,128]{2,1,0:T(8,128)S(1)}, f32[576,128]{1,0:T(8,128)S(1)}) custom-call(s32[1]{0:T(128)S(6)} %copy.12.row, f32[2,8,32,128]{3,2,1,0:T(8,128)S(1)} %get-tuple-element.23.pool, f32[3,8,32,128]{3,2,1,0:T(8,128)S(1)} %copy-done, f32[8,32,128]{2,1,0:T(8,128)S(1)} %copy-done.1, f32[38,32,128]{2,1,0:T(8,128)S(1)} %collective-permute-done.4.near, ...), custom_call_target="tpu_custom_call" | custom-call | tf_op jit(solution)/shard_map/pallas_call | solution.py:348
  19.0 0.0 collective-permute-done.9.inner
  19.0 0.5 %shard_map.60.known = f32[7,3,576,128]{3,2,1,0:T(8,128)S(1)} custom-call(f32[6,576,128]{2,1,0:T(8,128)S(1)} %get-tuple-element.30.coef, f32[576,128]{1,0:T(8,128)S(1)} %get-tuple-element.31.scaled, f32[3,5,32,128]{3,2,1,0:T(8,128)S(1)} %shard_map.58.middle, f32[3,3,32,128]{3,2,1,0:T(8,128)S(1)} %collective-permute-done.9.inner), custom_call_target="tpu_custom_call" | custom-call | tf_op jit(solution)/shard_map/pallas_call | solution.py:359
  19.5 1.0 %collective-permute-done.3.halo = f32[3,5,32,128]{3,2,1,0:T(8,128)S(1)} collective-permute-done((f32[3,5,32,128]{3,2,1,0:T(8,128)S(1)}, f32[3,5,32,128]{3,2,1,0:T(8,128)S(1)}, u32[]{:S(2)}, u32[]{:S(2)}) %collective-permute-start.3) | collective-permute-done | bytes 245792 | tf_op jit(solution)/shard_map/ppermute | solution.py:296
  20.5 0.0 collective-permute-start.10
  20.5 0.7 %shard_map.61 = (f32[7,3,576,128]{3,2,1,0:T(8,128)S(1)}, f32[3,32,128]{2,1,0:T(8,128)S(1)}) custom-call(f32[6,576,128]{2,1,0:T(8,128)S(1)} %get-tuple-element.30.coef, f32[576,128]{1,0:T(8,128)S(1)} %get-tuple-element.31.scaled, f32[3,5,32,128]{3,2,1,0:T(8,128)S(1)} %collective-permute-done.3.halo, ...), custom_call_target="tpu_custom_call", output_to_operand_aliasing={{0}: (3, {})} | custom-call | tf_op jit(solution)/shard_map/pallas_call | solution.py:365
  21.2 0.8 %collective-permute-done.10.halo = f32[3,5,32,128]{3,2,1,0:T(8,128)S(1)} collective-permute-done((f32[3,5,32,128]{3,2,1,0:T(8,128)S(1)}, f32[3,5,32,128]{3,2,1,0:T(8,128)S(1)}, u32[]{:S(2)}, u32[]{:S(2)}) %collective-permute-start.10) | collective-permute-done | bytes 245792 | tf_op jit(solution)/shard_map/ppermute | solution.py:296
  22.0 1.4 %shard_map.62 = (f32[7,3,576,128]{3,2,1,0:T(8,128)S(1)}, f32[1,8,32,128]{3,2,1,0:T(8,128)}) custom-call(f32[6,576,128]{2,1,0:T(8,128)S(1)} %get-tuple-element.30.coef, f32[576,128]{1,0:T(8,128)S(1)} %get-tuple-element.31.scaled, f32[3,5,32,128]{3,2,1,0:T(8,128)S(1)} %collective-permute-done.10.halo, ...), custom_call_target="tpu_custom_call", output_to_operand_aliasing={{0}: (3, {})} | custom-call | tf_op jit(solution)/shard_map/pallas_call | solution.py:371
  (5 shorter events, 0.1 us)
Async XLA Ops:
  0.0 1.8 %collective-permute-start = (f32[2,8,32,128]{3,2,1,0:T(8,128)}, f32[2,8,32,128]{3,2,1,0:T(8,128)S(1)}, u32[]{:S(2)}, u32[]{:S(2)}) collective-permute-start(f32[2,8,32,128]{3,2,1,0:T(8,128)} %pool_hbm.1), channel_id=1, source_target_pairs={{0,4},{1,5},{2,6},{3,7},{4,0},{5,1},{6,2},{7,3},{8,12},{9,13},{10,... | collective-permute-start | bytes 786440 | tf_op jit(solution)/shard_map/ppermute | solution.py:296
  1.9 6.6 %collective-permute-start.1 = (f32[3,5,32,128]{3,2,1,0:T(8,128)S(1)}, f32[3,5,32,128]{3,2,1,0:T(8,128)S(1)}, u32[]{:S(2)}, u32[]{:S(2)}) collective-permute-start(f32[3,5,32,128]{3,2,1,0:T(8,128)S(1)} %get-tuple-element.26), channel_id=1, source_target_pairs={{0,12},{1,13},{2,14},{3,15},{4,16},{5,17},{6,18},{7,19},{8,4},{9,5... | collective-permute-start | bytes 737288 | tf_op jit(solution)/shard_map/ppermute | solution.py:296
  4.6 11.5 %collective-permute-start.4 = (f32[38,32,128]{2,1,0:T(8,128)S(1)}, f32[38,32,128]{2,1,0:T(8,128)S(1)}, u32[]{:S(2)}, u32[]{:S(2)}) collective-permute-start(f32[38,32,128]{2,1,0:T(8,128)S(1)} %get-tuple-element.27), channel_id=1, source_target_pairs={{0,5},{1,6},{2,7},{5,0},{6,1},{7,2},{8,13},{9,14},{10,15},{13,8},{... | collective-permute-start | bytes 1867784 | tf_op jit(solution)/shard_map/ppermute | solution.py:296
  8.5 9.9 %copy-start = (f32[3,8,32,128]{3,2,1,0:T(8,128)S(1)}, f32[3,8,32,128]{3,2,1,0:T(8,128)}, u32[]{:S(2)}) copy-start(f32[3,8,32,128]{3,2,1,0:T(8,128)} %metric.1) | copy-start | bytes 1179652
  8.5 9.9 %copy-start.1 = (f32[8,32,128]{2,1,0:T(8,128)S(1)}, f32[8,32,128]{2,1,0:T(8,128)}, u32[]{:S(2)}) copy-start(f32[8,32,128]{2,1,0:T(8,128)} %screening.1) | copy-start | bytes 393220
  8.5 6.3 %collective-permute-start.2 = (f32[3,5,32,128]{3,2,1,0:T(8,128)S(1)}, f32[3,5,32,128]{3,2,1,0:T(8,128)S(1)}, u32[]{:S(2)}, u32[]{:S(2)}) collective-permute-start(f32[3,5,32,128]{3,2,1,0:T(8,128)S(1)} %shard_map.57.mine), channel_id=1, source_target_pairs={{0,8},{1,9},{2,10},{3,11},{4,20},{5,21},{6,22},{7,23},{8,0},{9,1},... | collective-permute-start | bytes 737288 | tf_op jit(solution)/shard_map/ppermute | solution.py:296
  14.8 5.7 %collective-permute-start.3 = (f32[3,5,32,128]{3,2,1,0:T(8,128)S(1)}, f32[3,5,32,128]{3,2,1,0:T(8,128)S(1)}, u32[]{:S(2)}, u32[]{:S(2)}) collective-permute-start(f32[3,5,32,128]{3,2,1,0:T(8,128)S(1)} %shard_map.58.middle), channel_id=1, source_target_pairs={{0,5},{1,6},{2,7},{3,11},{4,12},{5,0},{6,1},{7,2},{8,13},{9,14},{1... | collective-permute-start | bytes 737288 | tf_op jit(solution)/shard_map/ppermute | solution.py:296
  16.2 1.4 %collective-permute-start.5 = (f32[7,32,128]{2,1,0:T(8,128)S(1)}, f32[7,32,128]{2,1,0:T(8,128)S(1)}, u32[]{:S(2)}, u32[]{:S(2)}) collective-permute-start(f32[7,32,128]{2,1,0:T(8,128)S(1)} %get-tuple-element.37), channel_id=1, source_target_pairs={{0,4},{1,5},{2,6},{3,7},{4,0},{5,1},{6,2},{7,3},{8,12},{9,13},{10,... | collective-permute-start | bytes 344072 | tf_op jit(solution)/shard_map/ppermute | solution.py:296
  16.2 2.1 %collective-permute-start.8 = (f32[7,32,128]{2,1,0:T(8,128)S(1)}, f32[7,32,128]{2,1,0:T(8,128)S(1)}, u32[]{:S(2)}, u32[]{:S(2)}) collective-permute-start(f32[7,32,128]{2,1,0:T(8,128)S(1)} %get-tuple-element.38), channel_id=1, source_target_pairs={{0,4},{1,5},{2,6},{3,7},{4,0},{5,1},{6,2},{7,3},{8,12},{9,13},{10,... | collective-permute-start | bytes 344072 | tf_op jit(solution)/shard_map/ppermute | solution.py:296
  16.7 1.6 %collective-permute-start.7 = (f32[7,32,128]{2,1,0:T(8,128)S(1)}, f32[7,32,128]{2,1,0:T(8,128)S(1)}, u32[]{:S(2)}, u32[]{:S(2)}) collective-permute-start(f32[7,32,128]{2,1,0:T(8,128)S(1)} %get-tuple-element.39), channel_id=1, source_target_pairs={{0,4},{1,5},{2,6},{3,7},{4,0},{5,1},{6,2},{7,3},{8,12},{9,13},{10,... | collective-permute-start | bytes 344072 | tf_op jit(solution)/shard_map/ppermute | solution.py:296
  16.8 1.6 %collective-permute-start.6 = (f32[7,32,128]{2,1,0:T(8,128)S(1)}, f32[7,32,128]{2,1,0:T(8,128)S(1)}, u32[]{:S(2)}, u32[]{:S(2)}) collective-permute-start(f32[7,32,128]{2,1,0:T(8,128)S(1)} %get-tuple-element.40), channel_id=1, source_target_pairs={{0,4},{1,5},{2,6},{3,7},{4,0},{5,1},{6,2},{7,3},{8,12},{9,13},{10,... | collective-permute-start | bytes 344072 | tf_op jit(solution)/shard_map/ppermute | solution.py:296
  17.5 1.4 %collective-permute-start.9 = (f32[3,3,32,128]{3,2,1,0:T(8,128)S(1)}, f32[3,3,32,128]{3,2,1,0:T(8,128)S(1)}, u32[]{:S(2)}, u32[]{:S(2)}) collective-permute-start(f32[3,3,32,128]{3,2,1,0:T(8,128)S(1)} %constant_dynamic-slice_fusion), channel_id=1, source_target_pairs={{0,4},{1,5},{2,6},{3,7},{4,0},{5,1},{6,2},{7,3},{8,12},{9,13},{10,... | collective-permute-start | bytes 442376 | tf_op jit(solution)/shard_map/ppermute | solution.py:296
  20.5 1.5 %collective-permute-start.10 = (f32[3,5,32,128]{3,2,1,0:T(8,128)S(1)}, f32[3,5,32,128]{3,2,1,0:T(8,128)S(1)}, u32[]{:S(2)}, u32[]{:S(2)}) collective-permute-start(f32[3,5,32,128]{3,2,1,0:T(8,128)S(1)} %collective-permute-done.3.halo), channel_id=1, source_target_pairs={{0,4},{1,5},{2,6},{3,7},{4,0},{5,1},{6,2},{7,3},{8,12},{9,13},{10,... | collective-permute-start | bytes 737288 | tf_op jit(solution)/shard_map/ppermute | solution.py:296
